TPU v7x, 32 devices: a whole 2x2x4 slice. The times are simulated.
32 devices in a mesh: seq: 4 (over y, x), grp: 8 (over z, core).
Axes of the slice: x: 2, y: 2, z: 4, core: 2. Of those that a mesh axis runs over, the one named last changes fastest.
Arguments:
- tokens: bfloat16 [2, 8, 512, 512], P(None, 'grp', 'seq'), may hold values from -6 to 6
- layout: int32 [2, 8], P(None, 'grp'), may hold values from 0 to 1, as said below
- filters: float32 [512, 24], replicated, may hold values from -0.25 to 0.25
- gain_mix: bfloat16 [512], P(('seq', 'grp')), may hold values from 0.25 to 1.75
- spectral_proj: bfloat16 [24576, 512], P(('seq', 'grp')), may hold values from -0.0546875 to 0.0546875
- ar_proj: bfloat16 [1536, 512], P(('seq', 'grp')), may hold values from -0.15625 to 0.15625
- gain_mlp: bfloat16 [512], P(('seq', 'grp')), may hold values from 0.25 to 1.75
- w_gate: bfloat16 [512, 2048], P(('seq', 'grp')), may hold values from -0.25 to 0.25
- w_up: bfloat16 [512, 2048], P(('seq', 'grp')), may hold values from -0.25 to 0.25
- w_down: bfloat16 [2048, 512], P(('seq', 'grp')), may hold values from -0.1875 to 0.1875
- out_grad: bfloat16 [2, 8, 512, 512], P(None, 'grp', 'seq'), may hold values from -6 to 6
Outputs:
- out: float32 [2, 8, 512, 512], P(None, 'grp', 'seq')
- tokens_grad: float32 [2, 8, 512, 512], P(None, 'grp', 'seq')
- gain_mix_grad: float32 [512], P(('seq', 'grp'))
- spectral_proj_grad: float32 [24576, 512], P(('seq', 'grp'))
- ar_proj_grad: float32 [1536, 512], P(('seq', 'grp'))
- gain_mlp_grad: float32 [512], P(('seq', 'grp'))
- w_gate_grad: float32 [512, 2048], P(('seq', 'grp'))
- w_up_grad: float32 [512, 2048], P(('seq', 'grp'))
- w_down_grad: float32 [2048, 512], P(('seq', 'grp'))
Inputs may be any that keep to these rules, and one draw needn't show every extreme that they name: In every group the layout alternates from one micro-batch to the next: 0 holds one sequence of 512 positions, 1 holds four of 128.
All inputs are finite; a program needn't handle non-finite values.
Results may differ from a plain program's by a relative error of at most 0.0069.
Values may be sent and summed in bfloat16 or wider, within the bound.
A program may use at most 208 MiB of HBM per device.

v0:
```python
import jax
import jax.numpy as jnp
from jax import lax
from jax.sharding import PartitionSpec as P

EPSILON = 1e-05
HIGHEST = lax.Precision.HIGHEST


def shifted(shard, axis, by):
    devices = lax.axis_size(axis)
    pairs = [(i, i + by) for i in range(devices) if 0 <= i + by < devices]
    return lax.ppermute(shard, axis, pairs)


def parity(positions):
    return 1.0 - 2.0 * (positions % 2).astype(jnp.float32)


def contract_rows(left, right):
    return lax.dot_general(
        left, right, (((0,), (0,)), ((), ())), preferred_element_type=jnp.float32
    )


def contract_cols(left, right):
    return lax.dot_general(
        left, right, (((1,), (1,)), ((), ())), preferred_element_type=jnp.float32
    )


def filter_block(table, arrived, out_pos, in_start, seq_edge, backward):
    arrived_rows = arrived.shape[0]
    in_pos = in_start + jnp.arange(arrived_rows, dtype=jnp.int32)
    if backward:
        lag_grid = in_pos[None, :] - out_pos[:, None]
        live_mask = (lag_grid >= 0) & (in_pos < seq_edge)[None, :]
    else:
        lag_grid = out_pos[:, None] - in_pos[None, :]
        live_mask = (lag_grid >= 0) & (in_pos >= seq_edge)[None, :]
    picked = jnp.take(table, jnp.clip(lag_grid, 0, table.shape[1] - 1), axis=1)
    filt_tile = jnp.where(live_mask[None], picked, 0.0)
    values = arrived.astype(jnp.float32)
    stacked = jnp.concatenate([values, values * parity(in_pos)[:, None]], axis=1)
    return jnp.einsum(
        "kab,bf->kaf", filt_tile, stacked, precision=HIGHEST, preferred_element_type=jnp.float32
    )


def fetch(gain_mix, spectral_proj, ar_proj, gain_mlp, w_gate, w_up, w_down):
    return (
        lax.all_gather(gain_mix, ("seq", "grp"), axis=0, tiled=True),
        lax.all_gather(spectral_proj, ("seq", "grp"), axis=0, tiled=True),
        lax.all_gather(ar_proj, ("seq", "grp"), axis=0, tiled=True),
        lax.all_gather(gain_mlp, ("seq", "grp"), axis=0, tiled=True),
        lax.all_gather(w_gate, ("seq", "grp"), axis=0, tiled=True),
        lax.all_gather(w_up, ("seq", "grp"), axis=0, tiled=True),
        lax.all_gather(w_down, ("seq", "grp"), axis=0, tiled=True),
    )


def reduce_grads(mix_grad, spec_grad, hist_grad, mlp_grad, gate_grad, up_grad, down_grad):
    return (
        lax.psum_scatter(mix_grad, ("seq", "grp"), scatter_dimension=0, tiled=True),
        lax.psum_scatter(spec_grad, ("seq", "grp"), scatter_dimension=0, tiled=True),
        lax.psum_scatter(hist_grad, ("seq", "grp"), scatter_dimension=0, tiled=True),
        lax.psum_scatter(mlp_grad, ("seq", "grp"), scatter_dimension=0, tiled=True),
        lax.psum_scatter(gate_grad, ("seq", "grp"), scatter_dimension=0, tiled=True),
        lax.psum_scatter(up_grad, ("seq", "grp"), scatter_dimension=0, tiled=True),
        lax.psum_scatter(down_grad, ("seq", "grp"), scatter_dimension=0, tiled=True),
    )


def body(
    tokens,
    layout,
    filters,
    gain_mix,
    spectral_proj,
    ar_proj,
    gain_mlp,
    w_gate,
    w_up,
    w_down,
    out_grad,
):
    seq_count = lax.axis_size("seq")
    seq_index = lax.axis_index("seq")
    block_rows = tokens.shape[2]
    width = tokens.shape[3]
    filter_count = filters.shape[1]
    group_rows = block_rows * seq_count
    my_start = seq_index * block_rows
    table = filters.T
    out_pos = my_start + jnp.arange(block_rows, dtype=jnp.int32)
    half_flip = jnp.concatenate(
        [
            jnp.ones((block_rows, width), jnp.float32),
            jnp.broadcast_to(parity(out_pos)[:, None], (block_rows, width)),
        ],
        axis=1,
    )[None]
    outputs = []
    input_grads = []
    grad_sums = None
    for micro_step in range(tokens.shape[0]):
        gathered = fetch(gain_mix, spectral_proj, ar_proj, gain_mlp, w_gate, w_up, w_down)
        mix_gain, spec_full, hist_full, mlp_gain, gate_full, up_full, down_full = gathered
        layout_flag = layout[micro_step, 0]
        seg_len = jnp.where(layout_flag == 1, group_rows // 4, group_rows)
        seg_start = my_start // seg_len * seg_len
        seg_end = seg_start + seg_len
        inputs = tokens[micro_step, 0].astype(jnp.float32)
        inv_one = lax.rsqrt(jnp.mean(inputs * inputs, axis=-1, keepdims=True) + EPSILON)
        mix_scale = mix_gain.astype(jnp.float32)
        normed = (inputs * inv_one * mix_scale).astype(jnp.bfloat16)
        spread_zero_sum = jnp.zeros((filter_count, block_rows, 2 * width), jnp.float32)

        def spread_add_block(partial_value, arrived, in_start):
            needed = (in_start < my_start + block_rows) & (in_start + arrived.shape[0] > seg_start)
            return lax.cond(
                needed,
                lambda running: running
                + filter_block(table, arrived, out_pos, in_start, seg_start, False),
                lambda running: running,
                partial_value,
            )

        spread_local_sum = spread_add_block(spread_zero_sum, normed, my_start)

        def spread_advance(step_index, carried):
            travel, running = carried
            travel = shifted(travel, "seq", 1)
            return (travel, spread_add_block(running, travel, my_start - step_index * block_rows))

        spread_summed = lax.fori_loop(1, seq_count, spread_advance, (normed, spread_local_sum))[1]
        spectral = (spread_summed * half_flip).astype(jnp.bfloat16)
        spec_three = spec_full.reshape(filter_count, 2 * width, width)
        edge_rows = shifted(normed[block_rows - 2 :], "seq", 1)
        edge_rows = jnp.where(my_start > seg_start, edge_rows, jnp.zeros_like(edge_rows))
        extended = jnp.concatenate([edge_rows, normed], axis=0)
        history = jnp.concatenate(
            [normed, extended[1 : block_rows + 1], extended[:block_rows]], axis=1
        )
        mixer = lax.dot_general(
            spectral, spec_three, (((0, 2), (0, 1)), ((), ())), preferred_element_type=jnp.float32
        )
        mixer = mixer + jnp.dot(history, hist_full, preferred_element_type=jnp.float32)
        hidden = inputs + mixer
        inv_two = lax.rsqrt(jnp.mean(hidden * hidden, axis=-1, keepdims=True) + EPSILON)
        mlp_scale = mlp_gain.astype(jnp.float32)
        mlp_in = (hidden * inv_two * mlp_scale).astype(jnp.bfloat16)
        gate = jnp.dot(mlp_in, gate_full, preferred_element_type=jnp.float32)
        upval = jnp.dot(mlp_in, up_full, preferred_element_type=jnp.float32)
        product_val, gelu_pull = jax.vjp(
            lambda gate_arg, up_arg: jax.nn.gelu(gate_arg) * up_arg, gate, upval
        )
        mixed = product_val.astype(jnp.bfloat16)
        outputs.append(hidden + jnp.dot(mixed, down_full, preferred_element_type=jnp.float32))
        cotangent = out_grad[micro_step, 0]
        down_grad = contract_rows(mixed, cotangent)
        mixed_grad = contract_cols(cotangent, down_full)
        gate_back, up_back = gelu_pull(mixed_grad)
        gate_back = gate_back.astype(jnp.bfloat16)
        up_back = up_back.astype(jnp.bfloat16)
        gate_grad = contract_rows(mlp_in, gate_back)
        up_grad = contract_rows(mlp_in, up_back)
        mlp_in_grad = contract_cols(gate_back, gate_full) + contract_cols(up_back, up_full)
        scaled_two = mlp_in_grad * mlp_scale
        mlp_grad = jnp.sum(mlp_in_grad * hidden * inv_two, axis=0)
        hidden_grad = (
            cotangent.astype(jnp.float32)
            + inv_two * scaled_two
            - hidden * inv_two**3 * jnp.mean(scaled_two * hidden, axis=-1, keepdims=True)
        )
        mixer_grad = hidden_grad.astype(jnp.bfloat16)
        spec_grad = lax.dot_general(
            spectral, mixer_grad, (((1,), (0,)), ((), ())), preferred_element_type=jnp.float32
        ).reshape(2 * filter_count * width, width)
        hist_grad = contract_rows(history, mixer_grad)
        zero_sum = jnp.zeros((filter_count, block_rows, 2 * width), jnp.float32)

        def add_block(partial_value, arrived, in_start):
            needed = (in_start + arrived.shape[0] > my_start) & (in_start < seg_end)
            return lax.cond(
                needed,
                lambda running: running
                + filter_block(table, arrived, out_pos, in_start, seg_end, True),
                lambda running: running,
                partial_value,
            )

        local_sum = add_block(zero_sum, mixer_grad, my_start)

        def advance(step_index, carried):
            travel, running = carried
            travel = shifted(travel, "seq", -1)
            return (travel, add_block(running, travel, my_start + step_index * block_rows))

        summed = lax.fori_loop(1, seq_count, advance, (mixer_grad, local_sum))[1]
        back_sum = (summed * half_flip).reshape(filter_count, block_rows, 2, width)
        spec_four = spec_full.astype(jnp.float32).reshape(filter_count, 2, width, width)
        normed_grad = lax.dot_general(
            back_sum,
            spec_four,
            (((0, 2, 3), (0, 1, 3)), ((), ())),
            precision=HIGHEST,
            preferred_element_type=jnp.float32,
        )
        lag_parts = contract_cols(mixer_grad, hist_full)
        part_zero = lag_parts[:, :width]
        part_one = lag_parts[:, width : 2 * width]
        part_two = lag_parts[:, 2 * width :]
        tail_send = jnp.concatenate([part_two[:1], part_one[:1] + part_two[1:2]], axis=0)
        tail_back = shifted(tail_send, "seq", -1)
        tail_back = jnp.where(my_start + block_rows < seg_end, tail_back, jnp.zeros_like(tail_back))
        zero_pad = jnp.zeros((2, width), jnp.float32)
        normed_grad = normed_grad + part_zero
        normed_grad = normed_grad + jnp.concatenate([part_one[1:], zero_pad[:1]], axis=0)
        normed_grad = normed_grad + jnp.concatenate([part_two[2:], zero_pad], axis=0)
        normed_grad = normed_grad + jnp.concatenate(
            [jnp.zeros((block_rows - 2, width), jnp.float32), tail_back], axis=0
        )
        scaled_one = normed_grad * mix_scale
        mix_grad = jnp.sum(normed_grad * inputs * inv_one, axis=0)
        input_grads.append(
            hidden_grad
            + inv_one * scaled_one
            - inputs * inv_one**3 * jnp.mean(scaled_one * inputs, axis=-1, keepdims=True)
        )
        step_grads = (mix_grad, spec_grad, hist_grad, mlp_grad, gate_grad, up_grad, down_grad)
        grad_sums = (
            step_grads if grad_sums is None else jax.tree.map(jnp.add, grad_sums, step_grads)
        )
    final_grads = reduce_grads(
        grad_sums[0],
        grad_sums[1],
        grad_sums[2],
        grad_sums[3],
        grad_sums[4],
        grad_sums[5],
        grad_sums[6],
    )
    result_out = jnp.stack(outputs)[:, None]
    result_grad = jnp.stack(input_grads)[:, None]
    return (result_out, result_grad) + tuple(final_grads)


def solution(mesh):
    placed = (
        P(None, "grp", "seq", None),
        P(None, "grp"),
        P(),
        P(("seq", "grp")),
        P(("seq", "grp"), None),
        P(("seq", "grp"), None),
        P(("seq", "grp")),
        P(("seq", "grp"), None),
        P(("seq", "grp"), None),
        P(("seq", "grp"), None),
        P(None, "grp", "seq", None),
    )
    return jax.shard_map(
        body,
        mesh=mesh,
        in_specs=placed,
        out_specs=(
            P(None, "grp", "seq", None),
            P(None, "grp", "seq", None),
            P(("seq", "grp")),
            P(("seq", "grp"), None),
            P(("seq", "grp"), None),
            P(("seq", "grp")),
            P(("seq", "grp"), None),
            P(("seq", "grp"), None),
            P(("seq", "grp"), None),
        ),
        check_vma=False,
    )
```

profile of v0, /device:TPU:0, one launch (start us, length us, event | category | flops | bytes accessed | tf_op | source)
XLA Modules:
  0.0 1514.8 jit_solution(15903862450365520843)
XLA Ops:
  11.7 44.1 %all-reduce.12 = (bf16[512]{0:T(512)(128)(2,1)S(1)}, bf16[512]{0:T(512)(128)(2,1)S(1)}) all-reduce(bf16[512]{0:T(512)(128)(2,1)S(1)} %dynamic-update-slice, bf16[512]{0:T(512)(128)(2,1)S(1)} %dynamic-update-slice.1), channel_id=1, replica_groups=mesh['seq'=4,'grp'=8] {'seq','grp'}, use_global_device_ids=true, to_apply=%add.7 | all-reduce | flops 1024 | bytes 4096
  71.7 72.6 %conditional.9 = (f32[24,128,1024]{2,1,0:T(8,128)}) conditional(s32[]{:T(128)} %convert_element_type.212, () %tuple.142, (s32[128]{0:T(128)S(1)}, s32[]{:T(128)}, s32[]{:T(128)}, f32[24,512]{0,1:T(8,128)S(1)}, bf16[128,512]{1,0:T(8,128)(2,1)S(1)}) %tuple.319), branch_computations={%region_9.11_spmd, %region_10.12_spmd} | conditional | flops 4833216512 | bytes 21958424 | solution.py:121
  72.1 54.4 %gather_fusion.1 = f32[16384,24]{1,0:T(8,128)} fusion(f32[24,512]{0,1:T(8,128)S(1)} %get-tuple-element.682, s32[16384]{0:T(1024)S(1)} %fusion.40), kind=kCustom, calls=%fused_computation.2.clone | custom fusion | bytes 3211264 | tf_op jit(solution)/shard_map/cond/branch_1_fun/jit(_take)/gather | solution.py:41
  144.2 72.7 %conditional.8 = (f32[24,128,1024]{2,1,0:T(8,128)}) conditional(s32[]{:T(128)} %convert_element_type.203, () %tuple.139, (s32[128]{0:T(128)S(1)}, s32[]{:T(128)}, s32[]{:T(128)}, f32[24,512]{0,1:T(8,128)S(1)}, bf16[128,512]{1,0:T(8,128)(2,1)S(1)}) %tuple.320), branch_computations={%region_1.2_spmd, %region_2.4_spmd} | conditional | flops 4833216512 | bytes 21958424 | solution.py:121
  144.8 54.4 %gather_fusion = f32[16384,24]{1,0:T(8,128)} fusion(f32[24,512]{0,1:T(8,128)S(1)} %get-tuple-element.662, s32[16384]{0:T(1024)S(1)} %fusion.19), kind=kCustom, calls=%fused_computation.clone | custom fusion | bytes 3211264 | tf_op jit(solution)/shard_map/cond/branch_1_fun/jit(_take)/gather | solution.py:41
  252.9 96.6 %while.82 = (s32[]{:T(128)}, bf16[128,512]{1,0:T(8,128)(2,1)S(1)}, f32[24,128,1024]{2,1,0:T(8,128)}, s32[]{:T(128)}, s32[]{:T(128)}, /*index=5*/s32[]{:T(128)}, f32[24,512]{0,1:T(8,128)S(1)}, s32[]{:T(128)}, s32[]{:T(128)}) while((s32[]{:T(128)}, bf16[128,512]{1,0:T(8,128)(2,1)S(1)}, f32[24,128,1024]{2,1,0:T(8,128)}, ...), condition=%wide.region_6.8_spmd.clone.clone, body=%wide.region_3.7_spmd.clone.clone.sunk | while | flops 4836362752 | bytes 35329560 | solution.py:136
  259.9 79.4 %collective-permute-start = (bf16[128,512]{1,0:T(8,128)(2,1)S(1)}, bf16[128,512]{1,0:T(8,128)(2,1)S(1)}, u32[]{:S(2)}, u32[]{:S(2)}) collective-permute-start(bf16[128,512]{1,0:T(8,128)(2,1)S(1)} %get-tuple-element.1255), channel_id=1, source_target_pairs={{0,8},{8,16},{16,24},{1,9},{9,17},{17,25},{2,10},{10,18},{18,26},{... | collective-permute-start | bytes 393224 | tf_op jit(solution)/shard_map/while/body/eval_jaxpr/ppermute | solution.py:13
  456.5 38.6 %convolution_add_fusion.4 = f32[24,1024,512]{2,1,0:T(8,128)} fusion(f32[24,1024,512]{2,1,0:T(8,128)} %fusion.178, f32[24,128,1024]{2,1,0:T(8,128)} %get-tuple-element.751, f32[128,1024]{1,0:T(8,128)S(1)} %concatenate.63, bf16[128,512]{1,0:T(8,128)(2,1)S(1)} %get-tuple-element.1297), kind=kOutput, calls=%fused_computation.272 | convolution fusion | flops 3240099840 | bytes 113901568 | tf_op jit(solution)/shard_map/dot_general | solution.py:177
  501.3 72.6 %conditional.11 = (f32[24,128,1024]{2,1,0:T(8,128)}) conditional(s32[]{:T(128)} %convert_element_type.225, () %tuple.148, (s32[]{:T(128)}, s32[128]{0:T(128)S(1)}, s32[]{:T(128)}, f32[24,512]{0,1:T(8,128)S(1)}, bf16[128,512]{1,0:T(8,128)(2,1)S(1)}) %tuple.328), branch_computations={%region_25.27_spmd, %region_26.28_spmd} | conditional | flops 4833216512 | bytes 21958424 | solution.py:185
  501.7 54.4 %gather_fusion.3 = f32[16384,24]{1,0:T(8,128)} fusion(f32[24,512]{0,1:T(8,128)S(1)} %get-tuple-element.721, s32[16384]{0:T(1024)S(1)} %fusion.82), kind=kCustom, calls=%fused_computation.6.clone | custom fusion | bytes 3211264 | tf_op jit(solution)/shard_map/cond/branch_1_fun/jit(_take)/gather | solution.py:41
  573.8 75.4 %conditional.10 = (f32[24,128,1024]{2,1,0:T(8,128)}) conditional(s32[]{:T(128)} %convert_element_type.220, () %tuple.145, (s32[]{:T(128)}, s32[128]{0:T(128)S(1)}, s32[]{:T(128)}, f32[24,512]{0,1:T(8,128)S(1)}, bf16[128,512]{1,0:T(8,128)(2,1)S(1)}) %tuple.329), branch_computations={%region_17.19_spmd, %region_18.20_spmd} | conditional | flops 4833216512 | bytes 21958424 | solution.py:185
  574.9 54.4 %gather_fusion.2 = f32[16384,24]{1,0:T(8,128)} fusion(f32[24,512]{0,1:T(8,128)S(1)} %get-tuple-element.702, s32[16384]{0:T(1024)S(1)} %fusion.61), kind=kCustom, calls=%fused_computation.4.clone | custom fusion | bytes 3211264 | tf_op jit(solution)/shard_map/cond/branch_1_fun/jit(_take)/gather | solution.py:41
  653.7 142.3 %while.85 = (s32[]{:T(128)}, bf16[128,512]{1,0:T(8,128)(2,1)S(1)}, f32[24,128,1024]{2,1,0:T(8,128)}, s32[]{:T(128)}, s32[]{:T(128)}, /*index=5*/f32[24,512]{0,1:T(8,128)S(1)}, s32[]{:T(128)}, s32[]{:T(128)}) while((s32[]{:T(128)}, bf16[128,512]{1,0:T(8,128)(2,1)S(1)}, f32[24,128,1024]{2,1,0:T(8,128)}, s32[]{:T(128)}, ...), condition=%wide.region_30.32_spmd.clone.clone, body=%wide.region_27.31_spmd.clone.clone.sunk | while | flops 4836362752 | bytes 35329552 | solution.py:200
  655.0 54.0 %collective-permute-done.3 = bf16[128,512]{1,0:T(8,128)(2,1)S(1)} collective-permute-done((bf16[128,512]{1,0:T(8,128)(2,1)S(1)}, bf16[128,512]{1,0:T(8,128)(2,1)S(1)}, u32[]{:S(2)}, u32[]{:S(2)}) %collective-permute-start.3) | collective-permute-done | bytes 131104 | tf_op jit(solution)/shard_map/while/body/eval_jaxpr/ppermute | solution.py:13
  718.3 77.6 %collective-permute-done.3 = bf16[128,512]{1,0:T(8,128)(2,1)S(1)} collective-permute-done((bf16[128,512]{1,0:T(8,128)(2,1)S(1)}, bf16[128,512]{1,0:T(8,128)(2,1)S(1)}, u32[]{:S(2)}, u32[]{:S(2)}) %collective-permute-start.3) | collective-permute-done | bytes 131104 | tf_op jit(solution)/shard_map/while/body/eval_jaxpr/ppermute | solution.py:13
  796.0 249.3 %while.84 = (s32[]{:T(128)}, bf16[128,512]{1,0:T(8,128)(2,1)S(1)}, f32[24,128,1024]{2,1,0:T(8,128)}, s32[]{:T(128)}, s32[]{:T(128)}, /*index=5*/f32[24,512]{0,1:T(8,128)S(1)}, s32[]{:T(128)}, s32[]{:T(128)}) while((s32[]{:T(128)}, bf16[128,512]{1,0:T(8,128)(2,1)S(1)}, f32[24,128,1024]{2,1,0:T(8,128)}, s32[]{:T(128)}, ...), condition=%wide.region_22.24_spmd.clone.clone, body=%wide.region_19.23_spmd.clone.clone.sunk | while | flops 4836362752 | bytes 35329552 | solution.py:200
  804.5 74.7 %conditional.26 = (f32[24,128,1024]{2,1,0:T(8,128)}) conditional(s32[]{:T(128)} %convert_element_type.321, f32[24,128,1024]{2,1,0:T(8,128)} %get-tuple-element.1282, (s32[]{:T(128)}, s32[]{:T(128)}, s32[]{:T(128)}, f32[24,512]{0,1:T(8,128)S(1)}, bf16[128,512]{1,0:T(8,128)(2,1)S(1)}, /*index=5*/f32[24,128,1024]{2,1,0:T(8,128)}, ...), branch_computations={%region_20.21_spmd, %region_21.22_spmd} | conditional | flops 4836362752 | bytes 34542364 | solution.py:185
  804.9 54.4 %gather_fusion.6 = f32[16384,24]{1,0:T(8,128)} fusion(f32[24,512]{0,1:T(8,128)S(1)} %get-tuple-element.708, s32[16384]{0:T(1024)S(1)} %fusion.142), kind=kCustom, calls=%fused_computation.5.clone | custom fusion | bytes 3211264 | tf_op jit(solution)/shard_map/while/body/eval_jaxpr/cond/branch_1_fun/jit(_take)/gather | solution.py:41
  888.2 74.7 %conditional.26 = (f32[24,128,1024]{2,1,0:T(8,128)}) conditional(s32[]{:T(128)} %convert_element_type.321, f32[24,128,1024]{2,1,0:T(8,128)} %get-tuple-element.1282, (s32[]{:T(128)}, s32[]{:T(128)}, s32[]{:T(128)}, f32[24,512]{0,1:T(8,128)S(1)}, bf16[128,512]{1,0:T(8,128)(2,1)S(1)}, /*index=5*/f32[24,128,1024]{2,1,0:T(8,128)}, ...), branch_computations={%region_20.21_spmd, %region_21.22_spmd} | conditional | flops 4836362752 | bytes 34542364 | solution.py:185
  888.6 54.4 %gather_fusion.6 = f32[16384,24]{1,0:T(8,128)} fusion(f32[24,512]{0,1:T(8,128)S(1)} %get-tuple-element.708, s32[16384]{0:T(1024)S(1)} %fusion.142), kind=kCustom, calls=%fused_computation.5.clone | custom fusion | bytes 3211264 | tf_op jit(solution)/shard_map/while/body/eval_jaxpr/cond/branch_1_fun/jit(_take)/gather | solution.py:41
  970.6 74.7 %conditional.26 = (f32[24,128,1024]{2,1,0:T(8,128)}) conditional(s32[]{:T(128)} %convert_element_type.321, f32[24,128,1024]{2,1,0:T(8,128)} %get-tuple-element.1282, (s32[]{:T(128)}, s32[]{:T(128)}, s32[]{:T(128)}, f32[24,512]{0,1:T(8,128)S(1)}, bf16[128,512]{1,0:T(8,128)(2,1)S(1)}, /*index=5*/f32[24,128,1024]{2,1,0:T(8,128)}, ...), branch_computations={%region_20.21_spmd, %region_21.22_spmd} | conditional | flops 4836362752 | bytes 34542364 | solution.py:185
  970.9 54.4 %gather_fusion.6 = f32[16384,24]{1,0:T(8,128)} fusion(f32[24,512]{0,1:T(8,128)S(1)} %get-tuple-element.708, s32[16384]{0:T(1024)S(1)} %fusion.142), kind=kCustom, calls=%fused_computation.5.clone | custom fusion | bytes 3211264 | tf_op jit(solution)/shard_map/while/body/eval_jaxpr/cond/branch_1_fun/jit(_take)/gather | solution.py:41
  1129.1 39.3 %all-reduce.11 = (f32[512]{0:T(512)S(1)}, f32[512]{0:T(512)S(1)}) all-reduce(f32[512]{0:T(512)S(1)} %add.594, f32[512]{0:T(512)S(1)} %add.598), channel_id=2, replica_groups=mesh['seq'=4,'grp'=8] {'seq','grp'}, use_global_device_ids=true, to_apply=%region_34.36.clone | all-reduce | flops 1024 | bytes 8192
  1170.7 336.8 %reduce-scatter.6.cloned.1.call-done = f32[768,512]{1,0:T(8,128)} async-done(((f32[24576,512]{1,0:T(8,128)}), f32[768,512]{1,0:T(8,128)}) %reduce-scatter.6.cloned.1.call-update) | async-done | bytes 1572880 | tf_op jit(solution)/shard_map/reduce_scatter | solution.py:65
  (341 shorter events, 464.0 us)
Async XLA Ops:
  7.2 229.5 %all-gather.6.cloned.1.call-start = ((), (), s32[]{:S(2)}) async-start(), calls=%async_computation.5 | async-start | bytes 25952256 | tf_op jit(solution)/shard_map/all_gather | solution.py:53
  7.9 242.5 %all-gather.8.cloned.1.call-start = ((), (), s32[]{:S(2)}) async-start(), calls=%async_computation.6 | async-start | bytes 1622016 | tf_op jit(solution)/shard_map/all_gather | solution.py:54
  8.7 356.5 %all-gather.12.cloned.1.call-start = ((), (), s32[]{:S(2)}) async-start(), calls=%async_computation.8 | async-start | bytes 2162688 | tf_op jit(solution)/shard_map/all_gather | solution.py:57
  9.4 358.8 %all-gather.10.cloned.1.call-start = ((), (), s32[]{:S(2)}) async-start(), calls=%async_computation.7 | async-start | bytes 2162688 | tf_op jit(solution)/shard_map/all_gather | solution.py:56
  10.0 390.3 %all-gather.14.cloned.1.call-start = ((), (), s32[]{:S(2)}) async-start(), calls=%async_computation.9 | async-start | bytes 2162688 | tf_op jit(solution)/shard_map/all_gather | solution.py:58
  58.7 159.0 %collective-permute-start.5 = (bf16[2,512]{1,0:T(2,128)(2,1)S(1)}, bf16[2,512]{1,0:T(2,128)(2,1)S(1)}, u32[]{:S(2)}, u32[]{:S(2)}) collective-permute-start(bf16[2,512]{1,0:T(2,128)(2,1)S(1)} %slice.129), channel_id=1, source_target_pairs={{0,8},{8,16},{16,24},{1,9},{9,17},{17,25},{2,10},{10,18},{18,26},{... | collective-permute-start | bytes 6152 | tf_op jit(solution)/shard_map/ppermute | solution.py:13
  63.1 153.9 %collective-permute-start.4 = (bf16[2,512]{1,0:T(2,128)(2,1)S(1)}, bf16[2,512]{1,0:T(2,128)(2,1)S(1)}, u32[]{:S(2)}, u32[]{:S(2)}) collective-permute-start(bf16[2,512]{1,0:T(2,128)(2,1)S(1)} %slice.126), channel_id=1, source_target_pairs={{0,8},{8,16},{16,24},{1,9},{9,17},{17,25},{2,10},{10,18},{18,26},{... | collective-permute-start | bytes 6152 | tf_op jit(solution)/shard_map/ppermute | solution.py:13
  66.5 1104.2 %reduce-scatter.8.cloned.1.call-start = ((), (), s32[]{:S(2)}) async-start(), calls=%async_computation.11 | async-start | bytes 3244032 | tf_op jit(solution)/shard_map/reduce_scatter | solution.py:66
  222.9 6.9 collective-permute-start.1
  252.9 6.9 collective-permute-start
  259.9 81.9 %collective-permute-start = (bf16[128,512]{1,0:T(8,128)(2,1)S(1)}, bf16[128,512]{1,0:T(8,128)(2,1)S(1)}, u32[]{:S(2)}, u32[]{:S(2)}) collective-permute-start(bf16[128,512]{1,0:T(8,128)(2,1)S(1)} %get-tuple-element.1255), channel_id=1, source_target_pairs={{0,8},{8,16},{16,24},{1,9},{9,17},{17,25},{2,10},{10,18},{18,26},{... | collective-permute-start | bytes 393224 | tf_op jit(solution)/shard_map/while/body/eval_jaxpr/ppermute | solution.py:13
  341.8 7.8 collective-permute-start
  417.0 753.7 %reduce-scatter.14.cloned.1.call-start = ((), (), s32[]{:S(2)}) async-start(), calls=%async_computation.14 | async-start | bytes 4325376 | tf_op jit(solution)/shard_map/reduce_scatter | solution.py:70
  422.6 748.1 %reduce-scatter.12.cloned.1.call-start = ((), (), s32[]{:S(2)}) async-start(), calls=%async_computation.13 | async-start | bytes 4325376 | tf_op jit(solution)/shard_map/reduce_scatter | solution.py:69
  428.1 742.6 %reduce-scatter.10.cloned.1.call-start = ((), (), s32[]{:S(2)}) async-start(), calls=%async_computation.12 | async-start | bytes 4325376 | tf_op jit(solution)/shard_map/reduce_scatter | solution.py:68
  432.7 1074.8 %reduce-scatter.6.cloned.1.call-start = ((), (), s32[]{:S(2)}) async-start(), calls=%async_computation.10 | async-start | bytes 51904512 | tf_op jit(solution)/shard_map/reduce_scatter | solution.py:65
  496.5 569.8 %collective-permute-start.6 = (f32[2,512]{1,0:T(2,128)}, f32[2,512]{1,0:T(2,128)}, u32[]{:S(2)}, u32[]{:S(2)}) collective-permute-start(f32[2,512]{1,0:T(2,128)} %pad_maximum_fusion.2), channel_id=1, source_target_pairs={{8,0},{16,8},{24,16},{9,1},{17,9},{25,17},{10,2},{18,10},{26,18},{... | collective-permute-start | bytes 12296 | tf_op jit(solution)/shard_map/ppermute | solution.py:13
  500.0 567.1 %collective-permute-start.7 = (f32[2,512]{1,0:T(2,128)}, f32[2,512]{1,0:T(2,128)}, u32[]{:S(2)}, u32[]{:S(2)}) collective-permute-start(f32[2,512]{1,0:T(2,128)} %pad_maximum_fusion.3), channel_id=1, source_target_pairs={{8,0},{16,8},{24,16},{9,1},{17,9},{25,17},{10,2},{18,10},{26,18},{... | collective-permute-start | bytes 12296 | tf_op jit(solution)/shard_map/ppermute | solution.py:13
  653.7 55.3 %collective-permute-start.3 = (bf16[128,512]{1,0:T(8,128)(2,1)S(1)}, bf16[128,512]{1,0:T(8,128)(2,1)S(1)}, u32[]{:S(2)}, u32[]{:S(2)}) collective-permute-start(bf16[128,512]{1,0:T(8,128)(2,1)S(1)} %get-tuple-element.1305), channel_id=1, source_target_pairs={{8,0},{16,8},{24,16},{9,1},{17,9},{25,17},{10,2},{18,10},{26,18},{... | collective-permute-start | bytes 393224 | tf_op jit(solution)/shard_map/while/body/eval_jaxpr/ppermute | solution.py:13
  709.0 7.9 collective-permute-start.3
  717.0 79.0 %collective-permute-start.3 = (bf16[128,512]{1,0:T(8,128)(2,1)S(1)}, bf16[128,512]{1,0:T(8,128)(2,1)S(1)}, u32[]{:S(2)}, u32[]{:S(2)}) collective-permute-start(bf16[128,512]{1,0:T(8,128)(2,1)S(1)} %get-tuple-element.1305), channel_id=1, source_target_pairs={{8,0},{16,8},{24,16},{9,1},{17,9},{25,17},{10,2},{18,10},{26,18},{... | collective-permute-start | bytes 393224 | tf_op jit(solution)/shard_map/while/body/eval_jaxpr/ppermute | solution.py:13
  796.0 8.5 collective-permute-start.2
  879.2 9.0 collective-permute-start.2
  963.0 7.6 collective-permute-start.2
  (56 other events, 1789.9 us)
Sparse Core Ops, SparseCore 0:
  11.0 158.3 all-gather.5
  172.4 53.1 all-gather.7
  228.6 55.4 all-gather.11
  286.9 55.2 all-gather.9
  345.0 55.2 all-gather.13
  417.1 223.4 reduce-scatter.7
  643.5 143.2 reduce-scatter.13
  789.6 141.2 reduce-scatter.11
  933.7 140.8 reduce-scatter.9
  1081.4 426.0 reduce-scatter.5
where the time goes:
time: 1520 us; the launch traced here: 1510 us
  waiting for transfers between devices  543 us (36%)
  local copies, waits for them, and re-layouts  428 us (28%)
  matrix products  290 us (19%)
  starting transfers between devices  118 us (8%)
  blocking collectives  83.5 us (5%)
  other arithmetic  34 us (2%)
  between operations  17 us (1%)
    gather x14, local copies, waits for them, and re-layouts, filter_block(): picked = jnp.take(table, jnp.clip(lag_grid, 0, table.shape[1] - 1), axis=1)  419 us
    reduce_scatter x1, waiting for transfers between devices, reduce_grads(): lax.psum_scatter(spec_grad, ('seq', 'grp'), scatter_dimension=0, tiled=True)  337 us
    ppermute x16, waiting for transfers between devices, shifted(): return lax.ppermute(shard, axis, pairs)  174 us
    ppermute x16, starting transfers between devices, shifted(): return lax.ppermute(shard, axis, pairs)  118 us
    dot_general x7, matrix products, filter_block(): jnp.einsum('kab,bf->kaf', filt_tile, stacked, precision=HIGHEST, preferre...  94 us
    unnamed x2, blocking collectives  83.5 us
    dot_general x2, matrix products, body(): lax.dot_general(spectral, mixer_grad, (((1,), (0,)), ((), ())), preferred...  62.4 us
    dot_general x2, matrix products, body(): lax.dot_general(back_sum, spec_four, (((0, 2, 3), (0, 1, 3)), ((), ())),...  61.9 us
  transfers between devices with their start and end apart: 26, of which 14 were waited for; matrix products, arithmetic and copies ran while one was open for 48% of the time, Pallas kernels for 0%

commit v1 on v0

v1 whole, which is shorter than its diff:
```python
import functools

import jax
import jax.numpy as jnp
from jax import lax
from jax.experimental import pallas as pl
from jax.experimental.pallas import tpu as pltpu
from jax.sharding import PartitionSpec as P

EPSILON = 1e-05
BF16 = jnp.bfloat16
F32 = jnp.float32
MESH = pl.DeviceIdType.MESH
DMA = pltpu.SemaphoreType.DMA
ANY = pl.BlockSpec(memory_space=pl.ANY)
WHOLE = pl.BlockSpec(memory_space=pltpu.VMEM)
VMEM_LIMIT = 60 * 1024 * 1024
CORES = 2


def dot_nn(a, b):
    return lax.dot_general(a, b, (((1,), (0,)), ((), ())), preferred_element_type=F32)


def dot_tn(a, b):
    return lax.dot_general(a, b, (((0,), (0,)), ((), ())), preferred_element_type=F32)


def dot_nt(a, b):
    return lax.dot_general(a, b, (((1,), (1,)), ((), ())), preferred_element_type=F32)


def params(collective_id=None):
    return pltpu.CompilerParams(
        collective_id=collective_id,
        has_side_effects=collective_id is not None,
        vmem_limit_bytes=VMEM_LIMIT,
    )


def remote(src, dst, send, recv, where):
    return pltpu.make_async_remote_copy(
        src_ref=src, dst_ref=dst, send_sem=send, recv_sem=recv, device_id=where, device_id_type=MESH
    )


def place(seq_count, line):
    s = lax.axis_index("seq")
    g = lax.axis_index("grp")
    return s, lax.div(g, CORES), lax.rem(g, CORES), g


def greet(seq_count, line, s, z, c, g, chain=False, twin=False, side=False, whole_line=False):
    barrier = pltpu.get_barrier_semaphore()

    def call(where):
        pl.semaphore_signal(barrier, inc=1, device_id=where, device_id_type=MESH)

    expected = (1 if twin else 0) + (seq_count - 1 if side else 0) + (line - 1 if whole_line else 0)
    if twin:
        call({"grp": g + 1 - 2 * c})
    if side:
        for i in range(1, seq_count):
            call({"seq": lax.rem(s + i, seq_count)})
    if whole_line:
        for j in range(1, line):
            call({"grp": lax.rem(g + CORES * j, CORES * line)})
    if chain:
        expected = expected + (z > 0).astype(jnp.int32) + (z < line - 1).astype(jnp.int32)

        @pl.when(z > 0)
        def _():
            call({"grp": g - CORES})

        @pl.when(z < line - 1)
        def _():
            call({"grp": g + CORES})

    pl.semaphore_wait(barrier, expected)


def line_conditions(line, z, way, t):
    if way == 0:
        return (z < line - 1) & (z >= t), z >= t + 1, z - t, z - 1 - t
    return (z > 0) & (z + t <= line - 1), z + t + 1 <= line - 1, z + t, z + 1 + t


def gather_kernel(seq_count, line, n_deep, n_wide, *refs):
    n_in = 1 + n_deep + n_wide
    ins, outs = refs[:n_in], refs[n_in : 2 * n_in]
    rest = refs[2 * n_in :]
    stage = rest[:n_in]
    (local_sem, tok_send, tok_recv, zs, zr, ws, wr, ps, pr, dps, dpr) = rest[n_in:]
    s, z, c, g = place(seq_count, line)
    twin = {"grp": g + 1 - 2 * c}
    tok, tok_out = ins[0], outs[0]
    rows = tok.shape[1]
    items = list(range(n_deep + n_wide))

    def own(i, l):
        out = outs[1 + i]
        return out.at[l, c] if i < n_deep else out.at[s, l, c]

    loads = [pltpu.make_async_copy(ins[i], stage[i], local_sem.at[0, i]) for i in range(n_in)]
    for x in loads:
        x.start()
    greet(seq_count, line, s, z, c, g, chain=True, twin=True, side=True)

    toks = []
    for i in range(1, seq_count):
        toks.append(
            remote(
                tok,
                tok_out.at[:, pl.ds(pl.multiple_of(s * rows, rows), rows), :],
                tok_send.at[i - 1],
                tok_recv.at[i - 1],
                {"seq": lax.rem(s + i, seq_count)},
            )
        )
        toks[-1].start()

    def hop(i, way, t, origin):
        src = ins[1 + i] if t == 0 else own(i, origin)
        to = g + CORES if way == 0 else g - CORES
        return remote(src, own(i, origin), zs.at[i, way, t], zr.at[i, way, t], {"grp": to})

    def hops(which, t):
        for way in (0, 1):
            sends, _, origin, _ = line_conditions(line, z, way, t)

            @pl.when(sends)
            def _():
                for i in which:
                    hop(i, way, t, origin).start()

    def arrive(which, t, after=None):
        for way in (0, 1):
            _, receives, _, origin = line_conditions(line, z, way, t)

            @pl.when(receives)
            def _():
                for i in which:
                    hop(i, way, t, origin).wait_recv()
                if after is not None:
                    after(origin)

    deep, wide = items[:n_deep], items[n_deep:]
    for t in range(line - 1):
        hops(wide, t)
        if t == 0:
            stores = []
            for i in range(n_in):
                loads[i].wait()
                dst = (
                    tok_out.at[:, pl.ds(pl.multiple_of(s * rows, rows), rows), :]
                    if i == 0
                    else own(i - 1, z)
                )
                stores.append(pltpu.make_async_copy(stage[i], dst, local_sem.at[1, i]))
                stores[-1].start()
        arrive(wide, t)
    hops(deep, 0)
    for x in stores:
        x.wait()
    sides = []
    for i in wide:
        for j in range(1, seq_count):
            part = outs[1 + i].at[s, :, c]
            sides.append(
                remote(
                    part,
                    part,
                    ws.at[i - n_deep, j - 1],
                    wr.at[i - n_deep, j - 1],
                    {"seq": lax.rem(s + j, seq_count)},
                )
            )
            sides[-1].start()

    def twin_wide(i, k):
        part = outs[1 + i].at[k, :, c]
        return remote(part, part, ps.at[i - n_deep, k], pr.at[i - n_deep, k], twin)

    def twin_deep(i, l):
        part = outs[1 + i].at[l, c]
        return remote(part, part, dps.at[i, l], dpr.at[i, l], twin)

    for i in wide:
        twin_wide(i, s).start()
    for i in deep:
        twin_deep(i, z).start()

    def pass_on(origin):
        for i in deep:
            twin_deep(i, origin).start()

    for t in range(line - 1):
        if t > 0:
            hops(deep, t)
        arrive(deep, t, pass_on)
    for x in sides:
        x.wait_recv()
    for i in wide:
        for j in range(1, seq_count):
            twin_wide(i, lax.rem(s + seq_count - j, seq_count)).start()
    for x in toks:
        x.wait_recv()
    for i in deep:
        for l in range(line):
            twin_deep(i, l).wait()
    for i in wide:
        for k in range(seq_count):
            twin_wide(i, k).wait()
    for x in toks + sides:
        x.wait_send()
    for t in range(line - 1):
        for way in (0, 1):
            sends, _, origin, _ = line_conditions(line, z, way, t)

            @pl.when(sends)
            def _():
                for i in items:
                    hop(i, way, t, origin).wait_send()


def gather_all(seq_count, line, tok, deep, wide):
    n_deep, n_wide = len(deep), len(wide)
    shapes = [
        jax.ShapeDtypeStruct((tok.shape[0], tok.shape[1] * seq_count, tok.shape[2]), tok.dtype)
    ]
    shapes += [jax.ShapeDtypeStruct((line, CORES) + x.shape, x.dtype) for x in deep]
    shapes += [jax.ShapeDtypeStruct((seq_count, line, CORES) + x.shape, x.dtype) for x in wide]
    arrays = [tok] + list(deep) + list(wide)
    n = len(arrays)
    scratch = [pltpu.VMEM(x.shape, x.dtype) for x in arrays]
    scratch += [
        DMA((2, n)),
        DMA((seq_count - 1,)),
        DMA((seq_count - 1,)),
        DMA((n_deep + n_wide, 2, line - 1)),
        DMA((n_deep + n_wide, 2, line - 1)),
        DMA((n_wide, seq_count - 1)),
        DMA((n_wide, seq_count - 1)),
        DMA((n_wide, seq_count)),
        DMA((n_wide, seq_count)),
        DMA((n_deep, line)),
        DMA((n_deep, line)),
    ]
    return pl.pallas_call(
        functools.partial(gather_kernel, seq_count, line, n_deep, n_wide),
        out_shape=shapes,
        in_specs=[ANY] * n,
        out_specs=[ANY] * n,
        scratch_shapes=scratch,
        compiler_params=params(1),
        name="gather_all",
    )(*arrays)


def side_gather_kernel(seq_count, line, x_ref, out_ref, local_sem, send, recv):
    s, z, c, g = place(seq_count, line)
    rows = x_ref.shape[1]
    mine = out_ref.at[:, pl.ds(pl.multiple_of(s * rows, rows), rows), :]
    local = pltpu.make_async_copy(x_ref, mine, local_sem)
    local.start()
    greet(seq_count, line, s, z, c, g, side=True)
    copies = []
    for i in range(1, seq_count):
        copies.append(
            remote(
                x_ref, mine, send.at[i - 1], recv.at[i - 1], {"seq": lax.rem(s + i, seq_count)}
            )
        )
        copies[-1].start()
    local.wait()
    for x in copies:
        x.wait()


def side_gather(seq_count, line, x):
    return pl.pallas_call(
        functools.partial(side_gather_kernel, seq_count, line),
        out_shape=jax.ShapeDtypeStruct((x.shape[0], x.shape[1] * seq_count, x.shape[2]), x.dtype),
        in_specs=[WHOLE],
        out_specs=WHOLE,
        scratch_shapes=[DMA, DMA((seq_count - 1,)), DMA((seq_count - 1,))],
        compiler_params=params(2),
        name="side_gather",
    )(x)


def side_sum_kernel(seq_count, line, x_ref, out_ref, slots, send, recv):
    s, z, c, g = place(seq_count, line)
    rows = out_ref.shape[1]
    greet(seq_count, line, s, z, c, g, side=True)
    copies = []
    for i in range(1, seq_count):
        to = lax.rem(s + i, seq_count)
        copies.append(
            remote(
                x_ref.at[:, pl.ds(pl.multiple_of(to * rows, rows), rows), :],
                slots.at[i - 1],
                send.at[i - 1],
                recv.at[i - 1],
                {"seq": to},
            )
        )
        copies[-1].start()
    total = x_ref[:, pl.ds(pl.multiple_of(s * rows, rows), rows), :].astype(F32)
    for i, x in enumerate(copies):
        x.wait_recv()
        total = total + slots[i].astype(F32)
    out_ref[...] = total
    for x in copies:
        x.wait_send()


def side_sum(seq_count, line, x, collective_id):
    rows = x.shape[1] // seq_count
    return pl.pallas_call(
        functools.partial(side_sum_kernel, seq_count, line),
        out_shape=jax.ShapeDtypeStruct((x.shape[0], rows, x.shape[2]), F32),
        in_specs=[WHOLE],
        out_specs=WHOLE,
        scratch_shapes=[
            pltpu.VMEM((seq_count - 1, x.shape[0], rows, x.shape[2]), x.dtype),
            DMA((seq_count - 1,)),
            DMA((seq_count - 1,)),
        ],
        compiler_params=params(collective_id),
        name=f"side_sum_{collective_id}",
    )(x)


def sum_kernel(seq_count, line, n_deep, n_wide, *refs):
    n = n_deep + n_wide
    ins, outs = refs[: n + 1], refs[n + 1 : 2 * n + 2]
    rest = refs[2 * n + 2 :]
    pair, side, chain = rest[:n], rest[n : n + n_wide], rest[n + n_wide : 2 * n + n_wide]
    rest = rest[2 * n + n_wide :]
    g_pair, g_side, g_line, g_a, g_b = rest[:5]
    (ps, pr, ws, wr, zs, zr, gs, gr) = rest[5:]
    s, z, c, g = place(seq_count, line)
    twin = {"grp": g + 1 - 2 * c}
    deep, wide = list(range(n_deep)), list(range(n_deep, n))
    small = ins[n]
    greet(seq_count, line, s, z, c, g, twin=True, side=True, whole_line=True)

    def theirs(i):
        return ins[i].at[:, 1 - c] if i < n_deep else ins[i].at[:, :, 1 - c]

    pairs = [remote(theirs(i), pair[i], ps.at[i], pr.at[i], twin) for i in range(n)]
    small_pair = remote(small, g_pair, gs.at[0], gr.at[0], twin)
    small_pair.start()
    for x in pairs[n_deep:] + pairs[:n_deep]:
        x.start()

    small_pair.wait()
    g_a[...] = small[...] + g_pair[...]
    small_sides = []
    for j in range(1, seq_count):
        small_sides.append(
            remote(
                g_a,
                g_side.at[j - 1],
                gs.at[j],
                gr.at[j],
                {"seq": lax.rem(s + j, seq_count)},
            )
        )
        small_sides[-1].start()

    for i in wide:
        pairs[i].wait_recv()
        for k in range(seq_count):

            @pl.loop(0, line)
            def _(l):
                mixed = ins[i][k, l, c].astype(F32) + pair[i][k, l].astype(F32)
                pair[i][k, l] = mixed.astype(BF16)

    sides = {}
    for i in wide:
        for j in range(1, seq_count):
            to = lax.rem(s + j, seq_count)
            sides[i, j] = remote(
                pair[i].at[to],
                side[i - n_deep].at[j - 1],
                ws.at[i - n_deep, j - 1],
                wr.at[i - n_deep, j - 1],
                {"seq": to},
            )
            sides[i, j].start()
    for i in deep:
        pairs[i].wait_recv()
        for l in range(line):
            pair[i][l] = (ins[i][l, c].astype(F32) + pair[i][l].astype(F32)).astype(BF16)

    for x in small_sides:
        x.wait()
    total = g_a[...]
    for j in range(seq_count - 1):
        total = total + g_side[j]
    g_b[...] = total
    small_lines = []
    for j in range(1, line):
        small_lines.append(
            remote(
                g_b,
                g_line.at[j - 1],
                gs.at[seq_count - 1 + j],
                gr.at[seq_count - 1 + j],
                {"grp": lax.rem(g + CORES * j, CORES * line)},
            )
        )
        small_lines[-1].start()

    def piece(i, l):
        return pair[i].at[l] if i < n_deep else pair[i].at[s, l]

    def run_line(which):
        def hop(i, way, t, dest, first):
            src = piece(i, dest) if first else chain[i].at[way, t]
            to = g + CORES if way == 0 else g - CORES
            return remote(src, chain[i].at[way, t], zs.at[i, way, t], zr.at[i, way, t], {"grp": to})

        for t in range(line - 1):
            for way in (0, 1):
                dest = line - 1 - t if way == 0 else t
                starts = z == 0 if way == 0 else z == line - 1
                relays = (z > 0) & (z < dest) if way == 0 else (z < line - 1) & (z > dest)

                @pl.when(starts)
                def _():
                    for i in which:
                        hop(i, way, t, dest, True).start()

                @pl.when(relays)
                def _():
                    for i in which:
                        hop(i, way, t, dest, False).wait_recv()
                        mixed = chain[i][way, t].astype(F32) + piece(i, dest)[...].astype(F32)
                        chain[i][way, t] = mixed.astype(BF16)
                        hop(i, way, t, dest, False).start()

        for i in which:
            outs[i][...] = piece(i, z)[...].astype(F32)
        for t in range(line - 1):
            for way in (0, 1):
                dest = line - 1 - t if way == 0 else t

                @pl.when((z == dest))
                def _():
                    for i in which:
                        hop(i, way, t, dest, False).wait_recv()
                        outs[i][...] += chain[i][way, t].astype(F32)

                @pl.when(z == 0 if way == 0 else z == line - 1)
                def _():
                    for i in which:
                        hop(i, way, t, dest, True).wait_send()

                @pl.when((z > 0) & (z < dest) if way == 0 else (z < line - 1) & (z > dest))
                def _():
                    for i in which:
                        hop(i, way, t, dest, False).wait_send()

    run_line(deep)
    for i in wide:
        for j in range(1, seq_count):
            sides[i, j].wait()

        @pl.loop(0, line)
        def _(l):
            mixed = pair[i][s, l].astype(F32)
            for j in range(1, seq_count):
                mixed = mixed + side[i - n_deep][j - 1, l].astype(F32)
            pair[i][s, l] = mixed.astype(BF16)

    run_line(wide)
    for x in pairs:
        x.wait_send()
    for x in small_lines:
        x.wait()
    total = g_b[...]
    for j in range(line - 1):
        total = total + g_line[j]
    outs[n][...] = total


def sum_all(seq_count, line, deep, wide, small):
    n_deep, n_wide = len(deep), len(wide)
    n = n_deep + n_wide
    shapes = [jax.ShapeDtypeStruct(x.shape[2:], F32) for x in deep]
    shapes += [jax.ShapeDtypeStruct(x.shape[3:], F32) for x in wide]
    shapes += [jax.ShapeDtypeStruct(small.shape, F32)]
    scratch = [pltpu.VMEM((line,) + x.shape[2:], BF16) for x in deep]
    scratch += [pltpu.VMEM((seq_count, line) + x.shape[3:], BF16) for x in wide]
    scratch += [pltpu.VMEM((seq_count - 1, line) + x.shape[3:], BF16) for x in wide]
    scratch += [pltpu.VMEM((2, line - 1) + x.shape[2:], BF16) for x in deep]
    scratch += [pltpu.VMEM((2, line - 1) + x.shape[3:], BF16) for x in wide]
    scratch += [
        pltpu.VMEM(small.shape, F32),
        pltpu.VMEM((seq_count - 1,) + small.shape, F32),
        pltpu.VMEM((line - 1,) + small.shape, F32),
        pltpu.VMEM(small.shape, F32),
        pltpu.VMEM(small.shape, F32),
        DMA((n,)),
        DMA((n,)),
        DMA((n_wide, seq_count - 1)),
        DMA((n_wide, seq_count - 1)),
        DMA((n, 2, line - 1)),
        DMA((n, 2, line - 1)),
        DMA((seq_count + line,)),
        DMA((seq_count + line,)),
    ]
    return pl.pallas_call(
        functools.partial(sum_kernel, seq_count, line, n_deep, n_wide),
        out_shape=shapes,
        in_specs=[WHOLE] * (n + 1),
        out_specs=[WHOLE] * (n + 1),
        scratch_shapes=scratch,
        compiler_params=params(5),
        name="sum_all",
    )(*deep, *wide, small)


def signs_of(rows):
    pos = lax.broadcasted_iota(jnp.int32, (rows, 1), 0)
    return 1.0 - 2.0 * lax.rem(pos, 2).astype(F32)


def lagged(values, lag, span):
    pos = lax.broadcasted_iota(jnp.int32, (values.shape[0], 1), 0)
    return jnp.where(lax.rem(pos, span) >= lag, pltpu.roll(values, lag, 0), 0.0)


def led(values, lag, span):
    rows = values.shape[0]
    pos = lax.broadcasted_iota(jnp.int32, (rows, 1), 0)
    return jnp.where(lax.rem(pos, span) < span - lag, pltpu.roll(values, rows - lag, 0), 0.0)


def spread(row, rows):
    wide = jnp.broadcast_to(row, (rows, row.shape[1]))
    return pltpu.roll(wide, 0, 1, stride=1, stride_axis=0)[:, :rows].astype(BF16)


def forward_kernel(spans, x_ref, gain_ref, row_ref, w_ref, ar_ref, ul_ref, u_ref, y_ref, both, acc):
    k = pl.program_id(0)
    rows, width = x_ref.shape[1], x_ref.shape[2]
    signs = signs_of(rows)

    @pl.when(k == 0)
    def _():
        for m in range(2):
            x = x_ref[m].astype(F32)
            inv = lax.rsqrt(jnp.mean(x * x, axis=-1, keepdims=True) + EPSILON)
            u = (x * inv * gain_ref[...]).astype(BF16)
            wide = u.astype(F32)
            u_ref[m] = u
            both[m, :, :width] = u
            both[m, :, width:] = (wide * signs).astype(BF16)
            acc[m] = dot_nn(u, ar_ref[:width])
            for lag in (1, 2):
                acc[m] += dot_nn(
                    lagged(wide, lag, spans[m]).astype(BF16),
                    ar_ref[lag * width : (lag + 1) * width],
                )

    table = spread(row_ref[0], rows)
    for m in range(2):
        span = spans[m]
        for j in range(rows // span):
            part = slice(j * span, (j + 1) * span)
            conv = dot_nn(table[:span, :span], both[m, part, :])
            plus = conv[:, :width].astype(BF16)
            minus = (conv[:, width:] * signs[part]).astype(BF16)
            ul_ref[0, 0, m, part, :] = plus
            ul_ref[0, 1, m, part, :] = minus
        acc[m] += dot_nn(ul_ref[0, 0, m], w_ref[0, 0]) + dot_nn(ul_ref[0, 1, m], w_ref[0, 1])

    @pl.when(k == pl.num_programs(0) - 1)
    def _():
        y_ref[...] = acc[...].astype(BF16)


def forward_mix(spans, x, gain, table, w, ar):
    count = table.shape[0]
    _, rows, width = x.shape
    full = lambda *shape: pl.BlockSpec(shape, lambda k: (0,) * len(shape))
    return pl.pallas_call(
        functools.partial(forward_kernel, spans),
        grid=(count,),
        out_shape=[
            jax.ShapeDtypeStruct((count, 2, 2, rows, width), BF16),
            jax.ShapeDtypeStruct((2, rows, width), BF16),
            jax.ShapeDtypeStruct((2, rows, width), BF16),
        ],
        in_specs=[
            full(2, rows, width),
            full(1, width),
            pl.BlockSpec((1, 1, 2 * rows), lambda k: (k, 0, 0)),
            pl.BlockSpec((1, 2, width, width), lambda k: (k, 0, 0, 0)),
            full(3 * width, width),
        ],
        out_specs=[
            pl.BlockSpec((1, 2, 2, rows, width), lambda k: (k, 0, 0, 0, 0)),
            full(2, rows, width),
            full(2, rows, width),
        ],
        scratch_shapes=[pltpu.VMEM((2, rows, 2 * width), BF16), pltpu.VMEM((2, rows, width), F32)],
        compiler_params=params(),
        name="forward_mix",
    )(x, gain, table, w, ar)


def backward_kernel(
    spans, dy_ref, u_ref, row_ref, w_ref, ul_ref, ar_ref, dw_ref, dar_ref, du_ref, both, acc
):
    k = pl.program_id(0)
    rows, width = dy_ref.shape[1], dy_ref.shape[2]
    signs = signs_of(rows)

    @pl.when(k == 0)
    def _():
        for m in range(2):
            dy = dy_ref[m]
            both[m, :, :width] = dy
            both[m, :, width:] = (dy.astype(F32) * signs).astype(BF16)
            acc[m] = dot_nt(dy, ar_ref[:width])
            for lag in (1, 2):
                acc[m] += led(
                    dot_nt(dy, ar_ref[lag * width : (lag + 1) * width]), lag, spans[m]
                )
        for lag in (0, 1, 2):
            total = 0.0
            for m in range(2):
                u = u_ref[m]
                if lag:
                    u = lagged(u.astype(F32), lag, spans[m]).astype(BF16)
                total = total + dot_tn(u, dy_ref[m])
            dar_ref[lag * width : (lag + 1) * width, :] = total.astype(BF16)

    table = spread(row_ref[0], rows)
    for m in range(2):
        span = spans[m]
        for j in range(rows // span):
            part = slice(j * span, (j + 1) * span)
            conv = dot_nn(table[:span, :span], both[m, part, :])
            plus = conv[:, :width].astype(BF16)
            minus = (conv[:, width:] * signs[part]).astype(BF16)
            acc[m, part, :] += dot_nt(plus, w_ref[0, 0]) + dot_nt(minus, w_ref[0, 1])
    for p in range(2):
        total = dot_tn(ul_ref[0, p, 0], dy_ref[0]) + dot_tn(ul_ref[0, p, 1], dy_ref[1])
        dw_ref[0, p] = total.astype(BF16)

    @pl.when(k == pl.num_programs(0) - 1)
    def _():
        du_ref[...] = acc[...].astype(BF16)


def backward_mix(spans, dy, u, table, w, ul, ar):
    count = table.shape[0]
    _, rows, width = dy.shape
    full = lambda *shape: pl.BlockSpec(shape, lambda k: (0,) * len(shape))
    return pl.pallas_call(
        functools.partial(backward_kernel, spans),
        grid=(count,),
        out_shape=[
            jax.ShapeDtypeStruct((count, 2, width, width), BF16),
            jax.ShapeDtypeStruct((3 * width, width), BF16),
            jax.ShapeDtypeStruct((2, rows, width), BF16),
        ],
        in_specs=[
            full(2, rows, width),
            full(2, rows, width),
            pl.BlockSpec((1, 1, 2 * rows), lambda k: (k, 0, 0)),
            pl.BlockSpec((1, 2, width, width), lambda k: (k, 0, 0, 0)),
            pl.BlockSpec((1, 2, 2, rows, width), lambda k: (k, 0, 0, 0, 0)),
            full(3 * width, width),
        ],
        out_specs=[
            pl.BlockSpec((1, 2, width, width), lambda k: (k, 0, 0, 0)),
            full(3 * width, width),
            full(2, rows, width),
        ],
        scratch_shapes=[pltpu.VMEM((2, rows, 2 * width), BF16), pltpu.VMEM((2, rows, width), F32)],
        compiler_params=params(),
        name="backward_mix",
    )(dy, u, table, w, ul, ar)


def body(
    tokens,
    layout,
    filters,
    gain_mix,
    spectral_proj,
    ar_proj,
    gain_mlp,
    w_gate,
    w_up,
    w_down,
    out_grad,
):
    seq_count = lax.axis_size("seq")
    line = lax.axis_size("grp") // CORES
    s = lax.axis_index("seq")
    g = lax.axis_index("grp")
    block, width = tokens.shape[2], tokens.shape[3]
    rows = block * seq_count
    count = filters.shape[1] // seq_count
    hidden_units = w_gate.shape[1]
    spans = (rows, rows // 4)

    swap = layout[0, 0] == 1
    own = jnp.where(swap, tokens[::-1, 0], tokens[:, 0])
    cotangent = jnp.where(swap, out_grad[::-1, 0], out_grad[:, 0])
    share = gain_mix.shape[0]
    gains = jnp.zeros((16, 128), BF16)
    gains = gains.at[0, :share].set(gain_mix).at[1, :share].set(gain_mlp)

    x_all, spec, ar, gate_w, up_w, down_w, gains = gather_all(
        seq_count, line, own, (spectral_proj, ar_proj), (w_gate, w_up, w_down, gains)
    )
    spec = spec.reshape(count, 2, width, width)
    ar_rows = ar.shape[0] * ar.shape[1] * ar.shape[2]
    ar_full = lax.dynamic_update_slice(
        jnp.zeros((3 * width, width), BF16), ar.reshape(ar_rows, width), (s * ar_rows, 0)
    )
    gate_w = gate_w.reshape(width, hidden_units)
    up_w = up_w.reshape(width, hidden_units)
    down_w = down_w.reshape(hidden_units, width)
    gains = gains.reshape(-1, 16, 128).astype(F32)
    mix_scale = gains[:, 0, :share].reshape(1, width)
    mlp_scale = gains[:, 1, :share].reshape(1, width)

    mine = lax.dynamic_slice(filters.T, (s * count, 0), (count, rows))[:, None, :]
    nothing = jnp.zeros((count, 1, rows), F32)
    back_table = jnp.concatenate([mine, nothing], axis=2)
    fore_table = jnp.concatenate([mine[:, :, :1], nothing, mine[:, :, :0:-1]], axis=2)

    ul, u, y = forward_mix(spans, x_all, mix_scale, fore_table, spec, ar_full)
    mixer = side_sum(seq_count, line, y, 3).reshape(2 * block, width)

    inputs = own.reshape(2 * block, width).astype(F32)
    cot = cotangent.reshape(2 * block, width)
    hidden = inputs + mixer
    inv_two = lax.rsqrt(jnp.mean(hidden * hidden, axis=-1, keepdims=True) + EPSILON)
    mlp_in = (hidden * inv_two * mlp_scale).astype(BF16)
    gate = dot_nn(mlp_in, gate_w)
    upval = dot_nn(mlp_in, up_w)
    product_val, gelu_pull = jax.vjp(lambda a, b: jax.nn.gelu(a) * b, gate, upval)
    mixed = product_val.astype(BF16)
    out = hidden + dot_nn(mixed, down_w)
    down_grad = dot_tn(mixed, cot)
    mixed_grad = dot_nt(cot, down_w)
    gate_back, up_back = gelu_pull(mixed_grad)
    gate_back = gate_back.astype(BF16)
    up_back = up_back.astype(BF16)
    gate_grad = dot_tn(mlp_in, gate_back)
    up_grad = dot_tn(mlp_in, up_back)
    mlp_in_grad = dot_nt(gate_back, gate_w) + dot_nt(up_back, up_w)
    scaled_two = mlp_in_grad * mlp_scale
    mlp_grad = jnp.sum(mlp_in_grad * hidden * inv_two, axis=0, keepdims=True)
    hidden_grad = (
        cot.astype(F32)
        + inv_two * scaled_two
        - hidden * inv_two**3 * jnp.mean(scaled_two * hidden, axis=-1, keepdims=True)
    )
    mixer_grad = hidden_grad.astype(BF16)

    dy = side_gather(seq_count, line, mixer_grad.reshape(2, block, width))
    dw, dar, du = backward_mix(spans, dy, u, back_table, spec, ul, ar_full)
    normed_grad = side_sum(seq_count, line, du, 4).reshape(2 * block, width)

    inv_one = lax.rsqrt(jnp.mean(inputs * inputs, axis=-1, keepdims=True) + EPSILON)
    scaled_one = normed_grad * mix_scale
    mix_grad = jnp.sum(normed_grad * inputs * inv_one, axis=0, keepdims=True)
    input_grad = (
        hidden_grad
        + inv_one * scaled_one
        - inputs * inv_one**3 * jnp.mean(scaled_one * inputs, axis=-1, keepdims=True)
    )

    dar = lax.dynamic_slice(dar, (s * ar_rows, 0), (ar_rows, width))
    deep = (dw.reshape(line, CORES, -1, width), dar.reshape(line, CORES, -1, width))
    wide = tuple(
        x.astype(BF16).reshape(seq_count, line, CORES, -1, x.shape[1])
        for x in (gate_grad, up_grad, down_grad)
    )
    small = jnp.concatenate([mix_grad, mlp_grad, jnp.zeros((6, width), F32)], axis=0)
    dw, dar, gate_grad, up_grad, down_grad, small = sum_all(seq_count, line, deep, wide, small)
    small = lax.dynamic_slice(small, (0, (s * CORES * line + g) * share), (2, share))

    def settle(x):
        x = x.reshape(2, 1, block, width)
        return jnp.where(swap, x[::-1], x)

    return (
        settle(out),
        settle(input_grad),
        small[0],
        dw,
        dar,
        small[1],
        gate_grad,
        up_grad,
        down_grad,
    )


def solution(mesh):
    placed = (
        P(None, "grp", "seq", None),
        P(None, "grp"),
        P(),
        P(("seq", "grp")),
        P(("seq", "grp"), None),
        P(("seq", "grp"), None),
        P(("seq", "grp")),
        P(("seq", "grp"), None),
        P(("seq", "grp"), None),
        P(("seq", "grp"), None),
        P(None, "grp", "seq", None),
    )
    return jax.shard_map(
        body,
        mesh=mesh,
        in_specs=placed,
        out_specs=(
            P(None, "grp", "seq", None),
            P(None, "grp", "seq", None),
            P(("seq", "grp")),
            P(("seq", "grp"), None),
            P(("seq", "grp"), None),
            P(("seq", "grp")),
            P(("seq", "grp"), None),
            P(("seq", "grp"), None),
            P(("seq", "grp"), None),
        ),
        check_vma=False,
    )
```

time: 1520 us -> 350 us (0.23)
  waiting for transfers between devices: 543 us -> 0 us
  local copies, waits for them, and re-layouts: 428 us -> 16.2 us
  Pallas kernels: 0 us -> 303 us
  matrix products: 290 us -> 15.4 us
  starting transfers between devices: 118 us -> 0 us
  blocking collectives: 83.5 us -> 0 us
  other arithmetic: 34 us -> 12.8 us
  between operations: 17 us -> 1.68 us
    gather x14 -> x0, local copies, waits for them, and re-layouts: 419 us -> none  [filter_block(): picked = jnp.take(table, jnp.clip(lag_grid, 0, table.shape[1] - 1), axis=1)]
    reduce_scatter x5 -> x0, waiting for transfers between devices: 337 us -> none  [the longest x1 337 us: reduce_grads(): lax.psum_scatter(spec_grad, ('seq', 'grp'), scatter_dimension=0, tiled=True)]
    pallas_call x0 -> x7, Pallas kernels: none -> 303 us  [the longest x1 116 us: sum_all(): pl.pallas_call(functools.partial(sum_kernel, seq_count, line, n_deep, n_w...]
    dot_general x37 -> x9, matrix products: 290 us -> 15.4 us  [the longest x3 6.37 us: dot_tn(): lax.dot_general(a, b, (((0,), (0,)), ((), ())), preferred_element_type=F32)]
    ppermute x16 -> x0, waiting for transfers between devices: 174 us -> none  [shifted(): return lax.ppermute(shard, axis, pairs)]
    ppermute x16 -> x0, starting transfers between devices: 118 us -> none  [shifted(): return lax.ppermute(shard, axis, pairs)]
    unnamed x2 -> x0, blocking collectives: 83.5 us -> none
    all_gather x5 -> x0, waiting for transfers between devices: 29.1 us -> none  [the longest x1 29.1 us: fetch(): lax.all_gather(w_down, ('seq', 'grp'), axis=0, tiled=True)]
  transfers between devices with their start and end apart: 26 -> 0, of which waited for: 14 -> 0; matrix products, arithmetic and copies ran while one was open for 48% -> 0% of each run, Pallas kernels for 0% -> 0%
where the time goes in v1:
time: 350 us; the launch traced here: 349 us
  Pallas kernels  303 us (87%)
  local copies, waits for them, and re-layouts  16.2 us (5%)
  matrix products  15.4 us (4%)
  other arithmetic  12.8 us (4%)
    pallas_call x1, Pallas kernels, sum_all(): pl.pallas_call(functools.partial(sum_kernel, seq_count, line, n_deep, n_w...  116 us
    pallas_call x1, Pallas kernels, gather_all(): pl.pallas_call(functools.partial(gather_kernel, seq_count, line, n_deep,...  83 us
    pallas_call x1, Pallas kernels, backward_mix(): pl.pallas_call(functools.partial(backward_kernel, spans), grid=(count,),...  34.9 us
    pallas_call x2, Pallas kernels, side_sum(): pl.pallas_call(functools.partial(side_sum_kernel, seq_count, line), out_s...  32.5 us
    pallas_call x1, Pallas kernels, forward_mix(): pl.pallas_call(functools.partial(forward_kernel, spans), grid=(count,), o...  19.5 us
    pallas_call x1, Pallas kernels, side_gather(): pl.pallas_call(functools.partial(side_gather_kernel, seq_count, line), ou...  16.9 us
    unnamed x41, local copies, waits for them, and re-layouts  8.62 us

profile of v1, /device:TPU:0, one launch (start us, length us, event | category | flops | bytes accessed | tf_op | source)
XLA Modules:
  0.0 349.2 jit_solution(3986307088871538959)
XLA Ops:
  1.4 1.2 fusion.15
  6.1 1.1 reverse_select_fusion.2
  7.3 1.8 fusion.17.refs_0_
  9.1 83.0 %gather_all.1 = (bf16[2,512,512]{2,1,0:T(8,128)(2,1)}, bf16[4,2,768,512]{3,2,1,0:T(8,128)(2,1)}, bf16[4,2,48,512]{3,2,1,0:T(8,128)(2,1)}, bf16[4,4,2,16,2048]{4,...) custom-call(bf16[2,128,512]{2,1,0:T(8,128)(2,1)} %fusion.17.refs_0_,, ...), custom_call_target="tpu_custom_call" | custom-call | tf_op jit(solution)/shard_map/gather_all/pallas_call | solution.py:249
  92.2 1.0 constant_dynamic-update-slice_fusion.ar_ref
  94.4 3.7 %fusion.23 = f32[256,2048]{1,0:T(8,128)} fusion(bf16[256,512]{1,0:T(8,128)(2,1)S(1)} %bitcast.115, bf16[2048,512]{1,0:T(8,128)(2,1)} %bitcast.112), kind=kOutput, calls=%fused_computation.65 | convolution fusion | flops 536870912 | bytes 4456448 | tf_op jit(solution)/shard_map/dot_general | solution.py:30
  98.1 19.5 %forward_mix.1 = (bf16[6,2,2,512,512]{4,3,2,1,0:T(8,128)(2,1)}, bf16[2,512,512]{2,1,0:T(8,128)(2,1)}, bf16[2,512,512]{2,1,0:T(8,128)(2,1)}) custom-call(bf16[2,512,512]{2,1,0:T(8,128)(2,1)} %get-tuple-element.52.x_ref, f32[1,512]{1,0:T(1,128)} %reshape_squeeze.4.gain_ref, f32[6,1,1024]{2,1,0:T(1,128)} %pad_maximum_fusion.row_ref, ...), custom_call_target="tpu_custom_call" | custom-call | tf_op jit(solution)/shard_map/forward_mix/pallas_call | solution.py:592
  117.5 16.9 %side_sum_3.1 = f32[2,128,512]{2,1,0:T(8,128)} custom-call(bf16[2,512,512]{2,1,0:T(8,128)(2,1)} %get-tuple-element.56.x_ref), custom_call_target="tpu_custom_call" | custom-call | tf_op jit(solution)/shard_map/side_sum_3/pallas_call | solution.py:320
  134.4 1.2 multiply_reduce_fusion.2
  135.7 1.2 multiply_convert_fusion.3
  139.1 2.2 multiply_convert_fusion.1
  145.0 1.1 fusion.20
  146.1 16.9 %side_gather.1.dy_ref = bf16[2,512,512]{2,1,0:T(8,128)(2,1)} custom-call(bf16[2,128,512]{2,1,0:T(8,128)(2,1)} %bitcast.126), custom_call_target="tpu_custom_call" | custom-call | tf_op jit(solution)/shard_map/side_gather/pallas_call | solution.py:281
  163.0 34.9 %backward_mix.1 = (bf16[6,2,512,512]{3,2,1,0:T(8,128)(2,1)}, bf16[1536,512]{1,0:T(8,128)(2,1)}, bf16[2,512,512]{2,1,0:T(8,128)(2,1)}) custom-call(bf16[2,512,512]{2,1,0:T(8,128)(2,1)} %side_gather.1.dy_ref, bf16[2,512,512]{2,1,0:T(8,128)(2,1)} %get-tuple-element.60.u_ref, f32[6,1,1024]{2,1,0:T(1,128)} %concatenate.14.row_ref, ...), custom_call_target="tpu_custom_call" | custom-call | tf_op jit(solution)/shard_map/backward_mix/pallas_call | solution.py:667
  197.9 15.6 %side_sum_4.1 = f32[2,128,512]{2,1,0:T(8,128)} custom-call(bf16[2,512,512]{2,1,0:T(8,128)(2,1)} %get-tuple-element.62.x_ref), custom_call_target="tpu_custom_call" | custom-call | tf_op jit(solution)/shard_map/side_sum_4/pallas_call | solution.py:320
  213.5 1.3 fusion.9
  214.8 1.4 fusion.14
  216.2 1.1 fusion.10
  218.0 1.8 constant_dynamic-slice_fusion.1
  219.7 2.1 convolution_convert_fusion
  221.8 2.1 convolution_convert_fusion.2
  224.0 2.1 convolution_convert_fusion.1
  226.1 116.5 %sum_all.1 = (f32[768,512]{1,0:T(8,128)}, f32[48,512]{1,0:T(8,128)}, f32[16,2048]{1,0:T(8,128)}, f32[16,2048]{1,0:T(8,128)}, f32[64,512]{1,0:T(8,128)}, /*index=5*/f32[8,512]{1,0:T(8,128)}) custom-call(bf16[4,2,768,512]{3,2,1,0:T(8,128)(2,1)} %bitcast.114, bf16[4,2,48,512]{3,2,1,0:T(8,128)(2,1)} %bitcast.123, bf16[4,4,2,16,2048]{4,3,2,1,0:T(8,128)(2,1)} %bitcast.110, ...), custom_call_target="tpu_custom_call" | custom-call | tf_op jit(solution)/shard_map/sum_all/pallas_call | solution.py:517
  344.0 2.7 copy.44
  (71 shorter events, 15.3 us)
Async XLA Ops:
  0.6 3.5 %copy-start = (f32[512,24]{0,1:T(8,128)S(1)}, f32[512,24]{0,1:T(8,128)}, u32[]{:S(2)}) copy-start(f32[512,24]{0,1:T(8,128)} %param.17) | copy-start | bytes 147460
  4.2 4.9 %copy-start.16 = (bf16[16,128]{1,0:T(8,128)(2,1)}, bf16[16,128]{1,0:T(8,128)(2,1)S(1)}, u32[]{:S(2)}) copy-start(bf16[16,128]{1,0:T(8,128)(2,1)S(1)} %scatter.9.refs_6_) | copy-start | bytes 12292
  92.1 1.2 copy-start.11
  93.3 4.8 %copy-start.1 = (bf16[1536,512]{1,0:T(8,128)(2,1)}, bf16[1536,512]{1,0:T(8,128)(2,1)S(1)}, u32[]{:S(2)}) copy-start(bf16[1536,512]{1,0:T(8,128)(2,1)S(1)} %constant_dynamic-update-slice_fusion.ar_ref) | copy-start | bytes 4718596
  98.1 36.3 %copy-start.2 = (bf16[2,1,128,512]{3,2,1,0:T(8,128)(2,1)S(1)}, bf16[2,1,128,512]{3,2,1,0:T(8,128)(2,1)}, u32[]{:S(2)}) copy-start(bf16[2,1,128,512]{3,2,1,0:T(8,128)(2,1)} %param.15) | copy-start | bytes 786436
  117.5 19.3 %copy-start.6 = (bf16[4,4,2,16,2048]{4,3,2,1,0:T(8,128)(2,1)S(1)}, bf16[4,4,2,16,2048]{4,3,2,1,0:T(8,128)(2,1)}, u32[]{:S(2)}) copy-start(bf16[4,4,2,16,2048]{4,3,2,1,0:T(8,128)(2,1)} %get-tuple-element.57) | copy-start | bytes 6291460
  136.8 1.6 copy-start.5
  136.8 2.2 copy-start.8
  139.1 2.2 copy-start.7
  141.3 2.4 copy-start.9
  141.3 1.4 copy-start.3
  142.7 1.6 copy-start.4
  219.7 2.1 copy-start.10
  342.6 4.1 %copy-start.15 = (f32[48,512]{1,0:T(8,128)S(1)}, f32[48,512]{1,0:T(8,128)}, u32[]{:S(2)}) copy-start(f32[48,512]{1,0:T(8,128)} %get-tuple-element.123) | copy-start | bytes 294916
  342.6 4.7 %copy-start.14 = (f32[16,2048]{1,0:T(8,128)S(1)}, f32[16,2048]{1,0:T(8,128)}, u32[]{:S(2)}) copy-start(f32[16,2048]{1,0:T(8,128)} %get-tuple-element.125) | copy-start | bytes 393220
  342.6 5.3 %copy-start.13 = (f32[16,2048]{1,0:T(8,128)S(1)}, f32[16,2048]{1,0:T(8,128)}, u32[]{:S(2)}) copy-start(f32[16,2048]{1,0:T(8,128)} %get-tuple-element.126) | copy-start | bytes 393220
  342.6 6.0 %copy-start.12 = (f32[64,512]{1,0:T(8,128)S(1)}, f32[64,512]{1,0:T(8,128)}, u32[]{:S(2)}) copy-start(f32[64,512]{1,0:T(8,128)} %get-tuple-element.127) | copy-start | bytes 393220

commit v2 on v1

--- a/solution.py
+++ b/solution.py
@@ -691,6 +691,422 @@
     )(dy, u, table, w, ul, ar)
 
 
+def lag_by(values, lag, span, move):
+    return jnp.where(
+        lag == 0, values, jnp.where(lag == 1, move(values, 1, span), move(values, 2, span))
+    )
+
+
+def mix_back_kernel(seq_count, line, spans, *refs):
+    (dy_ref, u_ref, row_ref, w_hbm, ul_hbm, ar_ref, x_ref, hg_ref, scale_ref) = refs[:9]
+    (z_ref, gb_ref, ub_ref, mixed_ref, cot_ref, mlp_ref) = refs[9:15]
+    (tg_ref, dw_ref, dar_ref, gg_ref, ug_ref, dg_ref, small_ref) = refs[15:22]
+    (dy, dsig, acc, conv, du_in, ul_buf, w_buf, dar) = refs[22:30]
+    (deep, deep_in, deep_run, wide, wide_in, wide_side, wide_run) = refs[30:37]
+    (g_own, g_pair, g_side, g_sum, g_line) = refs[37:42]
+    (load_sem, dys, dyr, dus, dur, ps, pr, zs, zr, wps, wpr, ws, wr, wzs, wzr, gs, gr) = refs[42:]
+    s, z, c, g = place(seq_count, line)
+    twin = {"grp": g + 1 - 2 * c}
+    rows, width = dy.shape[1], dy.shape[2]
+    block = dy_ref.shape[1]
+    count = w_hbm.shape[0]
+    per_chip = 2 * count // line
+    n = per_chip * width // CORES
+    ar_rows = ar_ref.shape[0]
+    ar_share = ar_rows // (line * CORES)
+    lanes = 128
+    ar_chunks = ar_rows // lanes
+    share = gg_ref.shape[0]
+    mine = pl.ds(pl.multiple_of(s * block, block), block)
+    low = (z < line // 2).astype(jnp.int32)
+
+    def dest(i):
+        return low * (line - 1 - 2 * i) + i
+
+    def load(i):
+        return pltpu.make_async_copy(
+            ul_hbm.at[pl.ds(dest(i) * per_chip, per_chip)], ul_buf.at[i % 2], load_sem.at[i % 2]
+        )
+
+    load_w = pltpu.make_async_copy(w_hbm, w_buf, load_sem.at[2])
+    load(0).start()
+    if line > 1:
+        load(1).start()
+    load_w.start()
+    greet(seq_count, line, s, z, c, g, twin=True, side=True, whole_line=True)
+
+    dy_copies = []
+    for i in range(1, seq_count):
+        dy_copies.append(
+            remote(
+                dy_ref,
+                dy.at[:, mine, :],
+                dys.at[i - 1],
+                dyr.at[i - 1],
+                {"seq": lax.rem(s + i, seq_count)},
+            )
+        )
+        dy_copies[-1].start()
+    dy[:, mine, :] = dy_ref[...]
+
+    span_f = gb_ref.shape[1] // seq_count
+    down_share = dg_ref.shape[0]
+    for j in range(seq_count):
+        part = slice(j * span_f, (j + 1) * span_f)
+        for which, back in ((0, gb_ref), (1, ub_ref)):
+            val = dot_tn(z_ref[...], back[:, part]).astype(BF16)
+            for k in range(seq_count):
+                for l in range(line):
+                    for cc in range(CORES):
+                        r = ((k * line + l) * CORES + cc) * share
+                        wide[cc, k, l, which * share : (which + 1) * share, part] = val[
+                            r : r + share
+                        ]
+        val = dot_tn(mixed_ref[:, part], cot_ref[...]).astype(BF16)
+        for l in range(line):
+            for cc in range(CORES):
+                r = (l * CORES + cc) * down_share
+                for q in range(down_share // share):
+                    wide[cc, j, l, 2 * share :, q * width : (q + 1) * width] = val[
+                        r + q * share : r + (q + 1) * share
+                    ]
+    wide_twin = remote(wide.at[1 - c], wide_in, wps, wpr, twin)
+    wide_twin.start()
+
+    for x in dy_copies:
+        x.wait_recv()
+
+    def ar_place(i):
+        at = s * ar_chunks + i
+        lag = lax.div(at, width // lanes)
+        col = lax.rem(at, width // lanes)
+        return lag, pl.ds(pl.multiple_of(col * lanes, lanes), lanes)
+
+    for i in range(ar_chunks):
+        lag, cols = ar_place(i)
+        total = 0.0
+        for m in range(2):
+            v = lag_by(u_ref[m, :, cols].astype(F32), lag, spans[m], lagged).astype(BF16)
+            total = total + dot_tn(v, dy[m])
+        dar[i * lanes : (i + 1) * lanes, :] = total.astype(BF16)
+    for l in range(line):
+        for cc in range(CORES):
+            r = (l * CORES + cc) * ar_share
+            deep[cc, l, n:, :] = dar[r : r + ar_share, :]
+
+    def twin_deep(i):
+        l = dest(i)
+        return remote(deep.at[1 - c, l], deep_in.at[l], ps.at[i], pr.at[i], twin)
+
+    def hop(run, own, send, recv, way, t, first):
+        target = line - 1 - t if way == 0 else t
+        src = own(target) if first else run.at[way, t]
+        to = g + CORES if way == 0 else g - CORES
+        return remote(src, run.at[way, t], send.at[way, t], recv.at[way, t], {"grp": to})
+
+    def deep_own(l):
+        return deep_in.at[l]
+
+    def wide_own(l):
+        return wide_in.at[s, l]
+
+    deep_line = (deep_run, deep_own, zs, zr)
+    wide_line = (wide_run, wide_own, wzs, wzr)
+
+    def begin(kind, t):
+        for way in (0, 1):
+
+            @pl.when(z == 0 if way == 0 else z == line - 1)
+            def _():
+                hop(*kind, way, t, True).start()
+
+    def relay(kind, phase):
+        run, own = kind[0], kind[1]
+        for way in (0, 1):
+            for t in range(phase):
+                at = phase - t if way == 0 else line - 1 - (phase - t)
+                target = line - 1 - t if way == 0 else t
+
+                @pl.when(z == at)
+                def _():
+                    hop(*kind, way, t, False).wait_recv()
+                    mixed = run[way, t].astype(F32) + own(target)[...].astype(F32)
+                    run[way, t] = mixed.astype(BF16)
+                    hop(*kind, way, t, False).start()
+
+    def compute(i):
+        l = dest(i)
+        load(i).wait()
+        for j in range(per_chip):
+            val = dot_tn(ul_buf[i % 2, j, 0], dy[0]) + dot_tn(ul_buf[i % 2, j, 1], dy[1])
+            val = val.astype(BF16)
+            for cc in range(CORES):
+                lo, hi = max(j * width, cc * n), min((j + 1) * width, (cc + 1) * n)
+                if lo < hi:
+                    deep[cc, l, lo - cc * n : hi - cc * n, :] = val[lo - j * width : hi - j * width]
+        twin_deep(i).start()
+        if i + 2 < line:
+            load(i + 2).start()
+
+    def combine(i):
+        l = dest(i)
+        twin_deep(i).wait_recv()
+        deep_in[l] = (deep[c, l].astype(F32) + deep_in[l].astype(F32)).astype(BF16)
+        if i < line - 1:
+            begin(deep_line, i)
+
+    for i in range(line):
+        compute(i)
+        if i > 0:
+            combine(i - 1)
+    combine(line - 1)
+
+    wide_twin.wait_recv()
+    for k in range(seq_count):
+
+        @pl.loop(0, line)
+        def _(l):
+            mixed = wide[c, k, l].astype(F32) + wide_in[k, l].astype(F32)
+            wide_in[k, l] = mixed.astype(BF16)
+
+    sides = []
+    for j in range(1, seq_count):
+        to = lax.rem(s + j, seq_count)
+        sides.append(
+            remote(wide_in.at[to], wide_side.at[j - 1], ws.at[j - 1], wr.at[j - 1], {"seq": to})
+        )
+        sides[-1].start()
+
+    signs = signs_of(rows)
+    for m in range(2):
+        dsig[m] = (dy[m].astype(F32) * signs).astype(BF16)
+    acc[...] = jnp.zeros_like(acc)
+    for i in range(ar_chunks):
+        lag, cols = ar_place(i)
+        for m in range(2):
+            val = dot_nt(dy[m], ar_ref[i * lanes : (i + 1) * lanes, :])
+            acc[m, :, cols] += lag_by(val, lag, spans[m], led)
+    load_w.wait()
+
+    def filter_step(k):
+        table = spread(row_ref[k], rows)
+        for m in range(2):
+            span = spans[m]
+            for j in range(rows // span):
+                part = slice(j * span, (j + 1) * span)
+                conv[0, part, :] = dot_nn(table[:span, :span], dy[m, part, :]).astype(BF16)
+                minus = dot_nn(table[:span, :span], dsig[m, part, :])
+                conv[1, part, :] = (minus * signs[part]).astype(BF16)
+            acc[m] += dot_nt(conv[0], w_buf[k, 0]) + dot_nt(conv[1], w_buf[k, 1])
+
+    half = count // 2
+    pl.loop(0, half)(filter_step)
+    for phase in range(1, line - 2):
+        relay(deep_line, phase)
+    pl.loop(half, count)(filter_step)
+    conv[...] = acc[...].astype(BF16)
+    du_copies = []
+    for i in range(1, seq_count):
+        to = lax.rem(s + i, seq_count)
+        du_copies.append(
+            remote(
+                conv.at[:, pl.ds(pl.multiple_of(to * block, block), block), :],
+                du_in.at[i - 1],
+                dus.at[i - 1],
+                dur.at[i - 1],
+                {"seq": to},
+            )
+        )
+        du_copies[-1].start()
+    if line > 2:
+        relay(deep_line, line - 2)
+
+    for x in du_copies:
+        x.wait_recv()
+    gain = jnp.zeros((1, width), F32)
+    for m in range(2):
+        grad = conv[m, mine, :].astype(F32)
+        for i in range(seq_count - 1):
+            grad = grad + du_in[i, m].astype(F32)
+        x = x_ref[m].astype(F32)
+        inv = lax.rsqrt(jnp.mean(x * x, axis=-1, keepdims=True) + EPSILON)
+        scaled = grad * scale_ref[...]
+        gain = gain + jnp.sum(grad * x * inv, axis=0, keepdims=True)
+        centre = jnp.mean(scaled * x, axis=-1, keepdims=True)
+        tg_ref[m] = hg_ref[m] + inv * scaled - x * (inv * inv * inv) * centre
+    g_own[...] = jnp.zeros_like(g_own)
+    g_own[0:1, :] = gain
+    g_own[1:2, :] = mlp_ref[...]
+    small_pair = remote(g_own, g_pair, gs.at[0], gr.at[0], twin)
+    small_pair.start()
+
+    for x in sides:
+        x.wait_recv()
+
+    @pl.loop(0, line)
+    def _(l):
+        mixed = wide_in[s, l].astype(F32)
+        for j in range(seq_count - 1):
+            mixed = mixed + wide_side[j, l].astype(F32)
+        wide_in[s, l] = mixed.astype(BF16)
+
+    for t in range(line - 1):
+        begin(wide_line, t)
+
+    small_pair.wait()
+    g_own[...] = g_own[...] + g_pair[...]
+    small_sides = []
+    for j in range(1, seq_count):
+        small_sides.append(
+            remote(
+                g_own, g_side.at[j - 1], gs.at[j], gr.at[j], {"seq": lax.rem(s + j, seq_count)}
+            )
+        )
+        small_sides[-1].start()
+
+    dw_ref[...] = deep_in[z, :n, :].astype(F32)
+    dar_ref[...] = deep_in[z, n:, :].astype(F32)
+    for x in small_sides:
+        x.wait()
+    total = g_own[...]
+    for j in range(seq_count - 1):
+        total = total + g_side[j]
+    g_sum[...] = total
+    small_lines = []
+    for j in range(1, line):
+        small_lines.append(
+            remote(
+                g_sum,
+                g_line.at[j - 1],
+                gs.at[seq_count - 1 + j],
+                gr.at[seq_count - 1 + j],
+                {"grp": lax.rem(g + CORES * j, CORES * line)},
+            )
+        )
+        small_lines[-1].start()
+
+    def last(kind, add):
+        for t in range(line - 1):
+            for way in (0, 1):
+                target = line - 1 - t if way == 0 else t
+
+                @pl.when(z == target)
+                def _():
+                    hop(*kind, way, t, False).wait_recv()
+                    add(kind[0][way, t].astype(F32))
+
+    def add_deep(val):
+        dw_ref[...] += val[:n]
+        dar_ref[...] += val[n:]
+
+    def add_wide(val):
+        gg_ref[...] += val[:share]
+        ug_ref[...] += val[share : 2 * share]
+        for q in range(down_share // share):
+            dg_ref[q * share : (q + 1) * share, :] += val[2 * share :, q * width : (q + 1) * width]
+
+    last(deep_line, add_deep)
+    for phase in range(1, line - 1):
+        relay(wide_line, phase)
+    own = wide_in[s, z].astype(F32)
+    gg_ref[...] = own[:share]
+    ug_ref[...] = own[share : 2 * share]
+    for q in range(down_share // share):
+        dg_ref[q * share : (q + 1) * share, :] = own[2 * share :, q * width : (q + 1) * width]
+    last(wide_line, add_wide)
+
+    for x in small_lines:
+        x.wait()
+    total = g_sum[...]
+    for j in range(line - 1):
+        total = total + g_line[j]
+    small_ref[...] = total
+
+    for x in dy_copies + sides + du_copies:
+        x.wait_send()
+    wide_twin.wait_send()
+    for i in range(line):
+        twin_deep(i).wait_send()
+    for kind in (deep_line, wide_line):
+        for t in range(line - 1):
+            for way in (0, 1):
+                target = line - 1 - t if way == 0 else t
+
+                @pl.when(z < target if way == 0 else z > target)
+                def _():
+                    hop(*kind, way, t, False).wait_send()
+
+
+def mix_back(seq_count, line, spans, dy, u, table, w, ul, ar, x, hg, scale, mlp, mlp_grad, shares):
+    z, gate_back, up_back, mixed, cot = mlp
+    share, down_share, deep_share, ar_share = shares
+    _, block, width = dy.shape
+    rows = block * seq_count
+    count = w.shape[0]
+    per_chip = 2 * count // line
+    small = (8, width)
+    hidden_units = gate_back.shape[1]
+    part = (2 * share + down_share * width // hidden_units, hidden_units)
+    out_shape = [
+        jax.ShapeDtypeStruct((2, block, width), F32),
+        jax.ShapeDtypeStruct((deep_share, width), F32),
+        jax.ShapeDtypeStruct((ar_share, width), F32),
+        jax.ShapeDtypeStruct((share, hidden_units), F32),
+        jax.ShapeDtypeStruct((share, hidden_units), F32),
+        jax.ShapeDtypeStruct((down_share, width), F32),
+        jax.ShapeDtypeStruct(small, F32),
+    ]
+    deep = (deep_share + ar_share, width)
+    scratch = [
+        pltpu.VMEM((2, rows, width), BF16),
+        pltpu.VMEM((2, rows, width), BF16),
+        pltpu.VMEM((2, rows, width), F32),
+        pltpu.VMEM((2, rows, width), BF16),
+        pltpu.VMEM((seq_count - 1, 2, block, width), BF16),
+        pltpu.VMEM((2, per_chip, 2, rows, width), BF16),
+        pltpu.VMEM(w.shape, BF16),
+        pltpu.VMEM(ar.shape, BF16),
+        pltpu.VMEM((CORES, line) + deep, BF16),
+        pltpu.VMEM((line,) + deep, BF16),
+        pltpu.VMEM((2, line - 1) + deep, BF16),
+        pltpu.VMEM((CORES, seq_count, line) + part, BF16),
+        pltpu.VMEM((seq_count, line) + part, BF16),
+        pltpu.VMEM((seq_count - 1, line) + part, BF16),
+        pltpu.VMEM((2, line - 1) + part, BF16),
+        pltpu.VMEM(small, F32),
+        pltpu.VMEM(small, F32),
+        pltpu.VMEM((seq_count - 1,) + small, F32),
+        pltpu.VMEM(small, F32),
+        pltpu.VMEM((line - 1,) + small, F32),
+        DMA((3,)),
+        DMA((seq_count - 1,)),
+        DMA((seq_count - 1,)),
+        DMA((seq_count - 1,)),
+        DMA((seq_count - 1,)),
+        DMA((line,)),
+        DMA((line,)),
+        DMA((2, line - 1)),
+        DMA((2, line - 1)),
+        DMA,
+        DMA,
+        DMA((seq_count - 1,)),
+        DMA((seq_count - 1,)),
+        DMA((2, line - 1)),
+        DMA((2, line - 1)),
+        DMA((seq_count + line,)),
+        DMA((seq_count + line,)),
+    ]
+    return pl.pallas_call(
+        functools.partial(mix_back_kernel, seq_count, line, spans),
+        out_shape=out_shape,
+        in_specs=[WHOLE] * 3 + [ANY] * 2 + [WHOLE] * 10,
+        out_specs=[WHOLE] * 7,
+        scratch_shapes=scratch,
+        compiler_params=params(6),
+        name="mix_back",
+    )(dy, u, table, w, ul.reshape(2 * count, 2, rows, width), ar, x, hg, scale, z, gate_back, up_back, mixed, cot, mlp_grad)
+
+
 def body(
     tokens,
     layout,
@@ -754,13 +1170,10 @@
     product_val, gelu_pull = jax.vjp(lambda a, b: jax.nn.gelu(a) * b, gate, upval)
     mixed = product_val.astype(BF16)
     out = hidden + dot_nn(mixed, down_w)
-    down_grad = dot_tn(mixed, cot)
     mixed_grad = dot_nt(cot, down_w)
     gate_back, up_back = gelu_pull(mixed_grad)
     gate_back = gate_back.astype(BF16)
     up_back = up_back.astype(BF16)
-    gate_grad = dot_tn(mlp_in, gate_back)
-    up_grad = dot_tn(mlp_in, up_back)
     mlp_in_grad = dot_nt(gate_back, gate_w) + dot_nt(up_back, up_w)
     scaled_two = mlp_in_grad * mlp_scale
     mlp_grad = jnp.sum(mlp_in_grad * hidden * inv_two, axis=0, keepdims=True)
@@ -771,27 +1184,50 @@
     )
     mixer_grad = hidden_grad.astype(BF16)
 
-    dy = side_gather(seq_count, line, mixer_grad.reshape(2, block, width))
-    dw, dar, du = backward_mix(spans, dy, u, back_table, spec, ul, ar_full)
-    normed_grad = side_sum(seq_count, line, du, 4).reshape(2 * block, width)
-
-    inv_one = lax.rsqrt(jnp.mean(inputs * inputs, axis=-1, keepdims=True) + EPSILON)
-    scaled_one = normed_grad * mix_scale
-    mix_grad = jnp.sum(normed_grad * inputs * inv_one, axis=0, keepdims=True)
-    input_grad = (
-        hidden_grad
-        + inv_one * scaled_one
-        - inputs * inv_one**3 * jnp.mean(scaled_one * inputs, axis=-1, keepdims=True)
-    )
-
-    dar = lax.dynamic_slice(dar, (s * ar_rows, 0), (ar_rows, width))
-    deep = (dw.reshape(line, CORES, -1, width), dar.reshape(line, CORES, -1, width))
-    wide = tuple(
-        x.astype(BF16).reshape(seq_count, line, CORES, -1, x.shape[1])
-        for x in (gate_grad, up_grad, down_grad)
-    )
-    small = jnp.concatenate([mix_grad, mlp_grad, jnp.zeros((6, width), F32)], axis=0)
-    dw, dar, gate_grad, up_grad, down_grad, small = sum_all(seq_count, line, deep, wide, small)
+    ar_share = ar_rows // (line * CORES)
+    if w_gate.shape[0] % 16 == 0 and ar_share % 16 == 0 and 2 * count % line == 0:
+        input_grad, dw, dar, gate_grad, up_grad, down_grad, small = mix_back(
+            seq_count,
+            line,
+            spans,
+            mixer_grad.reshape(2, block, width),
+            u,
+            back_table,
+            spec,
+            ul,
+            ar.reshape(ar_rows, width),
+            own,
+            hidden_grad.reshape(2, block, width),
+            mix_scale,
+            (mlp_in, gate_back, up_back, mixed, cot),
+            mlp_grad,
+            (w_gate.shape[0], w_down.shape[0], spectral_proj.shape[0], ar_share),
+        )
+    else:
+        down_grad = dot_tn(mixed, cot)
+        gate_grad = dot_tn(mlp_in, gate_back)
+        up_grad = dot_tn(mlp_in, up_back)
+        dy = side_gather(seq_count, line, mixer_grad.reshape(2, block, width))
+        dw, dar, du = backward_mix(spans, dy, u, back_table, spec, ul, ar_full)
+        normed_grad = side_sum(seq_count, line, du, 4).reshape(2 * block, width)
+
+        inv_one = lax.rsqrt(jnp.mean(inputs * inputs, axis=-1, keepdims=True) + EPSILON)
+        scaled_one = normed_grad * mix_scale
+        mix_grad = jnp.sum(normed_grad * inputs * inv_one, axis=0, keepdims=True)
+        input_grad = (
+            hidden_grad
+            + inv_one * scaled_one
+            - inputs * inv_one**3 * jnp.mean(scaled_one * inputs, axis=-1, keepdims=True)
+        )
+
+        dar = lax.dynamic_slice(dar, (s * ar_rows, 0), (ar_rows, width))
+        deep = (dw.reshape(line, CORES, -1, width), dar.reshape(line, CORES, -1, width))
+        wide = tuple(
+            x.astype(BF16).reshape(seq_count, line, CORES, -1, x.shape[1])
+            for x in (gate_grad, up_grad, down_grad)
+        )
+        small = jnp.concatenate([mix_grad, mlp_grad, jnp.zeros((6, width), F32)], axis=0)
+        dw, dar, gate_grad, up_grad, down_grad, small = sum_all(seq_count, line, deep, wide, small)
     small = lax.dynamic_slice(small, (0, (s * CORES * line + g) * share), (2, share))
 
     def settle(x):

time: 350 us -> 252 us (0.72)
  Pallas kernels: 303 us -> 217 us
  matrix products: 15.4 us -> 8.96 us
    pallas_call x3 -> x1, Pallas kernels: 168 us -> 97.6 us  [mix_back(): pl.pallas_call(functools.partial(mix_back_kernel, seq_count, line, spans)...]
    pallas_call x2 -> x1, Pallas kernels: 32.5 us -> 16.9 us  [side_sum(): pl.pallas_call(functools.partial(side_sum_kernel, seq_count, line), out_s...]
    dot_general x3 -> x0, matrix products: 6.37 us -> none  [dot_tn(): lax.dot_general(a, b, (((0,), (0,)), ((), ())), preferred_element_type=F32)]
    unnamed x41 -> x43, local copies, waits for them, and re-layouts: 8.62 us -> 8.32 us
where the time goes in v2:
time: 252 us; the launch traced here: 251 us
  Pallas kernels  217 us (86%)
  local copies, waits for them, and re-layouts  13.9 us (6%)
  other arithmetic  10 us (4%)
  matrix products  8.96 us (4%)
    pallas_call x1, Pallas kernels, mix_back(): pl.pallas_call(functools.partial(mix_back_kernel, seq_count, line, spans)...  97.6 us
    pallas_call x1, Pallas kernels, gather_all(): pl.pallas_call(functools.partial(gather_kernel, seq_count, line, n_deep,...  83 us
    pallas_call x1, Pallas kernels, forward_mix(): pl.pallas_call(functools.partial(forward_kernel, spans), grid=(count,), o...  19.4 us
    pallas_call x1, Pallas kernels, side_sum(): pl.pallas_call(functools.partial(side_sum_kernel, seq_count, line), out_s...  16.9 us
    unnamed x43, local copies, waits for them, and re-layouts  8.32 us
    dot_general x3, matrix products, dot_nt(): lax.dot_general(a, b, (((1,), (1,)), ((), ())), preferred_element_type=F32)  5.13 us

profile of v2, /device:TPU:0, one launch (start us, length us, event | category | flops | bytes accessed | tf_op | source)
XLA Modules:
  0.0 251.3 jit_solution(12151119436879135029)
XLA Ops:
  0.7 0.8 copy-done
  3.5 2.0 reverse_select_fusion.2
  6.2 0.8 scatter.9.refs_6_
  7.6 83.0 %gather_all.1 = (bf16[2,512,512]{2,1,0:T(8,128)(2,1)}, bf16[4,2,768,512]{3,2,1,0:T(8,128)(2,1)}, bf16[4,2,48,512]{3,2,1,0:T(8,128)(2,1)}, bf16[4,4,2,16,2048]{4,...) custom-call(bf16[2,128,512]{2,1,0:T(8,128)(2,1)} %bitcast.72, ...), custom_call_target="tpu_custom_call" | custom-call | tf_op jit(solution)/shard_map/gather_all/pallas_call | solution.py:249
  90.7 1.0 constant_dynamic-update-slice_fusion.ar_ref
  91.8 0.8 reshape_squeeze.4.gain_ref.refs_8_
  92.9 19.4 %forward_mix.1 = (bf16[6,2,2,512,512]{4,3,2,1,0:T(8,128)(2,1)}, bf16[2,512,512]{2,1,0:T(8,128)(2,1)}, bf16[2,512,512]{2,1,0:T(8,128)(2,1)}) custom-call(bf16[2,512,512]{2,1,0:T(8,128)(2,1)} %get-tuple-element.50.x_ref, f32[1,512]{1,0:T(1,128)} %reshape_squeeze.4.gain_ref.refs_8_, f32[6,1,1024]{2,1,0:T(1,128)} %pad_maximum_fusion.row_ref, ...), custom_call_target="tpu_custom_call" | custom-call | tf_op jit(solution)/shard_map/forward_mix/pallas_call | solution.py:592
  112.3 16.9 %side_sum_3.1 = f32[2,128,512]{2,1,0:T(8,128)} custom-call(bf16[2,512,512]{2,1,0:T(8,128)(2,1)} %get-tuple-element.54.x_ref), custom_call_target="tpu_custom_call" | custom-call | tf_op jit(solution)/shard_map/side_sum_3/pallas_call | solution.py:320
  129.2 1.2 multiply_reduce_fusion.2
  130.5 1.2 multiply_convert_fusion.3
  131.7 0.7 fusion.13
  132.4 0.9 copy-done.9
  134.0 0.9 copy-done.8
  134.8 3.0 %multiply_convert_fusion = (bf16[256,2048]{1,0:T(8,128)(2,1)S(1)}, bf16[256,2048]{1,0:T(8,128)(2,1)S(1)}, bf16[256,2048]{1,0:T(8,128)(2,1)}) fusion(f32[256,2048]{1,0:T(8,128)S(1)} %fusion.12, f32[256,2048]{1,0:T(8,128)S(1)} %fusion.13, bf16[256,512]{1,0:T(8,128)(2,1)S(1)} %bitcast.76, bf16[2048,512]{1,0:T(8,128)(2,1)S(1)} %bitcast.81), kind=kOutput, calls=%fused_computation.9 | convolution fusion | flops 550502400 | bytes 9699328 | tf_op jit(solution)/shard_map/dot_general | solution.py:30
  137.8 0.7 fusion.14
  139.2 0.8 multiply_convert_fusion.2
  140.1 1.4 multiply_reduce_fusion
  141.5 1.1 fusion.10
  143.2 97.6 %mix_back.1 = (f32[2,128,512]{2,1,0:T(8,128)}, f32[768,512]{1,0:T(8,128)}, f32[48,512]{1,0:T(8,128)}, f32[16,2048]{1,0:T(8,128)}, f32[16,2048]{1,0:T(8,128)}, /*index=5*/f32[64,512]{1,0:T(8,128)}, f32[8,512]{1,0:T(8,128)}) custom-call(bf16[2,128,512]{2,1,0:T(8,128)(2,1)} %bitcast.88, bf16[2,512,512]{2,1,0:T(8,128)(2,1)} %get-tuple-element.58.refs_1_, ...), custom_call_target="tpu_custom_call" | custom-call | tf_op jit(solution)/shard_map/mix_back/pallas_call | solution.py:1099
  240.8 2.1 fusion.8
  243.0 0.7 constant_dynamic-slice_fusion
  244.2 2.4 convolution_add_fusion.1
  246.7 0.8 fusion.7
  247.5 1.1 copy.44
  (57 shorter events, 8.3 us)
Async XLA Ops:
  0.6 0.8 copy-start
  5.5 136.0 %copy-start.7 = (bf16[2,1,128,512]{3,2,0,1:T(8,128)(2,1)}, bf16[2,1,128,512]{3,2,0,1:T(8,128)(2,1)S(1)}, u32[]{:S(2)}) copy-start(bf16[2,1,128,512]{3,2,0,1:T(8,128)(2,1)S(1)} %get-tuple-element.101) | copy-start | bytes 786436
  7.0 0.6 copy-start.17
  90.6 1.2 copy-start.12
  91.7 1.1 copy-start.4
  92.9 36.3 %copy-start.1 = (bf16[2,1,128,512]{3,2,0,1:T(8,128)(2,1)S(1)}, bf16[2,1,128,512]{3,2,0,1:T(8,128)(2,1)}, u32[]{:S(2)}) copy-start(bf16[2,1,128,512]{3,2,0,1:T(8,128)(2,1)} %get-tuple-element.102) | copy-start | bytes 786436
  112.3 19.3 %copy-start.3 = (bf16[4,4,2,16,2048]{4,3,2,1,0:T(8,128)(2,1)S(1)}, bf16[4,4,2,16,2048]{4,3,2,1,0:T(8,128)(2,1)}, u32[]{:S(2)}) copy-start(bf16[4,4,2,16,2048]{4,3,2,1,0:T(8,128)(2,1)} %get-tuple-element.56) | copy-start | bytes 6291460
  131.7 1.6 copy-start.9
  133.2 1.6 copy-start.8
  137.8 2.2 copy-start.11
  137.8 2.2 copy-start.5
  137.8 1.4 copy-start.2
  143.2 101.0 %copy-start.6 = (bf16[256,2048]{1,0:T(8,128)(2,1)S(1)}, bf16[256,2048]{1,0:T(8,128)(2,1)}, u32[]{:S(2)}) copy-start(bf16[256,2048]{1,0:T(8,128)(2,1)} %get-tuple-element.93.refs_12_) | copy-start | bytes 3145732
  244.2 3.3 %copy-start.10 = (f32[768,512]{1,0:T(8,128)S(1)}, f32[768,512]{1,0:T(8,128)}, u32[]{:S(2)}) copy-start(f32[768,512]{1,0:T(8,128)} %get-tuple-element.115) | copy-start | bytes 4718596
  246.7 2.0 copy-start.16
  246.7 2.7 %copy-start.15 = (f32[16,2048]{1,0:T(8,128)S(1)}, f32[16,2048]{1,0:T(8,128)}, u32[]{:S(2)}) copy-start(f32[16,2048]{1,0:T(8,128)} %get-tuple-element.118) | copy-start | bytes 393220
  246.7 3.3 %copy-start.14 = (f32[16,2048]{1,0:T(8,128)S(1)}, f32[16,2048]{1,0:T(8,128)}, u32[]{:S(2)}) copy-start(f32[16,2048]{1,0:T(8,128)} %get-tuple-element.119) | copy-start | bytes 393220
  247.5 3.1 %copy-start.13 = (f32[64,512]{1,0:T(8,128)S(1)}, f32[64,512]{1,0:T(8,128)}, u32[]{:S(2)}) copy-start(f32[64,512]{1,0:T(8,128)} %get-tuple-element.120) | copy-start | bytes 393220

commit v3 on v2

--- a/solution.py
+++ b/solution.py
@@ -1107,6 +1107,348 @@
     )(dy, u, table, w, ul.reshape(2 * count, 2, rows, width), ar, x, hg, scale, z, gate_back, up_back, mixed, cot, mlp_grad)
 
 
+def mix_front_kernel(seq_count, line, spans, *refs):
+    (tok_ref, row_ref, gain_ref, spec_hbm, ar_hbm) = refs[:5]
+    wide_in = refs[5:8]
+    (w_hbm, ul_hbm, u_ref, y_ref, ar_ref, gain_out) = refs[8:14]
+    wide_out = refs[14:17]
+    (x_all, both, acc, y_bf, y_in, w_buf, ul_buf) = refs[17:24]
+    stage = refs[24:27]
+    (g_own, g_side, g_sum, g_line, g_all, g_twin) = refs[27:33]
+    (load_sem, store_sem, ul_sem, w_sem, ts, tr, ys, yr, zs, zr, hs, hr) = refs[33:45]
+    (ps, pr, ws, wr, wps, wpr, gs, gr) = refs[45:]
+    s, z, c, g = place(seq_count, line)
+    twin = {"grp": g + 1 - 2 * c}
+    rows, width = x_all.shape[1], x_all.shape[2]
+    block = tok_ref.shape[1]
+    n = spec_hbm.shape[0]
+    blocks = ul_buf.shape[0]
+    count = blocks // 2
+    per_chip = blocks // line
+    lanes = 128
+    wide = range(3)
+    mine = pl.ds(pl.multiple_of(s * block, block), block)
+
+    def piece(l):
+        return w_buf.at[l, pl.ds(pl.multiple_of(c * n, n), n), :]
+
+    load_w = pltpu.make_async_copy(spec_hbm, piece(z), load_sem.at[0])
+    load_ar = pltpu.make_async_copy(ar_hbm, ar_ref.at[z, c], load_sem.at[1])
+    loads = [pltpu.make_async_copy(wide_in[i], stage[i], load_sem.at[2 + i]) for i in wide]
+    for x in loads + [load_ar, load_w]:
+        x.start()
+    at = (s * (CORES * line) + g) * (width // (seq_count * CORES * line))
+    g_own[...] = pltpu.roll(gain_ref[...], at, 1).astype(BF16)
+    greet(seq_count, line, s, z, c, g, twin=True, side=True, whole_line=True)
+
+    gain_sides = []
+    toks = []
+    for i in range(1, seq_count):
+        to = {"seq": lax.rem(s + i, seq_count)}
+        gain_sides.append(remote(g_own, g_side.at[i - 1], gs.at[i - 1], gr.at[i - 1], to))
+        gain_sides[-1].start()
+    for i in range(1, seq_count):
+        to = {"seq": lax.rem(s + i, seq_count)}
+        toks.append(remote(tok_ref, x_all.at[:, mine, :], ts.at[i - 1], tr.at[i - 1], to))
+        toks[-1].start()
+
+    def early_own(i, l):
+        return ar_ref.at[l, c] if i == 3 else wide_out[i].at[s, l, c]
+
+    def early_hop(i, way, t, origin):
+        if t > 0:
+            src = early_own(i, origin)
+        else:
+            src = ar_hbm if i == 3 else wide_in[i]
+        to = g + CORES if way == 0 else g - CORES
+        return remote(src, early_own(i, origin), hs.at[i, way, t], hr.at[i, way, t], {"grp": to})
+
+    def deep_hop(way, t, origin):
+        to = g + CORES if way == 0 else g - CORES
+        return remote(
+            piece(origin), piece(origin), zs.at[way, t], zr.at[way, t], {"grp": to}
+        )
+
+    def each_hop(way, t, which, origin, act):
+        if which == "early":
+            for i in range(4):
+                act(early_hop(i, way, t, origin))
+        else:
+            act(deep_hop(way, t, origin))
+
+    def first(which):
+        for way in (0, 1):
+            sends, _, origin, _ = line_conditions(line, z, way, 0)
+
+            @pl.when(sends)
+            def _():
+                each_hop(way, 0, which, origin, lambda x: x.start())
+
+    def arrive(which, t, after=None):
+        for way in (0, 1):
+            _, receives, _, origin = line_conditions(line, z, way, t)
+
+            @pl.when(receives)
+            def _():
+                each_hop(way, t, which, origin, lambda x: x.wait_recv())
+                if t + 1 < line - 1:
+                    sends = line_conditions(line, z, way, t + 1)[0]
+
+                    @pl.when(sends)
+                    def _():
+                        each_hop(way, t + 1, which, origin, lambda x: x.start())
+
+                if after is not None:
+                    after(origin)
+
+    def sent(which):
+        for t in range(line - 1):
+            for way in (0, 1):
+                sends, _, origin, _ = line_conditions(line, z, way, t)
+
+                @pl.when(sends)
+                def _():
+                    each_hop(way, t, which, origin, lambda x: x.wait_send())
+
+    first("early")
+    x_all[:, mine, :] = tok_ref[...]
+    stores = []
+    for i in wide:
+        loads[i].wait()
+        stores.append(pltpu.make_async_copy(stage[i], wide_out[i].at[s, z, c], store_sem.at[i]))
+        stores[-1].start()
+    load_ar.wait()
+    load_w.wait()
+
+    def twin_deep(l):
+        return remote(piece(l), piece(l), ps.at[l], pr.at[l], twin)
+
+    twin_deep(z).start()
+
+    total = g_own[...]
+    for i, x in enumerate(gain_sides):
+        x.wait_recv()
+        total = total + g_side[i]
+    g_sum[...] = total
+    gain_lines = []
+    for j in range(1, line):
+        k = seq_count - 2 + j
+        to = {"grp": lax.rem(g + CORES * j, CORES * line)}
+        gain_lines.append(remote(g_sum, g_line.at[j - 1], gs.at[k], gr.at[k], to))
+        gain_lines[-1].start()
+    arrive("early", 0)
+    first("deep")
+    total = g_sum[...]
+    for j, x in enumerate(gain_lines):
+        x.wait_recv()
+        total = total + g_line[j]
+    g_all[...] = total
+    k = seq_count + line - 2
+    gain_twin = remote(g_all, g_twin, gs.at[k], gr.at[k], twin)
+    gain_twin.start()
+    for x in toks:
+        x.wait_recv()
+    gain_twin.wait_recv()
+    gain = g_all[...].astype(F32) + g_twin[...].astype(F32)
+    gain_out[...] = gain[:8]
+
+    signs = signs_of(rows)
+    for m in range(2):
+        x = x_all[m].astype(F32)
+        inv = lax.rsqrt(jnp.mean(x * x, axis=-1, keepdims=True) + EPSILON)
+        u = (x * inv * gain[0:1, :]).astype(BF16)
+        u_ref[m] = u
+        both[m, :, :width] = u
+        both[m, :, width:] = (u.astype(F32) * signs).astype(BF16)
+
+    def ul_store(k):
+        part = pl.ds(2 * k, 2)
+        return pltpu.make_async_copy(ul_buf.at[part], ul_hbm.at[part], ul_sem.at[k])
+
+    def filter_step(k):
+        table = spread(row_ref[k], rows)
+        for m in range(2):
+            span = spans[m]
+            for j in range(rows // span):
+                part = slice(j * span, (j + 1) * span)
+                val = dot_tn(table[:span, :span], both[m, part, :])
+                ul_buf[2 * k, m, part, :] = val[:, :width].astype(BF16)
+                ul_buf[2 * k + 1, m, part, :] = (val[:, width:] * signs[part]).astype(BF16)
+        ul_store(k).start()
+
+    half = count // 2
+    pl.loop(0, half)(filter_step)
+    if line > 2:
+        arrive("early", 1)
+    pl.loop(half, count)(filter_step)
+    for x in stores:
+        x.wait()
+
+    acc[...] = jnp.zeros_like(acc)
+
+    def add_chip(l):
+        for m in range(2):
+            total = 0.0
+            for j in range(per_chip):
+                total = total + dot_nn(
+                    ul_buf[l * per_chip + j, m], w_buf[l, j * width : (j + 1) * width, :]
+                )
+            acc[m] += total
+
+    def w_store(l):
+        return pltpu.make_async_copy(w_buf.at[l], w_hbm.at[l], w_sem.at[l])
+
+    twin_deep(z).wait_recv()
+    w_store(z).start()
+    add_chip(z)
+    for t in range(2, line - 1):
+        arrive("early", t)
+
+    ar_twin = remote(ar_ref.at[:, c], ar_ref.at[:, c], wps.at[3, 0], wpr.at[3, 0], twin)
+    ar_twin.start()
+    sides = []
+    for i in wide:
+        for j in range(1, seq_count):
+            part = wide_out[i].at[s, :, c]
+            to = {"seq": lax.rem(s + j, seq_count)}
+            sides.append(remote(part, part, ws.at[i, j - 1], wr.at[i, j - 1], to))
+            sides[-1].start()
+
+    def twin_wide(i, k):
+        part = wide_out[i].at[k, :, c]
+        return remote(part, part, wps.at[i, k], wpr.at[i, k], twin)
+
+    for i in wide:
+        twin_wide(i, s).start()
+
+    ar_twin.wait_recv()
+    ar_rows = ar_ref.shape[0] * ar_ref.shape[1] * ar_ref.shape[2]
+    ar_all = ar_ref[...].reshape(ar_rows, width)
+    chunks = ar_rows // lanes
+    for i in range(chunks):
+        place_at = s * chunks + i
+        lag = lax.div(place_at, width // lanes)
+        col = lax.rem(place_at, width // lanes)
+        cols = pl.ds(pl.multiple_of(col * lanes, lanes), lanes)
+        for m in range(2):
+            v = lag_by(u_ref[m, :, cols].astype(F32), lag, spans[m], lagged).astype(BF16)
+            acc[m] += dot_nn(v, ar_all[i * lanes : (i + 1) * lanes])
+
+    for t in range(line - 1):
+        if t == line - 2:
+            for x in sides:
+                x.wait_recv()
+            for i in wide:
+                for j in range(1, seq_count):
+                    twin_wide(i, lax.rem(s + seq_count - j, seq_count)).start()
+        arrive("deep", t, lambda origin: twin_deep(origin).start())
+        for way in (0, 1):
+            _, receives, _, origin = line_conditions(line, z, way, t)
+
+            @pl.when(receives)
+            def _():
+                twin_deep(origin).wait_recv()
+                w_store(origin).start()
+                add_chip(origin)
+
+    y_bf[...] = acc[...].astype(BF16)
+    y_copies = []
+    for i in range(1, seq_count):
+        to = lax.rem(s + i, seq_count)
+        y_copies.append(
+            remote(
+                y_bf.at[:, pl.ds(pl.multiple_of(to * block, block), block), :],
+                y_in.at[i - 1],
+                ys.at[i - 1],
+                yr.at[i - 1],
+                {"seq": to},
+            )
+        )
+        y_copies[-1].start()
+
+    sent("early")
+    sent("deep")
+    for l in range(line):
+        twin_deep(l).wait_send()
+        w_store(l).wait()
+    for i in wide:
+        for k in range(seq_count):
+            twin_wide(i, k).wait()
+    for x in toks + sides + gain_sides + gain_lines + [ar_twin, gain_twin]:
+        x.wait_send()
+    for k in range(count):
+        ul_store(k).wait()
+    for m in range(2):
+        y_ref[m] = acc[m, mine, :]
+    for i, x in enumerate(y_copies):
+        x.wait_recv()
+        y_ref[...] += y_in[i].astype(F32)
+    for x in y_copies:
+        x.wait_send()
+
+
+def mix_front(seq_count, line, spans, tok, table, gain, spec, ar, wide):
+    _, block, width = tok.shape
+    rows = block * seq_count
+    count = table.shape[0]
+    small = (16, width)
+    out_shape = [
+        jax.ShapeDtypeStruct((line, CORES * spec.shape[0], width), BF16),
+        jax.ShapeDtypeStruct((2 * count, 2, rows, width), BF16),
+        jax.ShapeDtypeStruct((2, rows, width), BF16),
+        jax.ShapeDtypeStruct((2, block, width), F32),
+        jax.ShapeDtypeStruct((line, CORES) + ar.shape, BF16),
+        jax.ShapeDtypeStruct((8, width), F32),
+    ] + [jax.ShapeDtypeStruct((seq_count, line, CORES) + x.shape, BF16) for x in wide]
+    scratch = [
+        pltpu.VMEM((2, rows, width), BF16),
+        pltpu.VMEM((2, rows, 2 * width), BF16),
+        pltpu.VMEM((2, rows, width), F32),
+        pltpu.VMEM((2, rows, width), BF16),
+        pltpu.VMEM((seq_count - 1, 2, block, width), BF16),
+        pltpu.VMEM((line, CORES * spec.shape[0], width), BF16),
+        pltpu.VMEM((2 * count, 2, rows, width), BF16),
+    ]
+    scratch += [pltpu.VMEM(x.shape, BF16) for x in wide]
+    scratch += [
+        pltpu.VMEM(small, BF16),
+        pltpu.VMEM((seq_count - 1,) + small, BF16),
+        pltpu.VMEM(small, BF16),
+        pltpu.VMEM((line - 1,) + small, BF16),
+        pltpu.VMEM(small, BF16),
+        pltpu.VMEM(small, BF16),
+        DMA((5,)),
+        DMA((3,)),
+        DMA((count,)),
+        DMA((line,)),
+        DMA((seq_count - 1,)),
+        DMA((seq_count - 1,)),
+        DMA((seq_count - 1,)),
+        DMA((seq_count - 1,)),
+        DMA((2, line - 1)),
+        DMA((2, line - 1)),
+        DMA((4, 2, line - 1)),
+        DMA((4, 2, line - 1)),
+        DMA((line,)),
+        DMA((line,)),
+        DMA((3, seq_count - 1)),
+        DMA((3, seq_count - 1)),
+        DMA((4, seq_count)),
+        DMA((4, seq_count)),
+        DMA((seq_count + line,)),
+        DMA((seq_count + line,)),
+    ]
+    return pl.pallas_call(
+        functools.partial(mix_front_kernel, seq_count, line, spans),
+        out_shape=out_shape,
+        in_specs=[WHOLE] * 3 + [ANY] * 5,
+        out_specs=[ANY] * 2 + [WHOLE] * 4 + [ANY] * 3,
+        scratch_shapes=scratch,
+        compiler_params=params(7),
+        name="mix_front",
+    )(tok, table, gain, spec, ar, *wide)
+
+
 def body(
     tokens,
     layout,
@@ -1134,31 +1476,48 @@
     own = jnp.where(swap, tokens[::-1, 0], tokens[:, 0])
     cotangent = jnp.where(swap, out_grad[::-1, 0], out_grad[:, 0])
     share = gain_mix.shape[0]
-    gains = jnp.zeros((16, 128), BF16)
-    gains = gains.at[0, :share].set(gain_mix).at[1, :share].set(gain_mlp)
-
-    x_all, spec, ar, gate_w, up_w, down_w, gains = gather_all(
-        seq_count, line, own, (spectral_proj, ar_proj), (w_gate, w_up, w_down, gains)
-    )
+    ar_rows = ar_proj.shape[0] * CORES * line
+    mine = lax.dynamic_slice(filters.T, (s * count, 0), (count, rows))[:, None, :]
+    nothing = jnp.zeros((count, 1, rows), F32)
+    back_table = jnp.concatenate([mine, nothing], axis=2)
+    aligned = share % 16 == 0 and ar_proj.shape[0] % 16 == 0 and 2 * count % line == 0
+    aligned = aligned and ar_rows % 128 == 0
+
+    if aligned:
+        gains = jnp.pad(jnp.stack([gain_mix, gain_mlp]), ((0, 14), (0, width - share)))
+        spec, ul, u, mixer, ar, gains, gate_w, up_w, down_w = mix_front(
+            seq_count,
+            line,
+            spans,
+            own,
+            back_table,
+            gains.astype(F32),
+            spectral_proj,
+            ar_proj,
+            (w_gate, w_up, w_down),
+        )
+        mix_scale, mlp_scale = gains[0:1], gains[1:2]
+        mixer = mixer.reshape(2 * block, width)
+    else:
+        gains = jnp.zeros((16, 128), BF16)
+        gains = gains.at[0, :share].set(gain_mix).at[1, :share].set(gain_mlp)
+        x_all, spec, ar, gate_w, up_w, down_w, gains = gather_all(
+            seq_count, line, own, (spectral_proj, ar_proj), (w_gate, w_up, w_down, gains)
+        )
+        ar_full = lax.dynamic_update_slice(
+            jnp.zeros((3 * width, width), BF16), ar.reshape(ar_rows, width), (s * ar_rows, 0)
+        )
+        gains = gains.reshape(-1, 16, 128).astype(F32)
+        mix_scale = gains[:, 0, :share].reshape(1, width)
+        mlp_scale = gains[:, 1, :share].reshape(1, width)
+        fore_table = jnp.concatenate([mine[:, :, :1], nothing, mine[:, :, :0:-1]], axis=2)
+        split = spec.reshape(count, 2, width, width)
+        ul, u, y = forward_mix(spans, x_all, mix_scale, fore_table, split, ar_full)
+        mixer = side_sum(seq_count, line, y, 3).reshape(2 * block, width)
     spec = spec.reshape(count, 2, width, width)
-    ar_rows = ar.shape[0] * ar.shape[1] * ar.shape[2]
-    ar_full = lax.dynamic_update_slice(
-        jnp.zeros((3 * width, width), BF16), ar.reshape(ar_rows, width), (s * ar_rows, 0)
-    )
     gate_w = gate_w.reshape(width, hidden_units)
     up_w = up_w.reshape(width, hidden_units)
     down_w = down_w.reshape(hidden_units, width)
-    gains = gains.reshape(-1, 16, 128).astype(F32)
-    mix_scale = gains[:, 0, :share].reshape(1, width)
-    mlp_scale = gains[:, 1, :share].reshape(1, width)
-
-    mine = lax.dynamic_slice(filters.T, (s * count, 0), (count, rows))[:, None, :]
-    nothing = jnp.zeros((count, 1, rows), F32)
-    back_table = jnp.concatenate([mine, nothing], axis=2)
-    fore_table = jnp.concatenate([mine[:, :, :1], nothing, mine[:, :, :0:-1]], axis=2)
-
-    ul, u, y = forward_mix(spans, x_all, mix_scale, fore_table, spec, ar_full)
-    mixer = side_sum(seq_count, line, y, 3).reshape(2 * block, width)
 
     inputs = own.reshape(2 * block, width).astype(F32)
     cot = cotangent.reshape(2 * block, width)
@@ -1184,8 +1543,7 @@
     )
     mixer_grad = hidden_grad.astype(BF16)
 
-    ar_share = ar_rows // (line * CORES)
-    if w_gate.shape[0] % 16 == 0 and ar_share % 16 == 0 and 2 * count % line == 0:
+    if aligned:
         input_grad, dw, dar, gate_grad, up_grad, down_grad, small = mix_back(
             seq_count,
             line,
@@ -1201,7 +1559,7 @@
             mix_scale,
             (mlp_in, gate_back, up_back, mixed, cot),
             mlp_grad,
-            (w_gate.shape[0], w_down.shape[0], spectral_proj.shape[0], ar_share),
+            (share, w_down.shape[0], spectral_proj.shape[0], ar_proj.shape[0]),
         )
     else:
         down_grad = dot_tn(mixed, cot)

time: 252 us -> 230 us (0.913)
  Pallas kernels: 217 us -> 197 us
  local copies, waits for them, and re-layouts: 13.9 us -> 9.64 us
    pallas_call x3 -> x1, Pallas kernels: 119 us -> 97.3 us  [mix_front(): pl.pallas_call(functools.partial(mix_front_kernel, seq_count, line, spans...]
    unnamed x43 -> x35, local copies, waits for them, and re-layouts: 8.32 us -> 6.34 us
where the time goes in v3:
time: 230 us
  Pallas kernels  197 us (86%)
  matrix products  10.8 us (5%)
  other arithmetic  10.7 us (5%)
  local copies, waits for them, and re-layouts  9.64 us (4%)
    pallas_call x1, Pallas kernels, mix_back(): pl.pallas_call(functools.partial(mix_back_kernel, seq_count, line, spans)...  99.5 us
    pallas_call x1, Pallas kernels, mix_front(): pl.pallas_call(functools.partial(mix_front_kernel, seq_count, line, spans...  97.3 us
    unnamed x35, local copies, waits for them, and re-layouts  6.34 us
    dot_general x3, matrix products, dot_nn(): lax.dot_general(a, b, (((1,), (0,)), ((), ())), preferred_element_type=F32)  5.57 us
    dot_general x3, matrix products, dot_nt(): lax.dot_general(a, b, (((1,), (1,)), ((), ())), preferred_element_type=F32)  5.27 us

profile of v3, /device:TPU:0, one launch (start us, length us, event | category | flops | bytes accessed | tf_op | source)
XLA Modules:
  0.0 229.5 jit_solution(15869084676911640859)
XLA Ops:
  0.7 0.8 copy-done
  2.7 2.0 reverse_select_fusion.2
  4.8 1.4 fusion.15.refs_2_
  6.2 97.3 %mix_front.1 = (bf16[4,1536,512]{2,1,0:T(8,128)(2,1)}, bf16[12,2,512,512]{3,2,1,0:T(8,128)(2,1)}, bf16[2,512,512]{2,1,0:T(8,128)(2,1)}, f32[2,128,512]{2,1,0:T(8...) custom-call(bf16[2,128,512]{2,1,0:T(8,128)(2,1)} %bitcast.59, ...), custom_call_target="tpu_custom_call" | custom-call | tf_op jit(solution)/shard_map/mix_front/pallas_call | solution.py:1441
  103.5 1.3 multiply_reduce_fusion.2
  104.8 1.4 fusion.18
  106.2 1.1 multiply_convert_fusion.3
  107.4 2.4 %fusion.20 = f32[256,2048]{1,0:T(8,128)S(1)} fusion(bf16[256,512]{1,0:T(8,128)(2,1)S(1)} %bitcast.66, bf16[512,2048]{1,0:T(8,128)(2,1)} %bitcast.61), kind=kOutput, calls=%fused_computation.48 | convolution fusion | flops 536870912 | bytes 4456448 | tf_op jit(solution)/shard_map/dot_general | solution.py:22
  109.8 0.7 fusion.19
  110.5 0.9 copy-done.7
  111.4 3.0 %multiply_convert_fusion = (bf16[256,2048]{1,0:T(8,128)(2,1)S(1)}, bf16[256,2048]{1,0:T(8,128)(2,1)S(1)}, bf16[256,2048]{1,0:T(8,128)(2,1)}) fusion(f32[256,2048]{1,0:T(8,128)S(1)} %fusion.19, f32[256,2048]{1,0:T(8,128)S(1)} %fusion.20, bf16[256,512]{1,0:T(8,128)(2,1)S(1)} %bitcast.64, bf16[2048,512]{1,0:T(8,128)(2,1)S(1)} %bitcast.69), kind=kOutput, calls=%fused_computation.9 | convolution fusion | flops 550502400 | bytes 9699328 | tf_op jit(solution)/shard_map/dot_general | solution.py:30
  114.4 0.7 fusion.21
  115.8 0.9 multiply_convert_fusion.2
  116.9 1.5 multiply_reduce_fusion
  118.5 1.1 fusion.17
  119.6 99.5 %mix_back.1 = (f32[2,128,512]{2,1,0:T(8,128)}, f32[768,512]{1,0:T(8,128)}, f32[48,512]{1,0:T(8,128)}, f32[16,2048]{1,0:T(8,128)}, f32[16,2048]{1,0:T(8,128)}, /*index=5*/f32[64,512]{1,0:T(8,128)}, f32[8,512]{1,0:T(8,128)}) custom-call(bf16[2,128,512]{2,1,0:T(8,128)(2,1)} %bitcast.74, bf16[2,512,512]{2,1,0:T(8,128)(2,1)} %get-tuple-element.30.refs_1_, ...), custom_call_target="tpu_custom_call" | custom-call | tf_op jit(solution)/shard_map/mix_back/pallas_call | solution.py:1099
  219.1 2.1 fusion.8
  221.2 0.8 constant_dynamic-slice_fusion
  222.4 2.4 %convolution_add_fusion.1 = f32[256,512]{1,0:T(8,128)S(1)} fusion(f32[256,512]{1,0:T(8,128)S(1)} %get-tuple-element.53, bf16[256,2048]{1,0:T(8,128)(2,1)S(1)} %copy-done.5, bf16[2048,512]{1,0:T(8,128)(2,1)} %bitcast.68), kind=kOutput, calls=%fused_computation.13 | convolution fusion | flops 537001984 | bytes 4194304 | tf_op jit(solution)/shard_map/dot_general | solution.py:22
  224.9 0.8 fusion.7
  225.7 1.1 copy.31
  227.5 0.7 copy.33
  228.2 0.7 copy.34
  228.8 0.7 copy.35
  (36 shorter events, 2.8 us)
Async XLA Ops:
  0.6 0.8 copy-start
  4.8 113.7 %copy-start.6 = (bf16[2,1,128,512]{3,2,0,1:T(8,128)(2,1)}, bf16[2,1,128,512]{3,2,0,1:T(8,128)(2,1)S(1)}, u32[]{:S(2)}) copy-start(bf16[2,1,128,512]{3,2,0,1:T(8,128)(2,1)S(1)} %get-tuple-element.66) | copy-start | bytes 786436
  4.8 101.4 %copy-start.1 = (bf16[2,1,128,512]{3,2,0,1:T(8,128)(2,1)S(1)}, bf16[2,1,128,512]{3,2,0,1:T(8,128)(2,1)}, u32[]{:S(2)}) copy-start(bf16[2,1,128,512]{3,2,0,1:T(8,128)(2,1)} %get-tuple-element.67) | copy-start | bytes 786436
  107.3 2.5 %copy-start.8 = (bf16[4,4,2,16,2048]{4,3,2,1,0:T(8,128)(2,1)S(1)}, bf16[4,4,2,16,2048]{4,3,2,1,0:T(8,128)(2,1)}, u32[]{:S(2)}) copy-start(bf16[4,4,2,16,2048]{4,3,2,1,0:T(8,128)(2,1)} %get-tuple-element.27) | copy-start | bytes 6291460
  109.8 1.6 copy-start.7
  114.4 2.3 copy-start.10
  114.4 2.3 copy-start.4
  114.4 1.4 copy-start.3
  114.4 2.5 %copy-start.2 = (bf16[4,4,2,16,2048]{4,3,2,1,0:T(8,128)(2,1)S(1)}, bf16[4,4,2,16,2048]{4,3,2,1,0:T(8,128)(2,1)}, u32[]{:S(2)}) copy-start(bf16[4,4,2,16,2048]{4,3,2,1,0:T(8,128)(2,1)} %get-tuple-element.28) | copy-start | bytes 6291460
  119.6 102.9 %copy-start.5 = (bf16[256,2048]{1,0:T(8,128)(2,1)S(1)}, bf16[256,2048]{1,0:T(8,128)(2,1)}, u32[]{:S(2)}) copy-start(bf16[256,2048]{1,0:T(8,128)(2,1)} %get-tuple-element.58.refs_12_) | copy-start | bytes 3145732
  222.4 3.3 %copy-start.9 = (f32[768,512]{1,0:T(8,128)S(1)}, f32[768,512]{1,0:T(8,128)}, u32[]{:S(2)}) copy-start(f32[768,512]{1,0:T(8,128)} %get-tuple-element.80) | copy-start | bytes 4718596
  224.9 2.0 copy-start.14
  224.9 2.7 %copy-start.13 = (f32[16,2048]{1,0:T(8,128)S(1)}, f32[16,2048]{1,0:T(8,128)}, u32[]{:S(2)}) copy-start(f32[16,2048]{1,0:T(8,128)} %get-tuple-element.83) | copy-start | bytes 393220
  224.9 3.3 %copy-start.12 = (f32[16,2048]{1,0:T(8,128)S(1)}, f32[16,2048]{1,0:T(8,128)}, u32[]{:S(2)}) copy-start(f32[16,2048]{1,0:T(8,128)} %get-tuple-element.84) | copy-start | bytes 393220
  225.7 3.1 %copy-start.11 = (f32[64,512]{1,0:T(8,128)S(1)}, f32[64,512]{1,0:T(8,128)}, u32[]{:S(2)}) copy-start(f32[64,512]{1,0:T(8,128)} %get-tuple-element.85) | copy-start | bytes 393220

commit v4 on v3

--- a/solution.py
+++ b/solution.py
@@ -691,24 +691,19 @@
     )(dy, u, table, w, ul, ar)
 
 
-def lag_by(values, lag, span, move):
-    return jnp.where(
-        lag == 0, values, jnp.where(lag == 1, move(values, 1, span), move(values, 2, span))
-    )
-
-
-def mix_back_kernel(seq_count, line, spans, *refs):
-    (dy_ref, u_ref, row_ref, w_hbm, ul_hbm, ar_ref, x_ref, hg_ref, scale_ref) = refs[:9]
-    (z_ref, gb_ref, ub_ref, mixed_ref, cot_ref, mlp_ref) = refs[9:15]
-    (tg_ref, dw_ref, dar_ref, gg_ref, ug_ref, dg_ref, small_ref) = refs[15:22]
-    (dy, dsig, acc, conv, du_in, ul_buf, w_buf, dar) = refs[22:30]
-    (deep, deep_in, deep_run, wide, wide_in, wide_side, wide_run) = refs[30:37]
-    (g_own, g_pair, g_side, g_sum, g_line) = refs[37:42]
-    (load_sem, dys, dyr, dus, dur, ps, pr, zs, zr, wps, wpr, ws, wr, wzs, wzr, gs, gr) = refs[42:]
+def mix_back_kernel(seq_count, line, *refs):
+    (layout_ref, dy, u_ref, row_ref, w_hbm, ul_hbm, ar_ref, x_ref, hg_ref, scale_ref) = refs[:10]
+    (z_ref, gb_ref, ub_ref, mixed_ref, cot_ref, mlp_ref) = refs[10:16]
+    (tg_ref, dw_ref, dar_ref, gg_ref, ug_ref, dg_ref, small_ref) = refs[16:23]
+    (keep, dsig, acc, conv, du_in, ul_buf, w_buf, dar) = refs[23:31]
+    (deep, deep_in, deep_run, wide, wide_in, wide_side, wide_run) = refs[31:38]
+    (g_own, g_pair, g_side, g_sum, g_line) = refs[38:43]
+    (load_sem, dus, dur, ps, pr, zs, zr, wps, wpr, ws, wr, wzs, wzr, gs, gr) = refs[43:]
     s, z, c, g = place(seq_count, line)
     twin = {"grp": g + 1 - 2 * c}
     rows, width = dy.shape[1], dy.shape[2]
-    block = dy_ref.shape[1]
+    block = x_ref.shape[1]
+    short = [layout_ref[m, 0].astype(F32) for m in range(2)]
     count = w_hbm.shape[0]
     per_chip = 2 * count // line
     n = per_chip * width // CORES
@@ -735,24 +730,95 @@
     load_w.start()
     greet(seq_count, line, s, z, c, g, twin=True, side=True, whole_line=True)
 
-    dy_copies = []
-    for i in range(1, seq_count):
-        dy_copies.append(
-            remote(
-                dy_ref,
-                dy.at[:, mine, :],
-                dys.at[i - 1],
-                dyr.at[i - 1],
-                {"seq": lax.rem(s + i, seq_count)},
-            )
-        )
-        dy_copies[-1].start()
-    dy[:, mine, :] = dy_ref[...]
+    def ar_place(i):
+        at = s * ar_chunks + i
+        lag = lax.div(at, width // lanes)
+        col = lax.rem(at, width // lanes)
+        return lag, pl.ds(pl.multiple_of(col * lanes, lanes), lanes)
+
+    for i in range(ar_chunks):
+        lag, cols = ar_place(i)
+        total = 0.0
+        for m in range(2):
+            v = lagged_by(u_ref[m, :, cols].astype(F32), lag, short[m]).astype(BF16)
+            total = total + dot_tn(v, dy[m])
+        dar[i * lanes : (i + 1) * lanes, :] = total.astype(BF16)
+    for l in range(line):
+        for cc in range(CORES):
+            r = (l * CORES + cc) * ar_share
+            deep[cc, l, n:, :] = dar[r : r + ar_share, :]
+
+    def twin_deep(i):
+        l = dest(i)
+        return remote(deep.at[1 - c, l], deep_in.at[l], ps.at[i], pr.at[i], twin)
+
+    def hop(run, own, send, recv, way, t, first):
+        target = line - 1 - t if way == 0 else t
+        src = own(target) if first else run.at[way, t]
+        to = g + CORES if way == 0 else g - CORES
+        return remote(src, run.at[way, t], send.at[way, t], recv.at[way, t], {"grp": to})
+
+    def deep_own(l):
+        return deep_in.at[l]
+
+    def wide_own(l):
+        return wide_in.at[s, l]
+
+    deep_line = (deep_run, deep_own, zs, zr)
+    wide_line = (wide_run, wide_own, wzs, wzr)
+
+    def begin(kind, t):
+        for way in (0, 1):
+
+            @pl.when(z == 0 if way == 0 else z == line - 1)
+            def _():
+                hop(*kind, way, t, True).start()
+
+    def relay(kind, phase):
+        run, own = kind[0], kind[1]
+        for way in (0, 1):
+            for t in range(phase):
+                at = phase - t if way == 0 else line - 1 - (phase - t)
+                target = line - 1 - t if way == 0 else t
+
+                @pl.when(z == at)
+                def _():
+                    hop(*kind, way, t, False).wait_recv()
+                    mixed = run[way, t].astype(F32) + own(target)[...].astype(F32)
+                    run[way, t] = mixed.astype(BF16)
+                    hop(*kind, way, t, False).start()
+
+    def compute(i):
+        l = dest(i)
+        load(i).wait()
+        for j in range(per_chip):
+            val = dot_tn(ul_buf[i % 2, j, 0], dy[0]) + dot_tn(ul_buf[i % 2, j, 1], dy[1])
+            val = val.astype(BF16)
+            for cc in range(CORES):
+                lo, hi = max(j * width, cc * n), min((j + 1) * width, (cc + 1) * n)
+                if lo < hi:
+                    deep[cc, l, lo - cc * n : hi - cc * n, :] = val[lo - j * width : hi - j * width]
+        twin_deep(i).start()
+        if i + 2 < line:
+            load(i + 2).start()
+
+    def combine(i):
+        l = dest(i)
+        twin_deep(i).wait_recv()
+        deep_in[l] = (deep[c, l].astype(F32) + deep_in[l].astype(F32)).astype(BF16)
+        if i < line - 1:
+            begin(deep_line, i)
+
+    compute(0)
+    compute(1)
+    combine(0)
 
     span_f = gb_ref.shape[1] // seq_count
     down_share = dg_ref.shape[0]
-    for j in range(seq_count):
-        part = slice(j * span_f, (j + 1) * span_f)
+
+    @pl.loop(0, seq_count)
+    def _(j):
+        part = pl.ds(pl.multiple_of(j * span_f, span_f), span_f)
         for which, back in ((0, gb_ref), (1, ub_ref)):
             val = dot_tn(z_ref[...], back[:, part]).astype(BF16)
             for k in range(seq_count):
@@ -773,92 +839,9 @@
     wide_twin = remote(wide.at[1 - c], wide_in, wps, wpr, twin)
     wide_twin.start()
 
-    for x in dy_copies:
-        x.wait_recv()
-
-    def ar_place(i):
-        at = s * ar_chunks + i
-        lag = lax.div(at, width // lanes)
-        col = lax.rem(at, width // lanes)
-        return lag, pl.ds(pl.multiple_of(col * lanes, lanes), lanes)
-
-    for i in range(ar_chunks):
-        lag, cols = ar_place(i)
-        total = 0.0
-        for m in range(2):
-            v = lag_by(u_ref[m, :, cols].astype(F32), lag, spans[m], lagged).astype(BF16)
-            total = total + dot_tn(v, dy[m])
-        dar[i * lanes : (i + 1) * lanes, :] = total.astype(BF16)
-    for l in range(line):
-        for cc in range(CORES):
-            r = (l * CORES + cc) * ar_share
-            deep[cc, l, n:, :] = dar[r : r + ar_share, :]
-
-    def twin_deep(i):
-        l = dest(i)
-        return remote(deep.at[1 - c, l], deep_in.at[l], ps.at[i], pr.at[i], twin)
-
-    def hop(run, own, send, recv, way, t, first):
-        target = line - 1 - t if way == 0 else t
-        src = own(target) if first else run.at[way, t]
-        to = g + CORES if way == 0 else g - CORES
-        return remote(src, run.at[way, t], send.at[way, t], recv.at[way, t], {"grp": to})
-
-    def deep_own(l):
-        return deep_in.at[l]
-
-    def wide_own(l):
-        return wide_in.at[s, l]
-
-    deep_line = (deep_run, deep_own, zs, zr)
-    wide_line = (wide_run, wide_own, wzs, wzr)
-
-    def begin(kind, t):
-        for way in (0, 1):
-
-            @pl.when(z == 0 if way == 0 else z == line - 1)
-            def _():
-                hop(*kind, way, t, True).start()
-
-    def relay(kind, phase):
-        run, own = kind[0], kind[1]
-        for way in (0, 1):
-            for t in range(phase):
-                at = phase - t if way == 0 else line - 1 - (phase - t)
-                target = line - 1 - t if way == 0 else t
-
-                @pl.when(z == at)
-                def _():
-                    hop(*kind, way, t, False).wait_recv()
-                    mixed = run[way, t].astype(F32) + own(target)[...].astype(F32)
-                    run[way, t] = mixed.astype(BF16)
-                    hop(*kind, way, t, False).start()
-
-    def compute(i):
-        l = dest(i)
-        load(i).wait()
-        for j in range(per_chip):
-            val = dot_tn(ul_buf[i % 2, j, 0], dy[0]) + dot_tn(ul_buf[i % 2, j, 1], dy[1])
-            val = val.astype(BF16)
-            for cc in range(CORES):
-                lo, hi = max(j * width, cc * n), min((j + 1) * width, (cc + 1) * n)
-                if lo < hi:
-                    deep[cc, l, lo - cc * n : hi - cc * n, :] = val[lo - j * width : hi - j * width]
-        twin_deep(i).start()
-        if i + 2 < line:
-            load(i + 2).start()
-
-    def combine(i):
-        l = dest(i)
-        twin_deep(i).wait_recv()
-        deep_in[l] = (deep[c, l].astype(F32) + deep_in[l].astype(F32)).astype(BF16)
-        if i < line - 1:
-            begin(deep_line, i)
-
-    for i in range(line):
+    for i in range(2, line):
         compute(i)
-        if i > 0:
-            combine(i - 1)
+        combine(i - 1)
     combine(line - 1)
 
     wide_twin.wait_recv()
@@ -880,23 +863,21 @@
     signs = signs_of(rows)
     for m in range(2):
         dsig[m] = (dy[m].astype(F32) * signs).astype(BF16)
+        keep[m] = same_quarter(rows, short[m])
     acc[...] = jnp.zeros_like(acc)
     for i in range(ar_chunks):
         lag, cols = ar_place(i)
         for m in range(2):
             val = dot_nt(dy[m], ar_ref[i * lanes : (i + 1) * lanes, :])
-            acc[m, :, cols] += lag_by(val, lag, spans[m], led)
+            acc[m, :, cols] += led_by(val, lag, short[m])
     load_w.wait()
 
     def filter_step(k):
         table = spread(row_ref[k], rows)
         for m in range(2):
-            span = spans[m]
-            for j in range(rows // span):
-                part = slice(j * span, (j + 1) * span)
-                conv[0, part, :] = dot_nn(table[:span, :span], dy[m, part, :]).astype(BF16)
-                minus = dot_nn(table[:span, :span], dsig[m, part, :])
-                conv[1, part, :] = (minus * signs[part]).astype(BF16)
+            kept_table = table * keep[m]
+            conv[0] = dot_nn(kept_table, dy[m]).astype(BF16)
+            conv[1] = (dot_nn(kept_table, dsig[m]) * signs).astype(BF16)
             acc[m] += dot_nt(conv[0], w_buf[k, 0]) + dot_nt(conv[1], w_buf[k, 1])
 
     half = count // 2
@@ -936,7 +917,7 @@
         tg_ref[m] = hg_ref[m] + inv * scaled - x * (inv * inv * inv) * centre
     g_own[...] = jnp.zeros_like(g_own)
     g_own[0:1, :] = gain
-    g_own[1:2, :] = mlp_ref[...]
+    g_own[1:2, :] = mlp_ref[0:1, :]
     small_pair = remote(g_own, g_pair, gs.at[0], gr.at[0], twin)
     small_pair.start()
 
@@ -1020,9 +1001,10 @@
     total = g_sum[...]
     for j in range(line - 1):
         total = total + g_line[j]
-    small_ref[...] = total
-
-    for x in dy_copies + sides + du_copies:
+    at = (s * (CORES * line) + g) * (width // (seq_count * CORES * line))
+    small_ref[...] = pltpu.roll(total, lax.rem(width - at, width), 1)
+
+    for x in sides + du_copies:
         x.wait_send()
     wide_twin.wait_send()
     for i in range(line):
@@ -1037,10 +1019,10 @@
                     hop(*kind, way, t, False).wait_send()
 
 
-def mix_back(seq_count, line, spans, dy, u, table, w, ul, ar, x, hg, scale, mlp, mlp_grad, shares):
+def mix_back(seq_count, line, layout, dy, u, table, w, ul, ar, x, hg, scale, mlp, mlp_grad, shares):
     z, gate_back, up_back, mixed, cot = mlp
     share, down_share, deep_share, ar_share = shares
-    _, block, width = dy.shape
+    _, block, width = x.shape
     rows = block * seq_count
     count = w.shape[0]
     per_chip = 2 * count // line
@@ -1058,7 +1040,7 @@
     ]
     deep = (deep_share + ar_share, width)
     scratch = [
-        pltpu.VMEM((2, rows, width), BF16),
+        pltpu.VMEM((2, rows, rows), BF16),
         pltpu.VMEM((2, rows, width), BF16),
         pltpu.VMEM((2, rows, width), F32),
         pltpu.VMEM((2, rows, width), BF16),
@@ -1081,8 +1063,6 @@
         DMA((3,)),
         DMA((seq_count - 1,)),
         DMA((seq_count - 1,)),
-        DMA((seq_count - 1,)),
-        DMA((seq_count - 1,)),
         DMA((line,)),
         DMA((line,)),
         DMA((2, line - 1)),
@@ -1097,45 +1077,79 @@
         DMA((seq_count + line,)),
     ]
     return pl.pallas_call(
-        functools.partial(mix_back_kernel, seq_count, line, spans),
+        functools.partial(mix_back_kernel, seq_count, line),
         out_shape=out_shape,
-        in_specs=[WHOLE] * 3 + [ANY] * 2 + [WHOLE] * 10,
+        in_specs=[pl.BlockSpec(memory_space=pltpu.SMEM)] + [WHOLE] * 3 + [ANY] * 2 + [WHOLE] * 10,
         out_specs=[WHOLE] * 7,
         scratch_shapes=scratch,
         compiler_params=params(6),
         name="mix_back",
-    )(dy, u, table, w, ul.reshape(2 * count, 2, rows, width), ar, x, hg, scale, z, gate_back, up_back, mixed, cot, mlp_grad)
-
-
-def mix_front_kernel(seq_count, line, spans, *refs):
-    (tok_ref, row_ref, gain_ref, spec_hbm, ar_hbm) = refs[:5]
-    wide_in = refs[5:8]
-    (w_hbm, ul_hbm, u_ref, y_ref, ar_ref, gain_out) = refs[8:14]
-    wide_out = refs[14:17]
-    (x_all, both, acc, y_bf, y_in, w_buf, ul_buf) = refs[17:24]
-    stage = refs[24:27]
-    (g_own, g_side, g_sum, g_line, g_all, g_twin) = refs[27:33]
-    (load_sem, store_sem, ul_sem, w_sem, ts, tr, ys, yr, zs, zr, hs, hr) = refs[33:45]
-    (ps, pr, ws, wr, wps, wpr, gs, gr) = refs[45:]
+    )(layout, dy, u, table, w, ul, ar, x, hg, scale, z, gate_back, up_back, mixed, cot, mlp_grad)
+
+
+def kept(rows, short, lag):
+    pos = lax.broadcasted_iota(jnp.int32, (rows, 1), 0)
+    whole = (pos >= lag).astype(F32)
+    return whole * (1.0 - short * (1.0 - (lax.rem(pos, rows // 4) >= lag).astype(F32)))
+
+
+def lagged_by(values, lag, short):
+    rows = values.shape[0]
+    one = pltpu.roll(values, 1, 0) * kept(rows, short, 1)
+    two = pltpu.roll(values, 2, 0) * kept(rows, short, 2)
+    return jnp.where(lag == 0, values, jnp.where(lag == 1, one, two))
+
+
+def led_by(values, lag, short):
+    rows = values.shape[0]
+    one = pltpu.roll(values * kept(rows, short, 1), rows - 1, 0)
+    two = pltpu.roll(values * kept(rows, short, 2), rows - 2, 0)
+    return jnp.where(lag == 0, values, jnp.where(lag == 1, one, two))
+
+
+def same_quarter(rows, short):
+    down = lax.div(lax.broadcasted_iota(jnp.int32, (rows, rows), 0), rows // 4)
+    over = lax.div(lax.broadcasted_iota(jnp.int32, (rows, rows), 1), rows // 4)
+    return (1.0 - short * (1.0 - (down == over).astype(F32))).astype(BF16)
+
+
+def mix_front_kernel(seq_count, line, *refs):
+    (layout_ref, tok_ref, row_ref, gain_ref, cot_ref, spec_hbm, ar_hbm) = refs[:7]
+    wide_in = refs[7:10]
+    (w_hbm, ul_hbm, u_ref, ar_ref, gain_out) = refs[10:15]
+    (z_ref, gb_ref, ub_ref, mixed_ref, hg_ref, dy_ref, mlp_ref, out_ref) = refs[15:23]
+    (x_all, both, acc, y_bf, y_in, w_buf, ul_buf, keep, hid, dz, dy_own) = refs[23:34]
+    wide_buf = refs[34:37]
+    (g_own, g_side, g_sum, g_line, g_all, g_twin) = refs[37:43]
+    (load_sem, ul_sem, w_sem, ts, tr, ys, yr, zs, zr, hs, hr) = refs[43:54]
+    (ps, pr, ws, wr, wps, wpr, gs, gr, ds_, dr_) = refs[54:]
     s, z, c, g = place(seq_count, line)
     twin = {"grp": g + 1 - 2 * c}
     rows, width = x_all.shape[1], x_all.shape[2]
     block = tok_ref.shape[1]
     n = spec_hbm.shape[0]
+    hn = n // 2
     blocks = ul_buf.shape[0]
     count = blocks // 2
     per_chip = blocks // line
     lanes = 128
     wide = range(3)
     mine = pl.ds(pl.multiple_of(s * block, block), block)
-
-    def piece(l):
-        return w_buf.at[l, pl.ds(pl.multiple_of(c * n, n), n), :]
-
-    load_w = pltpu.make_async_copy(spec_hbm, piece(z), load_sem.at[0])
-    load_ar = pltpu.make_async_copy(ar_hbm, ar_ref.at[z, c], load_sem.at[1])
-    loads = [pltpu.make_async_copy(wide_in[i], stage[i], load_sem.at[2 + i]) for i in wide]
-    for x in loads + [load_ar, load_w]:
+    short = [layout_ref[m, 0].astype(F32) for m in range(2)]
+
+    def piece(l, h):
+        return w_buf.at[l, pl.ds(pl.multiple_of(c * n + h * hn, hn), hn), :]
+
+    def wide_own(i, l):
+        return wide_buf[i].at[s, l, c]
+
+    load_w = [
+        pltpu.make_async_copy(spec_hbm.at[pl.ds(h * hn, hn)], piece(z, h), load_sem.at[h])
+        for h in range(2)
+    ]
+    load_ar = pltpu.make_async_copy(ar_hbm, ar_ref.at[z, c], load_sem.at[2])
+    loads = [pltpu.make_async_copy(wide_in[i], wide_own(i, z), load_sem.at[3 + i]) for i in wide]
+    for x in load_w + [load_ar] + loads:
         x.start()
     at = (s * (CORES * line) + g) * (width // (seq_count * CORES * line))
     g_own[...] = pltpu.roll(gain_ref[...], at, 1).astype(BF16)
@@ -1152,79 +1166,88 @@
         toks.append(remote(tok_ref, x_all.at[:, mine, :], ts.at[i - 1], tr.at[i - 1], to))
         toks[-1].start()
 
+    def onward(way):
+        return {"grp": g + CORES if way == 0 else g - CORES}
+
     def early_own(i, l):
-        return ar_ref.at[l, c] if i == 3 else wide_out[i].at[s, l, c]
-
-    def early_hop(i, way, t, origin):
-        if t > 0:
-            src = early_own(i, origin)
-        else:
-            src = ar_hbm if i == 3 else wide_in[i]
-        to = g + CORES if way == 0 else g - CORES
-        return remote(src, early_own(i, origin), hs.at[i, way, t], hr.at[i, way, t], {"grp": to})
-
-    def deep_hop(way, t, origin):
-        to = g + CORES if way == 0 else g - CORES
-        return remote(
-            piece(origin), piece(origin), zs.at[way, t], zr.at[way, t], {"grp": to}
-        )
-
-    def each_hop(way, t, which, origin, act):
-        if which == "early":
-            for i in range(4):
-                act(early_hop(i, way, t, origin))
-        else:
-            act(deep_hop(way, t, origin))
-
-    def first(which):
+        return ar_ref.at[l, c] if i == 3 else wide_own(i, l)
+
+    def early_hops(way, t, origin):
+        hops = []
+        for i in range(4):
+            if t > 0:
+                src = early_own(i, origin)
+            else:
+                src = ar_hbm if i == 3 else wide_in[i]
+            hops.append(
+                remote(src, early_own(i, origin), hs.at[i, way, t], hr.at[i, way, t], onward(way))
+            )
+        return hops
+
+    def deep_hops(h):
+        def build(way, t, origin):
+            src = spec_hbm.at[pl.ds(h * hn, hn)] if t == 0 else piece(origin, h)
+            dst = piece(origin, h)
+            return [remote(src, dst, zs.at[h, way, t], zr.at[h, way, t], onward(way))]
+
+        return build
+
+    def first(build):
         for way in (0, 1):
             sends, _, origin, _ = line_conditions(line, z, way, 0)
 
             @pl.when(sends)
             def _():
-                each_hop(way, 0, which, origin, lambda x: x.start())
-
-    def arrive(which, t, after=None):
+                for x in build(way, 0, origin):
+                    x.start()
+
+    def arrive(build, t, after):
         for way in (0, 1):
             _, receives, _, origin = line_conditions(line, z, way, t)
 
             @pl.when(receives)
             def _():
-                each_hop(way, t, which, origin, lambda x: x.wait_recv())
+                for x in build(way, t, origin):
+                    x.wait_recv()
                 if t + 1 < line - 1:
                     sends = line_conditions(line, z, way, t + 1)[0]
 
                     @pl.when(sends)
                     def _():
-                        each_hop(way, t + 1, which, origin, lambda x: x.start())
-
-                if after is not None:
-                    after(origin)
-
-    def sent(which):
+                        for x in build(way, t + 1, origin):
+                            x.start()
+
+                after(origin)
+
+    def sent(build):
         for t in range(line - 1):
             for way in (0, 1):
                 sends, _, origin, _ = line_conditions(line, z, way, t)
 
                 @pl.when(sends)
                 def _():
-                    each_hop(way, t, which, origin, lambda x: x.wait_send())
-
-    first("early")
-    x_all[:, mine, :] = tok_ref[...]
-    stores = []
-    for i in wide:
-        loads[i].wait()
-        stores.append(pltpu.make_async_copy(stage[i], wide_out[i].at[s, z, c], store_sem.at[i]))
-        stores[-1].start()
-    load_ar.wait()
-    load_w.wait()
-
-    def twin_deep(l):
-        return remote(piece(l), piece(l), ps.at[l], pr.at[l], twin)
-
-    twin_deep(z).start()
-
+                    for x in build(way, t, origin):
+                        x.wait_send()
+
+    def sides(l, own=False):
+        copies = []
+        for i in wide:
+            for j in range(1, seq_count):
+                src = wide_in[i] if own else wide_own(i, l)
+                to = {"seq": lax.rem(s + j, seq_count)}
+                copies.append(
+                    remote(src, wide_own(i, l), ws.at[i, l, j - 1], wr.at[i, l, j - 1], to)
+                )
+        return copies
+
+    def begin_sides(l):
+        for x in sides(l):
+            x.start()
+
+    def twin_deep(l, h):
+        return remote(piece(l, h), piece(l, h), ps.at[h, l], pr.at[h, l], twin)
+
+    first(early_hops)
     total = g_own[...]
     for i, x in enumerate(gain_sides):
         x.wait_recv()
@@ -1236,8 +1259,19 @@
         to = {"grp": lax.rem(g + CORES * j, CORES * line)}
         gain_lines.append(remote(g_sum, g_line.at[j - 1], gs.at[k], gr.at[k], to))
         gain_lines[-1].start()
-    arrive("early", 0)
-    first("deep")
+    first(deep_hops(0))
+    for x in sides(z, True):
+        x.start()
+    x_all[:, mine, :] = tok_ref[...]
+    for h in range(2):
+        load_w[h].wait()
+        twin_deep(z, h).start()
+    for x in loads + [load_ar]:
+        x.wait()
+    for m in range(2):
+        keep[m] = same_quarter(rows, short[m])
+    arrive(early_hops, 0, begin_sides)
+    first(deep_hops(1))
     total = g_sum[...]
     for j, x in enumerate(gain_lines):
         x.wait_recv()
@@ -1268,58 +1302,63 @@
     def filter_step(k):
         table = spread(row_ref[k], rows)
         for m in range(2):
-            span = spans[m]
-            for j in range(rows // span):
-                part = slice(j * span, (j + 1) * span)
-                val = dot_tn(table[:span, :span], both[m, part, :])
-                ul_buf[2 * k, m, part, :] = val[:, :width].astype(BF16)
-                ul_buf[2 * k + 1, m, part, :] = (val[:, width:] * signs[part]).astype(BF16)
+            val = dot_tn(table * keep[m], both[m])
+            ul_buf[2 * k, m] = val[:, :width].astype(BF16)
+            ul_buf[2 * k + 1, m] = (val[:, width:] * signs).astype(BF16)
         ul_store(k).start()
 
+    def add_part(l, h):
+        @pl.loop(0, 2)
+        def _(m):
+            total = 0.0
+            for cc in range(CORES):
+                lo, end = cc * n + h * hn, cc * n + (h + 1) * hn
+                while lo < end:
+                    j = lo // width
+                    hi = min(end, (j + 1) * width)
+                    left = ul_buf[l * per_chip + j, m, :, lo - j * width : hi - j * width]
+                    total = total + dot_nn(left, w_buf[l, lo:hi, :])
+                    lo = hi
+            acc[m] += total
+
+    def w_store(l):
+        return pltpu.make_async_copy(w_buf.at[l], w_hbm.at[l], w_sem.at[l])
+
+    def nothing(origin):
+        pass
+
+    def deep_arrive(t, h):
+        arrive(deep_hops(h), t, lambda origin: twin_deep(origin, h).start())
+
+    def deep_add(t, h):
+        for way in (0, 1):
+            _, receives, _, origin = line_conditions(line, z, way, t)
+
+            @pl.when(receives)
+            def _():
+                twin_deep(origin, h).wait_recv()
+                if h == 1:
+                    w_store(origin).start()
+                add_part(origin, h)
+
     half = count // 2
+    acc[...] = jnp.zeros_like(acc)
     pl.loop(0, half)(filter_step)
     if line > 2:
-        arrive("early", 1)
+        arrive(early_hops, 1, begin_sides)
+    deep_arrive(0, 0)
     pl.loop(half, count)(filter_step)
-    for x in stores:
-        x.wait()
-
-    acc[...] = jnp.zeros_like(acc)
-
-    def add_chip(l):
-        for m in range(2):
-            total = 0.0
-            for j in range(per_chip):
-                total = total + dot_nn(
-                    ul_buf[l * per_chip + j, m], w_buf[l, j * width : (j + 1) * width, :]
-                )
-            acc[m] += total
-
-    def w_store(l):
-        return pltpu.make_async_copy(w_buf.at[l], w_hbm.at[l], w_sem.at[l])
-
-    twin_deep(z).wait_recv()
+    for h in range(2):
+        twin_deep(z, h).wait_recv()
+        add_part(z, h)
     w_store(z).start()
-    add_chip(z)
+    deep_arrive(0, 1)
     for t in range(2, line - 1):
-        arrive("early", t)
-
+        arrive(early_hops, t, begin_sides)
     ar_twin = remote(ar_ref.at[:, c], ar_ref.at[:, c], wps.at[3, 0], wpr.at[3, 0], twin)
     ar_twin.start()
-    sides = []
-    for i in wide:
-        for j in range(1, seq_count):
-            part = wide_out[i].at[s, :, c]
-            to = {"seq": lax.rem(s + j, seq_count)}
-            sides.append(remote(part, part, ws.at[i, j - 1], wr.at[i, j - 1], to))
-            sides[-1].start()
-
-    def twin_wide(i, k):
-        part = wide_out[i].at[k, :, c]
-        return remote(part, part, wps.at[i, k], wpr.at[i, k], twin)
-
-    for i in wide:
-        twin_wide(i, s).start()
+    for h in range(2):
+        deep_add(0, h)
 
     ar_twin.wait_recv()
     ar_rows = ar_ref.shape[0] * ar_ref.shape[1] * ar_ref.shape[2]
@@ -1331,25 +1370,25 @@
         col = lax.rem(place_at, width // lanes)
         cols = pl.ds(pl.multiple_of(col * lanes, lanes), lanes)
         for m in range(2):
-            v = lag_by(u_ref[m, :, cols].astype(F32), lag, spans[m], lagged).astype(BF16)
+            v = lagged_by(u_ref[m, :, cols].astype(F32), lag, short[m]).astype(BF16)
             acc[m] += dot_nn(v, ar_all[i * lanes : (i + 1) * lanes])
 
-    for t in range(line - 1):
+    def twin_wide(i, k):
+        part = wide_buf[i].at[k, :, c]
+        return remote(part, part, wps.at[i, k], wpr.at[i, k], twin)
+
+    for t in range(1, line - 1):
+        deep_arrive(t, 0)
         if t == line - 2:
-            for x in sides:
-                x.wait_recv()
+            for l in range(line):
+                for x in sides(l):
+                    x.wait_recv()
             for i in wide:
-                for j in range(1, seq_count):
-                    twin_wide(i, lax.rem(s + seq_count - j, seq_count)).start()
-        arrive("deep", t, lambda origin: twin_deep(origin).start())
-        for way in (0, 1):
-            _, receives, _, origin = line_conditions(line, z, way, t)
-
-            @pl.when(receives)
-            def _():
-                twin_deep(origin).wait_recv()
-                w_store(origin).start()
-                add_chip(origin)
+                for k in range(seq_count):
+                    twin_wide(i, k).start()
+        deep_add(t, 0)
+        deep_arrive(t, 1)
+        deep_add(t, 1)
 
     y_bf[...] = acc[...].astype(BF16)
     y_copies = []
@@ -1366,87 +1405,164 @@
         )
         y_copies[-1].start()
 
-    sent("early")
-    sent("deep")
-    for l in range(line):
-        twin_deep(l).wait_send()
-        w_store(l).wait()
     for i in wide:
         for k in range(seq_count):
             twin_wide(i, k).wait()
-    for x in toks + sides + gain_sides + gain_lines + [ar_twin, gain_twin]:
+    sent(early_hops)
+    for h in range(2):
+        sent(deep_hops(h))
+        for l in range(line):
+            twin_deep(l, h).wait_send()
+    for l in range(line):
+        w_store(l).wait()
+        for x in sides(l):
+            x.wait_send()
+    for x in toks + gain_sides + gain_lines + [ar_twin, gain_twin]:
         x.wait_send()
     for k in range(count):
         ul_store(k).wait()
+
     for m in range(2):
-        y_ref[m] = acc[m, mine, :]
+        part = slice(m * block, (m + 1) * block)
+        hid[part, :] = tok_ref[m].astype(F32) + acc[m, mine, :]
     for i, x in enumerate(y_copies):
         x.wait_recv()
-        y_ref[...] += y_in[i].astype(F32)
+        for m in range(2):
+            hid[m * block : (m + 1) * block, :] += y_in[i, m].astype(F32)
+    h = hid[...]
+    inv_two = lax.rsqrt(jnp.mean(h * h, axis=-1, keepdims=True) + EPSILON)
+    mlp_scale = gain[1:2, :]
+    z_ref[...] = (h * inv_two * mlp_scale).astype(BF16)
+    dz[...] = jnp.zeros_like(dz)
+    hidden_units = gb_ref.shape[1]
+    step = hidden_units // seq_count
+    root = 0.7978845608028654
+
+    @pl.loop(0, seq_count)
+    def _(j):
+        part = pl.ds(pl.multiple_of(j * step, step), step)
+        gate_w = wide_buf[0][:, :, :, :, part].reshape(width, step)
+        up_w = wide_buf[1][:, :, :, :, part].reshape(width, step)
+        down_w = wide_buf[2][j].reshape(step, width)
+        gate = dot_nn(z_ref[...], gate_w)
+        up = dot_nn(z_ref[...], up_w)
+        back = dot_nt(cot_ref[...], down_w)
+        square = gate * gate
+        tan = jnp.tanh(root * (gate + 0.044715 * (square * gate)))
+        share = 0.5 * (1.0 + tan)
+        gelu = gate * share
+        slope = share + 0.5 * gate * (1.0 - tan * tan) * (
+            root * (1.0 + (3.0 * 0.044715) * square)
+        )
+        mixed_ref[:, part] = (gelu * up).astype(BF16)
+        gate_back = (back * up * slope).astype(BF16)
+        up_back = (back * gelu).astype(BF16)
+        gb_ref[:, part] = gate_back
+        ub_ref[:, part] = up_back
+        dz[...] += dot_nt(gate_back, gate_w) + dot_nt(up_back, up_w)
+    grad = dz[...]
+    h = hid[...]
+    scaled = grad * mlp_scale
+    centre = jnp.mean(scaled * h, axis=-1, keepdims=True)
+    dh = cot_ref[...].astype(F32) + inv_two * scaled - h * (inv_two * inv_two * inv_two) * centre
+    mlp_ref[...] = jnp.zeros_like(mlp_ref)
+    mlp_ref[0:1, :] = jnp.sum(grad * h * inv_two, axis=0, keepdims=True)
+    for m in range(2):
+        part = slice(m * block, (m + 1) * block)
+        hg_ref[m] = dh[part]
+        dy_own[m] = dh[part].astype(BF16)
+    dy_copies = []
+    for i in range(1, seq_count):
+        to = {"seq": lax.rem(s + i, seq_count)}
+        dy_copies.append(remote(dy_own, dy_ref.at[:, mine, :], ds_.at[i - 1], dr_.at[i - 1], to))
+        dy_copies[-1].start()
+    dy_ref[:, mine, :] = dy_own[...]
+    total = hid[...]
+    for j in range(seq_count):
+        down_w = wide_buf[2][j].reshape(step, width)
+        total = total + dot_nn(mixed_ref[:, j * step : (j + 1) * step], down_w)
+    for m in range(2):
+        out_ref[m] = total[m * block : (m + 1) * block]
     for x in y_copies:
         x.wait_send()
-
-
-def mix_front(seq_count, line, spans, tok, table, gain, spec, ar, wide):
+    for x in dy_copies:
+        x.wait()
+
+
+def mix_front(seq_count, line, layout, tok, table, gain, cot, spec, ar, wide):
     _, block, width = tok.shape
     rows = block * seq_count
     count = table.shape[0]
+    hidden_units = wide[0].shape[1]
     small = (16, width)
+    vmem = pltpu.VMEM
     out_shape = [
         jax.ShapeDtypeStruct((line, CORES * spec.shape[0], width), BF16),
         jax.ShapeDtypeStruct((2 * count, 2, rows, width), BF16),
         jax.ShapeDtypeStruct((2, rows, width), BF16),
-        jax.ShapeDtypeStruct((2, block, width), F32),
         jax.ShapeDtypeStruct((line, CORES) + ar.shape, BF16),
         jax.ShapeDtypeStruct((8, width), F32),
-    ] + [jax.ShapeDtypeStruct((seq_count, line, CORES) + x.shape, BF16) for x in wide]
+        jax.ShapeDtypeStruct((2 * block, width), BF16),
+        jax.ShapeDtypeStruct((2 * block, hidden_units), BF16),
+        jax.ShapeDtypeStruct((2 * block, hidden_units), BF16),
+        jax.ShapeDtypeStruct((2 * block, hidden_units), BF16),
+        jax.ShapeDtypeStruct((2, block, width), F32),
+        jax.ShapeDtypeStruct((2, rows, width), BF16),
+        jax.ShapeDtypeStruct((8, width), F32),
+        jax.ShapeDtypeStruct((2, block, width), F32),
+    ]
     scratch = [
-        pltpu.VMEM((2, rows, width), BF16),
-        pltpu.VMEM((2, rows, 2 * width), BF16),
-        pltpu.VMEM((2, rows, width), F32),
-        pltpu.VMEM((2, rows, width), BF16),
-        pltpu.VMEM((seq_count - 1, 2, block, width), BF16),
-        pltpu.VMEM((line, CORES * spec.shape[0], width), BF16),
-        pltpu.VMEM((2 * count, 2, rows, width), BF16),
+        vmem((2, rows, width), BF16),
+        vmem((2, rows, 2 * width), BF16),
+        vmem((2, rows, width), F32),
+        vmem((2, rows, width), BF16),
+        vmem((seq_count - 1, 2, block, width), BF16),
+        vmem((line, CORES * spec.shape[0], width), BF16),
+        vmem((2 * count, 2, rows, width), BF16),
+        vmem((2, rows, rows), BF16),
+        vmem((2 * block, width), F32),
+        vmem((2 * block, width), F32),
+        vmem((2, block, width), BF16),
     ]
-    scratch += [pltpu.VMEM(x.shape, BF16) for x in wide]
+    scratch += [vmem((seq_count, line, CORES) + x.shape, BF16) for x in wide]
     scratch += [
-        pltpu.VMEM(small, BF16),
-        pltpu.VMEM((seq_count - 1,) + small, BF16),
-        pltpu.VMEM(small, BF16),
-        pltpu.VMEM((line - 1,) + small, BF16),
-        pltpu.VMEM(small, BF16),
-        pltpu.VMEM(small, BF16),
-        DMA((5,)),
-        DMA((3,)),
+        vmem(small, BF16),
+        vmem((seq_count - 1,) + small, BF16),
+        vmem(small, BF16),
+        vmem((line - 1,) + small, BF16),
+        vmem(small, BF16),
+        vmem(small, BF16),
+        DMA((6,)),
         DMA((count,)),
         DMA((line,)),
         DMA((seq_count - 1,)),
         DMA((seq_count - 1,)),
         DMA((seq_count - 1,)),
         DMA((seq_count - 1,)),
-        DMA((2, line - 1)),
-        DMA((2, line - 1)),
+        DMA((2, 2, line - 1)),
+        DMA((2, 2, line - 1)),
         DMA((4, 2, line - 1)),
         DMA((4, 2, line - 1)),
-        DMA((line,)),
-        DMA((line,)),
-        DMA((3, seq_count - 1)),
-        DMA((3, seq_count - 1)),
+        DMA((2, line)),
+        DMA((2, line)),
+        DMA((3, line, seq_count - 1)),
+        DMA((3, line, seq_count - 1)),
         DMA((4, seq_count)),
         DMA((4, seq_count)),
         DMA((seq_count + line,)),
         DMA((seq_count + line,)),
+        DMA((seq_count - 1,)),
+        DMA((seq_count - 1,)),
     ]
     return pl.pallas_call(
-        functools.partial(mix_front_kernel, seq_count, line, spans),
+        functools.partial(mix_front_kernel, seq_count, line),
         out_shape=out_shape,
-        in_specs=[WHOLE] * 3 + [ANY] * 5,
-        out_specs=[ANY] * 2 + [WHOLE] * 4 + [ANY] * 3,
+        in_specs=[pl.BlockSpec(memory_space=pltpu.SMEM)] + [WHOLE] * 4 + [ANY] * 5,
+        out_specs=[ANY] * 2 + [WHOLE] * 11,
         scratch_shapes=scratch,
         compiler_params=params(7),
         name="mix_front",
-    )(tok, table, gain, spec, ar, *wide)
+    )(layout, tok, table, gain, cot, spec, ar, *wide)
 
 
 def body(
@@ -1472,48 +1588,77 @@
     hidden_units = w_gate.shape[1]
     spans = (rows, rows // 4)
 
-    swap = layout[0, 0] == 1
-    own = jnp.where(swap, tokens[::-1, 0], tokens[:, 0])
-    cotangent = jnp.where(swap, out_grad[::-1, 0], out_grad[:, 0])
     share = gain_mix.shape[0]
     ar_rows = ar_proj.shape[0] * CORES * line
     mine = lax.dynamic_slice(filters.T, (s * count, 0), (count, rows))[:, None, :]
     nothing = jnp.zeros((count, 1, rows), F32)
     back_table = jnp.concatenate([mine, nothing], axis=2)
     aligned = share % 16 == 0 and ar_proj.shape[0] % 16 == 0 and 2 * count % line == 0
-    aligned = aligned and ar_rows % 128 == 0
+    aligned = aligned and ar_rows % 128 == 0 and line > 2
 
     if aligned:
         gains = jnp.pad(jnp.stack([gain_mix, gain_mlp]), ((0, 14), (0, width - share)))
-        spec, ul, u, mixer, ar, gains, gate_w, up_w, down_w = mix_front(
+        own = tokens[:, 0]
+        cot = out_grad.reshape(2 * block, width)
+        spec, ul, u, ar, gains, mlp_in, gate_back, up_back, mixed, dh, dy, mlp_grad, out = mix_front(
             seq_count,
             line,
-            spans,
+            layout,
             own,
             back_table,
             gains.astype(F32),
+            cot,
             spectral_proj,
             ar_proj,
             (w_gate, w_up, w_down),
         )
-        mix_scale, mlp_scale = gains[0:1], gains[1:2]
-        mixer = mixer.reshape(2 * block, width)
-    else:
-        gains = jnp.zeros((16, 128), BF16)
-        gains = gains.at[0, :share].set(gain_mix).at[1, :share].set(gain_mlp)
-        x_all, spec, ar, gate_w, up_w, down_w, gains = gather_all(
-            seq_count, line, own, (spectral_proj, ar_proj), (w_gate, w_up, w_down, gains)
+        input_grad, dw, dar, gate_grad, up_grad, down_grad, small = mix_back(
+            seq_count,
+            line,
+            layout,
+            dy,
+            u,
+            back_table,
+            spec.reshape(count, 2, width, width),
+            ul,
+            ar.reshape(ar_rows, width),
+            own,
+            dh,
+            gains[0:1],
+            (mlp_in, gate_back, up_back, mixed, cot),
+            mlp_grad,
+            (share, w_down.shape[0], spectral_proj.shape[0], ar_proj.shape[0]),
         )
-        ar_full = lax.dynamic_update_slice(
-            jnp.zeros((3 * width, width), BF16), ar.reshape(ar_rows, width), (s * ar_rows, 0)
+        return (
+            out.reshape(tokens.shape),
+            input_grad.reshape(tokens.shape),
+            small[0, :share],
+            dw,
+            dar,
+            small[1, :share],
+            gate_grad,
+            up_grad,
+            down_grad,
         )
-        gains = gains.reshape(-1, 16, 128).astype(F32)
-        mix_scale = gains[:, 0, :share].reshape(1, width)
-        mlp_scale = gains[:, 1, :share].reshape(1, width)
-        fore_table = jnp.concatenate([mine[:, :, :1], nothing, mine[:, :, :0:-1]], axis=2)
-        split = spec.reshape(count, 2, width, width)
-        ul, u, y = forward_mix(spans, x_all, mix_scale, fore_table, split, ar_full)
-        mixer = side_sum(seq_count, line, y, 3).reshape(2 * block, width)
+
+    swap = layout[0, 0] == 1
+    own = jnp.where(swap, tokens[::-1, 0], tokens[:, 0])
+    cotangent = jnp.where(swap, out_grad[::-1, 0], out_grad[:, 0])
+    gains = jnp.zeros((16, 128), BF16)
+    gains = gains.at[0, :share].set(gain_mix).at[1, :share].set(gain_mlp)
+    x_all, spec, ar, gate_w, up_w, down_w, gains = gather_all(
+        seq_count, line, own, (spectral_proj, ar_proj), (w_gate, w_up, w_down, gains)
+    )
+    ar_full = lax.dynamic_update_slice(
+        jnp.zeros((3 * width, width), BF16), ar.reshape(ar_rows, width), (s * ar_rows, 0)
+    )
+    gains = gains.reshape(-1, 16, 128).astype(F32)
+    mix_scale = gains[:, 0, :share].reshape(1, width)
+    mlp_scale = gains[:, 1, :share].reshape(1, width)
+    fore_table = jnp.concatenate([mine[:, :, :1], nothing, mine[:, :, :0:-1]], axis=2)
+    split = spec.reshape(count, 2, width, width)
+    ul, u, y = forward_mix(spans, x_all, mix_scale, fore_table, split, ar_full)
+    mixer = side_sum(seq_count, line, y, 3).reshape(2 * block, width)
     spec = spec.reshape(count, 2, width, width)
     gate_w = gate_w.reshape(width, hidden_units)
     up_w = up_w.reshape(width, hidden_units)
@@ -1543,49 +1688,30 @@
     )
     mixer_grad = hidden_grad.astype(BF16)
 
-    if aligned:
-        input_grad, dw, dar, gate_grad, up_grad, down_grad, small = mix_back(
-            seq_count,
-            line,
-            spans,
-            mixer_grad.reshape(2, block, width),
-            u,
-            back_table,
-            spec,
-            ul,
-            ar.reshape(ar_rows, width),
-            own,
-            hidden_grad.reshape(2, block, width),
-            mix_scale,
-            (mlp_in, gate_back, up_back, mixed, cot),
-            mlp_grad,
-            (share, w_down.shape[0], spectral_proj.shape[0], ar_proj.shape[0]),
-        )
-    else:
-        down_grad = dot_tn(mixed, cot)
-        gate_grad = dot_tn(mlp_in, gate_back)
-        up_grad = dot_tn(mlp_in, up_back)
-        dy = side_gather(seq_count, line, mixer_grad.reshape(2, block, width))
-        dw, dar, du = backward_mix(spans, dy, u, back_table, spec, ul, ar_full)
-        normed_grad = side_sum(seq_count, line, du, 4).reshape(2 * block, width)
-
-        inv_one = lax.rsqrt(jnp.mean(inputs * inputs, axis=-1, keepdims=True) + EPSILON)
-        scaled_one = normed_grad * mix_scale
-        mix_grad = jnp.sum(normed_grad * inputs * inv_one, axis=0, keepdims=True)
-        input_grad = (
-            hidden_grad
-            + inv_one * scaled_one
-            - inputs * inv_one**3 * jnp.mean(scaled_one * inputs, axis=-1, keepdims=True)
-        )
-
-        dar = lax.dynamic_slice(dar, (s * ar_rows, 0), (ar_rows, width))
-        deep = (dw.reshape(line, CORES, -1, width), dar.reshape(line, CORES, -1, width))
-        wide = tuple(
-            x.astype(BF16).reshape(seq_count, line, CORES, -1, x.shape[1])
-            for x in (gate_grad, up_grad, down_grad)
-        )
-        small = jnp.concatenate([mix_grad, mlp_grad, jnp.zeros((6, width), F32)], axis=0)
-        dw, dar, gate_grad, up_grad, down_grad, small = sum_all(seq_count, line, deep, wide, small)
+    down_grad = dot_tn(mixed, cot)
+    gate_grad = dot_tn(mlp_in, gate_back)
+    up_grad = dot_tn(mlp_in, up_back)
+    dy = side_gather(seq_count, line, mixer_grad.reshape(2, block, width))
+    dw, dar, du = backward_mix(spans, dy, u, back_table, spec, ul, ar_full)
+    normed_grad = side_sum(seq_count, line, du, 4).reshape(2 * block, width)
+
+    inv_one = lax.rsqrt(jnp.mean(inputs * inputs, axis=-1, keepdims=True) + EPSILON)
+    scaled_one = normed_grad * mix_scale
+    mix_grad = jnp.sum(normed_grad * inputs * inv_one, axis=0, keepdims=True)
+    input_grad = (
+        hidden_grad
+        + inv_one * scaled_one
+        - inputs * inv_one**3 * jnp.mean(scaled_one * inputs, axis=-1, keepdims=True)
+    )
+
+    dar = lax.dynamic_slice(dar, (s * ar_rows, 0), (ar_rows, width))
+    deep = (dw.reshape(line, CORES, -1, width), dar.reshape(line, CORES, -1, width))
+    wide = tuple(
+        x.astype(BF16).reshape(seq_count, line, CORES, -1, x.shape[1])
+        for x in (gate_grad, up_grad, down_grad)
+    )
+    small = jnp.concatenate([mix_grad, mlp_grad, jnp.zeros((6, width), F32)], axis=0)
+    dw, dar, gate_grad, up_grad, down_grad, small = sum_all(seq_count, line, deep, wide, small)
     small = lax.dynamic_slice(small, (0, (s * CORES * line + g) * share), (2, share))
 
     def settle(x):

time: 230 us -> 221 us (0.961)
  matrix products: 10.8 us -> 0 us
  other arithmetic: 10.7 us -> 1.29 us
  local copies, waits for them, and re-layouts: 9.64 us -> 16.1 us
  Pallas kernels: 197 us -> 203 us
    dot_general x6 -> x0, matrix products: 10.8 us -> none  [the longest x3 5.57 us: dot_nn(): lax.dot_general(a, b, (((1,), (0,)), ((), ())), preferred_element_type=F32)]
    unnamed x35 -> x12, local copies, waits for them, and re-layouts: 6.34 us -> 12.9 us
    pallas_call x2, Pallas kernels: 197 us -> 203 us  [the longest x1 114 us: mix_front(): pl.pallas_call(functools.partial(mix_front_kernel, seq_count, line), out_...]
    convert_element_type x3 -> x0, other arithmetic: 3.1 us -> none  [the longest x2 2 us: body(): mlp_in = (hidden * inv_two * mlp_scale).astype(BF16)]
    unnamed x2 -> x0, other arithmetic: 2.91 us -> none
where the time goes in v4:
time: 221 us
  Pallas kernels  203 us (92%)
  local copies, waits for them, and re-layouts  16.1 us (7%)
    pallas_call x1, Pallas kernels, mix_front(): pl.pallas_call(functools.partial(mix_front_kernel, seq_count, line), out_...  114 us
    pallas_call x1, Pallas kernels, mix_back(): pl.pallas_call(functools.partial(mix_back_kernel, seq_count, line), out_s...  89 us
    unnamed x12, local copies, waits for them, and re-layouts  12.9 us

profile of v4, /device:TPU:0, one launch (start us, length us, event | category | flops | bytes accessed | tf_op | source)
XLA Modules:
  0.0 220.9 jit_solution(8159023792876861088)
XLA Ops:
  0.6 0.0 copy-start
  0.7 1.3 copy.20.refs_0_
  2.0 0.0 copy-done
  2.0 0.6 concatenate.3.refs_2_.refs_3_
  2.6 1.3 fusion.6.refs_3_
  3.9 113.9 %mix_front.1 = (bf16[4,1536,512]{2,1,0:T(8,128)(2,1)}, bf16[12,2,512,512]{3,2,1,0:T(8,128)(2,1)}, bf16[2,512,512]{2,1,0:T(8,128)(2,1)}, bf16[4,2,48,512]{3,2,1,0...) custom-call(s32[2,1]{1,0:T(2,128)} %copy.20.refs_0_, ...), custom_call_target="tpu_custom_call" | custom-call | tf_op jit(solution)/shard_map/mix_front/pallas_call | solution.py:1557
  117.8 1.3 slice.9.refs_9_
  119.1 0.0 copy-start.1
  119.1 89.0 %mix_back.1 = (f32[2,128,512]{2,1,0:T(8,128)}, f32[768,512]{1,0:T(8,128)}, f32[48,512]{1,0:T(8,128)}, f32[16,2048]{1,0:T(8,128)}, f32[16,2048]{1,0:T(8,128)}, /*index=5*/f32[64,512]{1,0:T(8,128)}, f32[8,512]{1,0:T(8,128)}) custom-call(s32[2,1]{1,0:T(2,128)} %copy.20.refs_0_, bf16[2,512,512]{2,1,0:T(8,128)(2,1)} %get-tuple-element.30.refs_1_, ...), custom_call_target="tpu_custom_call" | custom-call | tf_op jit(solution)/shard_map/mix_back/pallas_call | solution.py:1079
  208.1 1.3 slice_bitcast_fusion
  209.3 0.0 copy-done.1
  209.3 0.8 copy.31
  210.1 1.9 copy.32
  212.0 2.7 %copy.33 = f32[768,512]{1,0:T(8,128)} copy(f32[768,512]{1,0:T(8,128)} %get-tuple-element.72) | data formatting | bytes 3145728
  214.7 1.5 copy.34
  216.2 1.6 copy.35
  217.8 1.6 copy.36
  219.3 1.6 copy.37
  (2 shorter events, 0.0 us)
Async XLA Ops:
  0.6 1.3 copy-start
  119.1 90.2 %copy-start.1 = (f32[2,128,512]{2,1,0:T(8,128)S(1)}, f32[2,128,512]{2,1,0:T(8,128)}, u32[]{:S(2)}) copy-start(f32[2,128,512]{2,1,0:T(8,128)} %get-tuple-element.29) | copy-start | bytes 1572868

commit v5 on v4

--- a/solution.py
+++ b/solution.py
@@ -692,18 +692,19 @@
 
 
 def mix_back_kernel(seq_count, line, *refs):
-    (layout_ref, dy, u_ref, row_ref, w_hbm, ul_hbm, ar_ref, x_ref, hg_ref, scale_ref) = refs[:10]
-    (z_ref, gb_ref, ub_ref, mixed_ref, cot_ref, mlp_ref) = refs[10:16]
+    (layout_ref, row_ref, ar_ref, x_ref, scale_ref, cot_ref, mlp_ref, w_hbm, ul_hbm) = refs[:9]
+    large = refs[9:16]
     (tg_ref, dw_ref, dar_ref, gg_ref, ug_ref, dg_ref, small_ref) = refs[16:23]
     (keep, dsig, acc, conv, du_in, ul_buf, w_buf, dar) = refs[23:31]
     (deep, deep_in, deep_run, wide, wide_in, wide_side, wide_run) = refs[31:38]
     (g_own, g_pair, g_side, g_sum, g_line) = refs[38:43]
-    (load_sem, dus, dur, ps, pr, zs, zr, wps, wpr, ws, wr, wzs, wzr, gs, gr) = refs[43:]
+    (dy, u_ref, z_ref, gb_ref, ub_ref, mixed_ref, hg_ref) = held = refs[43:50]
+    (load_sem, dus, dur, ps, pr, zs, zr, wps, wpr, ws, wr, wzs, wzr, gs, gr) = refs[50:]
     s, z, c, g = place(seq_count, line)
     twin = {"grp": g + 1 - 2 * c}
     rows, width = dy.shape[1], dy.shape[2]
     block = x_ref.shape[1]
-    short = [layout_ref[m, 0].astype(F32) for m in range(2)]
+    short = [layout_ref[0, m].astype(F32) for m in range(2)]
     count = w_hbm.shape[0]
     per_chip = 2 * count // line
     n = per_chip * width // CORES
@@ -724,10 +725,9 @@
         )
 
     load_w = pltpu.make_async_copy(w_hbm, w_buf, load_sem.at[2])
-    load(0).start()
-    if line > 1:
-        load(1).start()
-    load_w.start()
+    fetch = [pltpu.make_async_copy(large[i], held[i], load_sem.at[3 + i]) for i in range(7)]
+    for x in fetch[:2] + [load(0), load(1)] + fetch[2:] + [load_w]:
+        x.start()
     greet(seq_count, line, s, z, c, g, twin=True, side=True, whole_line=True)
 
     def ar_place(i):
@@ -736,6 +736,8 @@
         col = lax.rem(at, width // lanes)
         return lag, pl.ds(pl.multiple_of(col * lanes, lanes), lanes)
 
+    for x in fetch[:2]:
+        x.wait()
     for i in range(ar_chunks):
         lag, cols = ar_place(i)
         total = 0.0
@@ -815,6 +817,8 @@
 
     span_f = gb_ref.shape[1] // seq_count
     down_share = dg_ref.shape[0]
+    for x in fetch[2:]:
+        x.wait()
 
     @pl.loop(0, seq_count)
     def _(j):
@@ -863,7 +867,7 @@
     signs = signs_of(rows)
     for m in range(2):
         dsig[m] = (dy[m].astype(F32) * signs).astype(BF16)
-        keep[m] = same_quarter(rows, short[m])
+        keep[m] = reach(rows, short[m])
     acc[...] = jnp.zeros_like(acc)
     for i in range(ar_chunks):
         lag, cols = ar_place(i)
@@ -873,7 +877,7 @@
     load_w.wait()
 
     def filter_step(k):
-        table = spread(row_ref[k], rows)
+        table = shifted(row_ref[pl.ds(s * count + k, 1), :], rows)
         for m in range(2):
             kept_table = table * keep[m]
             conv[0] = dot_nn(kept_table, dy[m]).astype(BF16)
@@ -911,7 +915,7 @@
             grad = grad + du_in[i, m].astype(F32)
         x = x_ref[m].astype(F32)
         inv = lax.rsqrt(jnp.mean(x * x, axis=-1, keepdims=True) + EPSILON)
-        scaled = grad * scale_ref[...]
+        scaled = grad * scale_ref[0:1, :]
         gain = gain + jnp.sum(grad * x * inv, axis=0, keepdims=True)
         centre = jnp.mean(scaled * x, axis=-1, keepdims=True)
         tg_ref[m] = hg_ref[m] + inv * scaled - x * (inv * inv * inv) * centre
@@ -1019,7 +1023,9 @@
                     hop(*kind, way, t, False).wait_send()
 
 
-def mix_back(seq_count, line, layout, dy, u, table, w, ul, ar, x, hg, scale, mlp, mlp_grad, shares):
+def mix_back(
+    seq_count, line, layout, dy, u, filters, w, ul, ar, x, hg, scale, mlp, mlp_grad, shares
+):
     z, gate_back, up_back, mixed, cot = mlp
     share, down_share, deep_share, ar_share = shares
     _, block, width = x.shape
@@ -1060,7 +1066,11 @@
         pltpu.VMEM((seq_count - 1,) + small, F32),
         pltpu.VMEM(small, F32),
         pltpu.VMEM((line - 1,) + small, F32),
-        DMA((3,)),
+    ]
+    large = [dy, u, z, gate_back, up_back, mixed, hg]
+    scratch += [pltpu.VMEM(v.shape, v.dtype) for v in large]
+    scratch += [
+        DMA((10,)),
         DMA((seq_count - 1,)),
         DMA((seq_count - 1,)),
         DMA((line,)),
@@ -1079,12 +1089,12 @@
     return pl.pallas_call(
         functools.partial(mix_back_kernel, seq_count, line),
         out_shape=out_shape,
-        in_specs=[pl.BlockSpec(memory_space=pltpu.SMEM)] + [WHOLE] * 3 + [ANY] * 2 + [WHOLE] * 10,
+        in_specs=[pl.BlockSpec(memory_space=pltpu.SMEM)] + [WHOLE] * 6 + [ANY] * 9,
         out_specs=[WHOLE] * 7,
         scratch_shapes=scratch,
         compiler_params=params(6),
         name="mix_back",
-    )(layout, dy, u, table, w, ul, ar, x, hg, scale, z, gate_back, up_back, mixed, cot, mlp_grad)
+    )(layout, filters, ar, x, scale, cot, mlp_grad, w, ul, *large)
 
 
 def kept(rows, short, lag):
@@ -1107,22 +1117,31 @@
     return jnp.where(lag == 0, values, jnp.where(lag == 1, one, two))
 
 
-def same_quarter(rows, short):
-    down = lax.div(lax.broadcasted_iota(jnp.int32, (rows, rows), 0), rows // 4)
-    over = lax.div(lax.broadcasted_iota(jnp.int32, (rows, rows), 1), rows // 4)
-    return (1.0 - short * (1.0 - (down == over).astype(F32))).astype(BF16)
+def reach(rows, short):
+    down = lax.broadcasted_iota(jnp.int32, (rows, rows), 0)
+    over = lax.broadcasted_iota(jnp.int32, (rows, rows), 1)
+    same = (lax.div(down, rows // 4) == lax.div(over, rows // 4)).astype(F32)
+    return ((over >= down).astype(F32) * (1.0 - short * (1.0 - same))).astype(BF16)
+
+
+def shifted(row, rows):
+    wide = jnp.broadcast_to(row, (rows, rows))
+    return pltpu.roll(wide, 0, 1, stride=1, stride_axis=0).astype(BF16)
 
 
 def mix_front_kernel(seq_count, line, *refs):
-    (layout_ref, tok_ref, row_ref, gain_ref, cot_ref, spec_hbm, ar_hbm) = refs[:7]
-    wide_in = refs[7:10]
-    (w_hbm, ul_hbm, u_ref, ar_ref, gain_out) = refs[10:15]
-    (z_ref, gb_ref, ub_ref, mixed_ref, hg_ref, dy_ref, mlp_ref, out_ref) = refs[15:23]
-    (x_all, both, acc, y_bf, y_in, w_buf, ul_buf, keep, hid, dz, dy_own) = refs[23:34]
-    wide_buf = refs[34:37]
-    (g_own, g_side, g_sum, g_line, g_all, g_twin) = refs[37:43]
-    (load_sem, ul_sem, w_sem, ts, tr, ys, yr, zs, zr, hs, hr) = refs[43:54]
-    (ps, pr, ws, wr, wps, wpr, gs, gr, ds_, dr_) = refs[54:]
+    (layout_ref, tok_ref, row_ref, mix_gain, mlp_gain, cot_ref, spec_hbm, ar_hbm) = refs[:8]
+    wide_in = refs[8:11]
+    (w_hbm, ul_hbm, u_hbm) = refs[11:14]
+    results = refs[14:20]
+    dy_hbm = refs[20]
+    (ar_ref, gain_out, mlp_ref) = refs[21:24]
+    (x_all, both, acc, y_bf, y_in, w_buf, ul_buf, keep, hid, dz, dy_own) = refs[24:35]
+    (z_ref, gb_ref, ub_ref, mixed_ref, hg_ref, out_ref) = local = refs[35:41]
+    wide_buf = refs[41:44]
+    (g_pad, g_own, g_side, g_sum, g_line, g_all, g_twin) = refs[44:51]
+    (load_sem, ul_sem, w_sem, ts, tr, ys, yr, zs, zr, hs, hr) = refs[51:62]
+    (ps, pr, ws, wr, wps, wpr, gs, gr, ds_, dr_, end_sem) = refs[62:]
     s, z, c, g = place(seq_count, line)
     twin = {"grp": g + 1 - 2 * c}
     rows, width = x_all.shape[1], x_all.shape[2]
@@ -1135,7 +1154,7 @@
     lanes = 128
     wide = range(3)
     mine = pl.ds(pl.multiple_of(s * block, block), block)
-    short = [layout_ref[m, 0].astype(F32) for m in range(2)]
+    short = [layout_ref[0, m].astype(F32) for m in range(2)]
 
     def piece(l, h):
         return w_buf.at[l, pl.ds(pl.multiple_of(c * n + h * hn, hn), hn), :]
@@ -1152,7 +1171,10 @@
     for x in load_w + [load_ar] + loads:
         x.start()
     at = (s * (CORES * line) + g) * (width // (seq_count * CORES * line))
-    g_own[...] = pltpu.roll(gain_ref[...], at, 1).astype(BF16)
+    g_pad[...] = jnp.zeros_like(g_pad)
+    g_pad[0:1, : mix_gain.shape[1]] = mix_gain[...].astype(F32)
+    g_pad[1:2, : mlp_gain.shape[1]] = mlp_gain[...].astype(F32)
+    g_own[...] = pltpu.roll(g_pad[...], at, 1).astype(BF16)
     greet(seq_count, line, s, z, c, g, twin=True, side=True, whole_line=True)
 
     gain_sides = []
@@ -1269,7 +1291,7 @@
     for x in loads + [load_ar]:
         x.wait()
     for m in range(2):
-        keep[m] = same_quarter(rows, short[m])
+        keep[m] = reach(rows, short[m])
     arrive(early_hops, 0, begin_sides)
     first(deep_hops(1))
     total = g_sum[...]
@@ -1291,16 +1313,17 @@
         x = x_all[m].astype(F32)
         inv = lax.rsqrt(jnp.mean(x * x, axis=-1, keepdims=True) + EPSILON)
         u = (x * inv * gain[0:1, :]).astype(BF16)
-        u_ref[m] = u
         both[m, :, :width] = u
         both[m, :, width:] = (u.astype(F32) * signs).astype(BF16)
+    u_store = pltpu.make_async_copy(both.at[:, :, pl.ds(0, width)], u_hbm, end_sem.at[0])
+    u_store.start()
 
     def ul_store(k):
         part = pl.ds(2 * k, 2)
         return pltpu.make_async_copy(ul_buf.at[part], ul_hbm.at[part], ul_sem.at[k])
 
     def filter_step(k):
-        table = spread(row_ref[k], rows)
+        table = shifted(row_ref[pl.ds(s * count + k, 1), :], rows)
         for m in range(2):
             val = dot_tn(table * keep[m], both[m])
             ul_buf[2 * k, m] = val[:, :width].astype(BF16)
@@ -1370,7 +1393,7 @@
         col = lax.rem(place_at, width // lanes)
         cols = pl.ds(pl.multiple_of(col * lanes, lanes), lanes)
         for m in range(2):
-            v = lagged_by(u_ref[m, :, cols].astype(F32), lag, short[m]).astype(BF16)
+            v = lagged_by(both[m, :, cols].astype(F32), lag, short[m]).astype(BF16)
             acc[m] += dot_nn(v, ar_all[i * lanes : (i + 1) * lanes])
 
     def twin_wide(i, k):
@@ -1474,25 +1497,33 @@
     dy_copies = []
     for i in range(1, seq_count):
         to = {"seq": lax.rem(s + i, seq_count)}
-        dy_copies.append(remote(dy_own, dy_ref.at[:, mine, :], ds_.at[i - 1], dr_.at[i - 1], to))
+        dy_copies.append(remote(dy_own, dy_hbm.at[:, mine, :], ds_.at[i - 1], dr_.at[i - 1], to))
         dy_copies[-1].start()
-    dy_ref[:, mine, :] = dy_own[...]
+    ends = [pltpu.make_async_copy(dy_own, dy_hbm.at[:, mine, :], end_sem.at[1])]
+    ends += [
+        pltpu.make_async_copy(local[i], results[i], end_sem.at[2 + i]) for i in range(6)
+    ]
+    for x in ends[:6]:
+        x.start()
     total = hid[...]
     for j in range(seq_count):
         down_w = wide_buf[2][j].reshape(step, width)
         total = total + dot_nn(mixed_ref[:, j * step : (j + 1) * step], down_w)
     for m in range(2):
         out_ref[m] = total[m * block : (m + 1) * block]
+    ends[6].start()
     for x in y_copies:
         x.wait_send()
+    for x in ends + [u_store]:
+        x.wait()
     for x in dy_copies:
         x.wait()
 
 
-def mix_front(seq_count, line, layout, tok, table, gain, cot, spec, ar, wide):
+def mix_front(seq_count, line, layout, tok, filters, gains, cot, spec, ar, wide):
     _, block, width = tok.shape
     rows = block * seq_count
-    count = table.shape[0]
+    count = filters.shape[0] // seq_count
     hidden_units = wide[0].shape[1]
     small = (16, width)
     vmem = pltpu.VMEM
@@ -1500,16 +1531,21 @@
         jax.ShapeDtypeStruct((line, CORES * spec.shape[0], width), BF16),
         jax.ShapeDtypeStruct((2 * count, 2, rows, width), BF16),
         jax.ShapeDtypeStruct((2, rows, width), BF16),
+    ]
+    local = [
+        ((2 * block, width), BF16),
+        ((2 * block, hidden_units), BF16),
+        ((2 * block, hidden_units), BF16),
+        ((2 * block, hidden_units), BF16),
+        ((2, block, width), F32),
+        ((2, block, width), F32),
+    ]
+    out_shape += [jax.ShapeDtypeStruct(*x) for x in local]
+    out_shape += [
+        jax.ShapeDtypeStruct((2, rows, width), BF16),
         jax.ShapeDtypeStruct((line, CORES) + ar.shape, BF16),
         jax.ShapeDtypeStruct((8, width), F32),
-        jax.ShapeDtypeStruct((2 * block, width), BF16),
-        jax.ShapeDtypeStruct((2 * block, hidden_units), BF16),
-        jax.ShapeDtypeStruct((2 * block, hidden_units), BF16),
-        jax.ShapeDtypeStruct((2 * block, hidden_units), BF16),
-        jax.ShapeDtypeStruct((2, block, width), F32),
-        jax.ShapeDtypeStruct((2, rows, width), BF16),
         jax.ShapeDtypeStruct((8, width), F32),
-        jax.ShapeDtypeStruct((2, block, width), F32),
     ]
     scratch = [
         vmem((2, rows, width), BF16),
@@ -1524,8 +1560,10 @@
         vmem((2 * block, width), F32),
         vmem((2, block, width), BF16),
     ]
+    scratch += [vmem(*x) for x in local]
     scratch += [vmem((seq_count, line, CORES) + x.shape, BF16) for x in wide]
     scratch += [
+        vmem(small, F32),
         vmem(small, BF16),
         vmem((seq_count - 1,) + small, BF16),
         vmem(small, BF16),
@@ -1553,16 +1591,48 @@
         DMA((seq_count + line,)),
         DMA((seq_count - 1,)),
         DMA((seq_count - 1,)),
+        DMA((8,)),
     ]
     return pl.pallas_call(
         functools.partial(mix_front_kernel, seq_count, line),
         out_shape=out_shape,
-        in_specs=[pl.BlockSpec(memory_space=pltpu.SMEM)] + [WHOLE] * 4 + [ANY] * 5,
-        out_specs=[ANY] * 2 + [WHOLE] * 11,
+        in_specs=[pl.BlockSpec(memory_space=pltpu.SMEM)] + [WHOLE] * 5 + [ANY] * 5,
+        out_specs=[ANY] * 10 + [WHOLE] * 3,
         scratch_shapes=scratch,
         compiler_params=params(7),
         name="mix_front",
-    )(layout, tok, table, gain, cot, spec, ar, *wide)
+    )(layout, tok, filters, *gains, cot, spec, ar, *wide)
+
+
+def finish_kernel(count, share, *refs):
+    ins, small = refs[:count], refs[count]
+    outs, first, second = refs[count + 1 : 2 * count + 1], refs[2 * count + 1], refs[2 * count + 2]
+    held, sem = refs[2 * count + 3 : 3 * count + 3], refs[3 * count + 3]
+    loads = [pltpu.make_async_copy(ins[i], held[i], sem.at[0, i]) for i in range(count)]
+    stores = [pltpu.make_async_copy(held[i], outs[i], sem.at[1, i]) for i in range(count)]
+    for x in loads:
+        x.start()
+    first[...] = small[0:1, :share]
+    second[...] = small[1:2, :share]
+    for x, y in zip(loads, stores):
+        x.wait()
+        y.start()
+    for x in stores:
+        x.wait()
+
+
+def finish(share, arrays, small):
+    count = len(arrays)
+    row = jax.ShapeDtypeStruct((1, share), F32)
+    return pl.pallas_call(
+        functools.partial(finish_kernel, count, share),
+        out_shape=[jax.ShapeDtypeStruct(x.shape, x.dtype) for x in arrays] + [row, row],
+        in_specs=[ANY] * count + [WHOLE],
+        out_specs=[ANY] * count + [WHOLE] * 2,
+        scratch_shapes=[pltpu.VMEM(x.shape, x.dtype) for x in arrays] + [DMA((2, count))],
+        compiler_params=params(),
+        name="finish",
+    )(*arrays, small)
 
 
 def body(
@@ -1597,16 +1667,16 @@
     aligned = aligned and ar_rows % 128 == 0 and line > 2
 
     if aligned:
-        gains = jnp.pad(jnp.stack([gain_mix, gain_mlp]), ((0, 14), (0, width - share)))
         own = tokens[:, 0]
         cot = out_grad.reshape(2 * block, width)
-        spec, ul, u, ar, gains, mlp_in, gate_back, up_back, mixed, dh, dy, mlp_grad, out = mix_front(
+        flags = layout.reshape(1, 2)
+        spec, ul, u, mlp_in, gate_back, up_back, mixed, dh, out, dy, ar, gains, mlp_grad = mix_front(
             seq_count,
             line,
-            layout,
+            flags,
             own,
-            back_table,
-            gains.astype(F32),
+            filters.T,
+            (gain_mix.reshape(1, share), gain_mlp.reshape(1, share)),
             cot,
             spectral_proj,
             ar_proj,
@@ -1615,27 +1685,30 @@
         input_grad, dw, dar, gate_grad, up_grad, down_grad, small = mix_back(
             seq_count,
             line,
-            layout,
+            flags,
             dy,
             u,
-            back_table,
+            filters.T,
             spec.reshape(count, 2, width, width),
             ul,
             ar.reshape(ar_rows, width),
             own,
             dh,
-            gains[0:1],
+            gains,
             (mlp_in, gate_back, up_back, mixed, cot),
             mlp_grad,
             (share, w_down.shape[0], spectral_proj.shape[0], ar_proj.shape[0]),
         )
+        dw, out, input_grad, down_grad, gate_grad, up_grad, dar, mix_grad, mlp_grad = finish(
+            share, (dw, out, input_grad, down_grad, gate_grad, up_grad, dar), small
+        )
         return (
             out.reshape(tokens.shape),
             input_grad.reshape(tokens.shape),
-            small[0, :share],
+            mix_grad.reshape(share),
             dw,
             dar,
-            small[1, :share],
+            mlp_grad.reshape(share),
             gate_grad,
             up_grad,
             down_grad,

time: 221 us -> 205 us (0.928)
  local copies, waits for them, and re-layouts: 16.1 us -> 0 us
    unnamed x12 -> x0, local copies, waits for them, and re-layouts: 12.9 us -> none
    pallas_call x0 -> x1, Pallas kernels: none -> 4.4 us  [finish(): pl.pallas_call(functools.partial(finish_kernel, count, share), out_shape=...]
where the time goes in v5:
time: 205 us
  Pallas kernels  204 us (100%)
    pallas_call x1, Pallas kernels, mix_front(): pl.pallas_call(functools.partial(mix_front_kernel, seq_count, line), out_...  112 us
    pallas_call x1, Pallas kernels, mix_back(): pl.pallas_call(functools.partial(mix_back_kernel, seq_count, line), out_s...  87.6 us
    pallas_call x1, Pallas kernels, finish(): pl.pallas_call(functools.partial(finish_kernel, count, share), out_shape=...  4.4 us

profile of v5, /device:TPU:0, one launch (start us, length us, event | category | flops | bytes accessed | tf_op | source)
XLA Modules:
  0.0 204.8 jit_solution(9983660063758943038)
XLA Ops:
  0.6 112.0 %mix_front.1 = (bf16[4,1536,512]{2,1,0:T(8,128)(2,1)}, bf16[12,2,512,512]{3,2,1,0:T(8,128)(2,1)}, bf16[2,512,512]{2,1,0:T(8,128)(2,1)}, bf16[256,512]{1,0:T(8,12...) custom-call(s32[1,2]{1,0:T(1,128)} %bitcast.24, ...), custom_call_target="tpu_custom_call" | custom-call | tf_op jit(solution)/shard_map/mix_front/pallas_call | solution.py:1596
  112.6 87.6 %mix_back.1 = (f32[2,128,512]{2,1,0:T(8,128)}, f32[768,512]{1,0:T(8,128)}, f32[48,512]{1,0:T(8,128)}, f32[16,2048]{1,0:T(8,128)}, f32[16,2048]{1,0:T(8,128)}, /*index=5*/f32[64,512]{1,0:T(8,128)}, f32[8,512]{1,0:T(8,128)}) custom-call(s32[1,2]{1,0:T(1,128)} %bitcast.25, f32[24,512]{1,0:T(8,128)} %bitcast.23, bf16[384,512]{1,0:T(8,128)(2,1)} %bitcast.21, ...), custom_call_target="tpu_custom_call" | custom-call | tf_op jit(solution)/shard_map/mix_back/pallas_call | solution.py:1089
  200.2 4.4 %finish.1 = (f32[768,512]{1,0:T(8,128)}, f32[2,128,512]{2,1,0:T(8,128)}, f32[2,128,512]{2,1,0:T(8,128)}, f32[64,512]{1,0:T(8,128)}, f32[16,2048]{1,0:T(8,128)}, ...) custom-call(f32[768,512]{1,0:T(8,128)} %get-tuple-element.50.refs_0_, ...), custom_call_target="tpu_custom_call" | custom-call | tf_op jit(solution)/shard_map/finish/pallas_call | solution.py:1627

commit v6 on v5

--- a/solution.py
+++ b/solution.py
@@ -694,12 +694,15 @@
 def mix_back_kernel(seq_count, line, *refs):
     (layout_ref, row_ref, ar_ref, x_ref, scale_ref, cot_ref, mlp_ref, w_hbm, ul_hbm) = refs[:9]
     large = refs[9:16]
-    (tg_ref, dw_ref, dar_ref, gg_ref, ug_ref, dg_ref, small_ref) = refs[16:23]
+    (tg_hbm, dw_hbm, dar_ref, gg_ref, ug_ref, dg_ref, small_ref) = refs[16:23]
     (keep, dsig, acc, conv, du_in, ul_buf, w_buf, dar) = refs[23:31]
     (deep, deep_in, deep_run, wide, wide_in, wide_side, wide_run) = refs[31:38]
     (g_own, g_pair, g_side, g_sum, g_line) = refs[38:43]
     (dy, u_ref, z_ref, gb_ref, ub_ref, mixed_ref, hg_ref) = held = refs[43:50]
-    (load_sem, dus, dur, ps, pr, zs, zr, wps, wpr, ws, wr, wzs, wzr, gs, gr) = refs[50:]
+    (tg_ref, dw_ref, end_sem) = refs[50:53]
+    (load_sem, dus, dur, ps, pr, zs, zr, wps, wpr, ws, wr, wzs, wzr, gs, gr) = refs[53:]
+    tg_store = pltpu.make_async_copy(tg_ref, tg_hbm, end_sem.at[0])
+    dw_store = pltpu.make_async_copy(dw_ref, dw_hbm, end_sem.at[1])
     s, z, c, g = place(seq_count, line)
     twin = {"grp": g + 1 - 2 * c}
     rows, width = dy.shape[1], dy.shape[2]
@@ -919,6 +922,7 @@
         gain = gain + jnp.sum(grad * x * inv, axis=0, keepdims=True)
         centre = jnp.mean(scaled * x, axis=-1, keepdims=True)
         tg_ref[m] = hg_ref[m] + inv * scaled - x * (inv * inv * inv) * centre
+    tg_store.start()
     g_own[...] = jnp.zeros_like(g_own)
     g_own[0:1, :] = gain
     g_own[1:2, :] = mlp_ref[0:1, :]
@@ -991,6 +995,7 @@
             dg_ref[q * share : (q + 1) * share, :] += val[2 * share :, q * width : (q + 1) * width]
 
     last(deep_line, add_deep)
+    dw_store.start()
     for phase in range(1, line - 1):
         relay(wide_line, phase)
     own = wide_in[s, z].astype(F32)
@@ -1010,6 +1015,8 @@
 
     for x in sides + du_copies:
         x.wait_send()
+    tg_store.wait()
+    dw_store.wait()
     wide_twin.wait_send()
     for i in range(line):
         twin_deep(i).wait_send()
@@ -1069,7 +1076,9 @@
     ]
     large = [dy, u, z, gate_back, up_back, mixed, hg]
     scratch += [pltpu.VMEM(v.shape, v.dtype) for v in large]
+    scratch += [pltpu.VMEM(v.shape, F32) for v in out_shape[:2]]
     scratch += [
+        DMA((2,)),
         DMA((10,)),
         DMA((seq_count - 1,)),
         DMA((seq_count - 1,)),
@@ -1090,7 +1099,7 @@
         functools.partial(mix_back_kernel, seq_count, line),
         out_shape=out_shape,
         in_specs=[pl.BlockSpec(memory_space=pltpu.SMEM)] + [WHOLE] * 6 + [ANY] * 9,
-        out_specs=[WHOLE] * 7,
+        out_specs=[ANY] * 2 + [WHOLE] * 5,
         scratch_shapes=scratch,
         compiler_params=params(6),
         name="mix_back",
@@ -1330,19 +1339,20 @@
             ul_buf[2 * k + 1, m] = (val[:, width:] * signs).astype(BF16)
         ul_store(k).start()
 
+    def add_one(l, h, m):
+        total = 0.0
+        for cc in range(CORES):
+            lo, end = cc * n + h * hn, cc * n + (h + 1) * hn
+            while lo < end:
+                j = lo // width
+                hi = min(end, (j + 1) * width)
+                left = ul_buf[l * per_chip + j, m, :, lo - j * width : hi - j * width]
+                total = total + dot_nn(left, w_buf[l, lo:hi, :])
+                lo = hi
+        acc[m] += total
+
     def add_part(l, h):
-        @pl.loop(0, 2)
-        def _(m):
-            total = 0.0
-            for cc in range(CORES):
-                lo, end = cc * n + h * hn, cc * n + (h + 1) * hn
-                while lo < end:
-                    j = lo // width
-                    hi = min(end, (j + 1) * width)
-                    left = ul_buf[l * per_chip + j, m, :, lo - j * width : hi - j * width]
-                    total = total + dot_nn(left, w_buf[l, lo:hi, :])
-                    lo = hi
-            acc[m] += total
+        pl.loop(0, 2)(lambda m: add_one(l, h, m))
 
     def w_store(l):
         return pltpu.make_async_copy(w_buf.at[l], w_hbm.at[l], w_sem.at[l])
@@ -1411,22 +1421,35 @@
                     twin_wide(i, k).start()
         deep_add(t, 0)
         deep_arrive(t, 1)
-        deep_add(t, 1)
-
-    y_bf[...] = acc[...].astype(BF16)
+        if t < line - 2:
+            deep_add(t, 1)
+
     y_copies = []
-    for i in range(1, seq_count):
-        to = lax.rem(s + i, seq_count)
-        y_copies.append(
-            remote(
-                y_bf.at[:, pl.ds(pl.multiple_of(to * block, block), block), :],
-                y_in.at[i - 1],
-                ys.at[i - 1],
-                yr.at[i - 1],
-                {"seq": to},
+    for m in range(2):
+        for way in (0, 1):
+            _, receives, _, origin = line_conditions(line, z, way, line - 2)
+
+            @pl.when(receives)
+            def _():
+                if m == 0:
+                    twin_deep(origin, 1).wait_recv()
+                    w_store(origin).start()
+                add_one(origin, 1, m)
+
+        y_bf[m] = acc[m].astype(BF16)
+        y_copies.append([])
+        for i in range(1, seq_count):
+            to = lax.rem(s + i, seq_count)
+            y_copies[m].append(
+                remote(
+                    y_bf.at[m, pl.ds(pl.multiple_of(to * block, block), block), :],
+                    y_in.at[i - 1, m],
+                    ys.at[m, i - 1],
+                    yr.at[m, i - 1],
+                    {"seq": to},
+                )
             )
-        )
-        y_copies[-1].start()
+            y_copies[m][-1].start()
 
     for i in wide:
         for k in range(seq_count):
@@ -1445,76 +1468,77 @@
     for k in range(count):
         ul_store(k).wait()
 
-    for m in range(2):
-        part = slice(m * block, (m + 1) * block)
-        hid[part, :] = tok_ref[m].astype(F32) + acc[m, mine, :]
-    for i, x in enumerate(y_copies):
-        x.wait_recv()
-        for m in range(2):
-            hid[m * block : (m + 1) * block, :] += y_in[i, m].astype(F32)
-    h = hid[...]
-    inv_two = lax.rsqrt(jnp.mean(h * h, axis=-1, keepdims=True) + EPSILON)
     mlp_scale = gain[1:2, :]
-    z_ref[...] = (h * inv_two * mlp_scale).astype(BF16)
-    dz[...] = jnp.zeros_like(dz)
     hidden_units = gb_ref.shape[1]
     step = hidden_units // seq_count
     root = 0.7978845608028654
-
-    @pl.loop(0, seq_count)
-    def _(j):
-        part = pl.ds(pl.multiple_of(j * step, step), step)
-        gate_w = wide_buf[0][:, :, :, :, part].reshape(width, step)
-        up_w = wide_buf[1][:, :, :, :, part].reshape(width, step)
-        down_w = wide_buf[2][j].reshape(step, width)
-        gate = dot_nn(z_ref[...], gate_w)
-        up = dot_nn(z_ref[...], up_w)
-        back = dot_nt(cot_ref[...], down_w)
-        square = gate * gate
-        tan = jnp.tanh(root * (gate + 0.044715 * (square * gate)))
-        share = 0.5 * (1.0 + tan)
-        gelu = gate * share
-        slope = share + 0.5 * gate * (1.0 - tan * tan) * (
-            root * (1.0 + (3.0 * 0.044715) * square)
-        )
-        mixed_ref[:, part] = (gelu * up).astype(BF16)
-        gate_back = (back * up * slope).astype(BF16)
-        up_back = (back * gelu).astype(BF16)
-        gb_ref[:, part] = gate_back
-        ub_ref[:, part] = up_back
-        dz[...] += dot_nt(gate_back, gate_w) + dot_nt(up_back, up_w)
-    grad = dz[...]
-    h = hid[...]
-    scaled = grad * mlp_scale
-    centre = jnp.mean(scaled * h, axis=-1, keepdims=True)
-    dh = cot_ref[...].astype(F32) + inv_two * scaled - h * (inv_two * inv_two * inv_two) * centre
     mlp_ref[...] = jnp.zeros_like(mlp_ref)
-    mlp_ref[0:1, :] = jnp.sum(grad * h * inv_two, axis=0, keepdims=True)
+    dy_copies = []
+    ends = []
     for m in range(2):
-        part = slice(m * block, (m + 1) * block)
-        hg_ref[m] = dh[part]
-        dy_own[m] = dh[part].astype(BF16)
-    dy_copies = []
-    for i in range(1, seq_count):
-        to = {"seq": lax.rem(s + i, seq_count)}
-        dy_copies.append(remote(dy_own, dy_hbm.at[:, mine, :], ds_.at[i - 1], dr_.at[i - 1], to))
-        dy_copies[-1].start()
-    ends = [pltpu.make_async_copy(dy_own, dy_hbm.at[:, mine, :], end_sem.at[1])]
-    ends += [
-        pltpu.make_async_copy(local[i], results[i], end_sem.at[2 + i]) for i in range(6)
-    ]
-    for x in ends[:6]:
-        x.start()
+        own = slice(m * block, (m + 1) * block)
+        h = tok_ref[m].astype(F32) + acc[m, mine, :]
+        for i, x in enumerate(y_copies[m]):
+            x.wait_recv()
+            h = h + y_in[i, m].astype(F32)
+        hid[own, :] = h
+        inv_two = lax.rsqrt(jnp.mean(h * h, axis=-1, keepdims=True) + EPSILON)
+        z_ref[own, :] = (h * inv_two * mlp_scale).astype(BF16)
+        dz[...] = jnp.zeros_like(dz)
+
+        @pl.loop(0, seq_count)
+        def _(j):
+            part = pl.ds(pl.multiple_of(j * step, step), step)
+            gate_w = wide_buf[0][:, :, :, :, part].reshape(width, step)
+            up_w = wide_buf[1][:, :, :, :, part].reshape(width, step)
+            down_w = wide_buf[2][j].reshape(step, width)
+            gate = dot_nn(z_ref[own, :], gate_w)
+            up = dot_nn(z_ref[own, :], up_w)
+            back = dot_nt(cot_ref[own, :], down_w)
+            square = gate * gate
+            tan = jnp.tanh(root * (gate + 0.044715 * (square * gate)))
+            share = 0.5 * (1.0 + tan)
+            gelu = gate * share
+            slope = share + 0.5 * gate * (1.0 - tan * tan) * (
+                root * (1.0 + (3.0 * 0.044715) * square)
+            )
+            mixed_ref[own, part] = (gelu * up).astype(BF16)
+            gate_back = (back * up * slope).astype(BF16)
+            up_back = (back * gelu).astype(BF16)
+            gb_ref[own, part] = gate_back
+            ub_ref[own, part] = up_back
+            dz[...] += dot_nt(gate_back, gate_w) + dot_nt(up_back, up_w)
+
+        grad = dz[...]
+        h = hid[own, :]
+        scaled = grad * mlp_scale
+        centre = jnp.mean(scaled * h, axis=-1, keepdims=True)
+        cube = inv_two * inv_two * inv_two
+        dh = cot_ref[own, :].astype(F32) + inv_two * scaled - h * cube * centre
+        dy_own[m] = dh.astype(BF16)
+        for i in range(1, seq_count):
+            to = {"seq": lax.rem(s + i, seq_count)}
+            dst = dy_hbm.at[m, mine, :]
+            dy_copies.append(remote(dy_own.at[m], dst, ds_.at[m, i - 1], dr_.at[m, i - 1], to))
+            dy_copies[-1].start()
+        ends.append(pltpu.make_async_copy(dy_own.at[m], dy_hbm.at[m, mine, :], end_sem.at[7 + m]))
+        ends[-1].start()
+        hg_ref[m] = dh
+        mlp_ref[0:1, :] += jnp.sum(grad * h * inv_two, axis=0, keepdims=True)
+    for i in range(5):
+        ends.append(pltpu.make_async_copy(local[i], results[i], end_sem.at[1 + i]))
+        ends[-1].start()
+    last = pltpu.make_async_copy(local[5], results[5], end_sem.at[6])
     total = hid[...]
     for j in range(seq_count):
         down_w = wide_buf[2][j].reshape(step, width)
         total = total + dot_nn(mixed_ref[:, j * step : (j + 1) * step], down_w)
     for m in range(2):
         out_ref[m] = total[m * block : (m + 1) * block]
-    ends[6].start()
-    for x in y_copies:
+    last.start()
+    for x in y_copies[0] + y_copies[1]:
         x.wait_send()
-    for x in ends + [u_store]:
+    for x in ends + [last, u_store]:
         x.wait()
     for x in dy_copies:
         x.wait()
@@ -1557,7 +1581,7 @@
         vmem((2 * count, 2, rows, width), BF16),
         vmem((2, rows, rows), BF16),
         vmem((2 * block, width), F32),
-        vmem((2 * block, width), F32),
+        vmem((block, width), F32),
         vmem((2, block, width), BF16),
     ]
     scratch += [vmem(*x) for x in local]
@@ -1575,8 +1599,8 @@
         DMA((line,)),
         DMA((seq_count - 1,)),
         DMA((seq_count - 1,)),
-        DMA((seq_count - 1,)),
-        DMA((seq_count - 1,)),
+        DMA((2, seq_count - 1)),
+        DMA((2, seq_count - 1)),
         DMA((2, 2, line - 1)),
         DMA((2, 2, line - 1)),
         DMA((4, 2, line - 1)),
@@ -1589,9 +1613,9 @@
         DMA((4, seq_count)),
         DMA((seq_count + line,)),
         DMA((seq_count + line,)),
-        DMA((seq_count - 1,)),
-        DMA((seq_count - 1,)),
-        DMA((8,)),
+        DMA((2, seq_count - 1)),
+        DMA((2, seq_count - 1)),
+        DMA((9,)),
     ]
     return pl.pallas_call(
         functools.partial(mix_front_kernel, seq_count, line),

time: 205 us -> 196 us (0.956)
  Pallas kernels: 204 us -> 195 us
    pallas_call x1, Pallas kernels: 112 us -> 104 us  [mix_front(): pl.pallas_call(functools.partial(mix_front_kernel, seq_count, line), out_...]
where the time goes in v6:
time: 196 us
  Pallas kernels  195 us (99%)
    pallas_call x1, Pallas kernels, mix_front(): pl.pallas_call(functools.partial(mix_front_kernel, seq_count, line), out_...  104 us
    pallas_call x1, Pallas kernels, mix_back(): pl.pallas_call(functools.partial(mix_back_kernel, seq_count, line), out_s...  86.2 us
    pallas_call x1, Pallas kernels, finish(): pl.pallas_call(functools.partial(finish_kernel, count, share), out_shape=...  4.4 us

profile of v6, /device:TPU:0, one launch (start us, length us, event | category | flops | bytes accessed | tf_op | source)
XLA Modules:
  0.0 195.8 jit_solution(10722409595541518800)
XLA Ops:
  0.6 104.4 %mix_front.1 = (bf16[4,1536,512]{2,1,0:T(8,128)(2,1)}, bf16[12,2,512,512]{3,2,1,0:T(8,128)(2,1)}, bf16[2,512,512]{2,1,0:T(8,128)(2,1)}, bf16[256,512]{1,0:T(8,12...) custom-call(s32[1,2]{1,0:T(1,128)} %bitcast.24, ...), custom_call_target="tpu_custom_call" | custom-call | tf_op jit(solution)/shard_map/mix_front/pallas_call | solution.py:1620
  105.1 86.2 %mix_back.1 = (f32[2,128,512]{2,1,0:T(8,128)}, f32[768,512]{1,0:T(8,128)}, f32[48,512]{1,0:T(8,128)}, f32[16,2048]{1,0:T(8,128)}, f32[16,2048]{1,0:T(8,128)}, /*index=5*/f32[64,512]{1,0:T(8,128)}, f32[8,512]{1,0:T(8,128)}) custom-call(s32[1,2]{1,0:T(1,128)} %bitcast.25, f32[24,512]{1,0:T(8,128)} %bitcast.23, bf16[384,512]{1,0:T(8,128)(2,1)} %bitcast.21, ...), custom_call_target="tpu_custom_call" | custom-call | tf_op jit(solution)/shard_map/mix_back/pallas_call | solution.py:1098
  191.3 4.4 %finish.1 = (f32[768,512]{1,0:T(8,128)}, f32[2,128,512]{2,1,0:T(8,128)}, f32[2,128,512]{2,1,0:T(8,128)}, f32[64,512]{1,0:T(8,128)}, f32[16,2048]{1,0:T(8,128)}, ...) custom-call(f32[768,512]{1,0:T(8,128)} %get-tuple-element.50.refs_0_, ...), custom_call_target="tpu_custom_call" | custom-call | tf_op jit(solution)/shard_map/finish/pallas_call | solution.py:1651

commit v7 on v6

--- a/solution.py
+++ b/solution.py
@@ -692,15 +692,15 @@
 
 
 def mix_back_kernel(seq_count, line, *refs):
-    (layout_ref, row_ref, ar_ref, x_ref, scale_ref, cot_ref, mlp_ref, w_hbm, ul_hbm) = refs[:9]
-    large = refs[9:16]
-    (tg_hbm, dw_hbm, dar_ref, gg_ref, ug_ref, dg_ref, small_ref) = refs[16:23]
-    (keep, dsig, acc, conv, du_in, ul_buf, w_buf, dar) = refs[23:31]
-    (deep, deep_in, deep_run, wide, wide_in, wide_side, wide_run) = refs[31:38]
-    (g_own, g_pair, g_side, g_sum, g_line) = refs[38:43]
-    (dy, u_ref, z_ref, gb_ref, ub_ref, mixed_ref, hg_ref) = held = refs[43:50]
-    (tg_ref, dw_ref, end_sem) = refs[50:53]
-    (load_sem, dus, dur, ps, pr, zs, zr, wps, wpr, ws, wr, wzs, wzr, gs, gr) = refs[53:]
+    (layout_ref, row_ref, ar_ref, x_ref, scale_ref, mlp_ref, w_hbm, ul_hbm, wide_hbm) = refs[:9]
+    large = refs[9:12]
+    (tg_hbm, dw_hbm, dar_ref, gg_ref, ug_ref, dg_ref, small_ref) = refs[12:19]
+    (keep, dsig, acc, conv, du_in, ul_buf, w_buf, dar) = refs[19:27]
+    (deep, deep_in, deep_run, wide, wide_in, wide_side, wide_run) = refs[27:34]
+    (g_own, g_pair, g_side, g_sum, g_line) = refs[34:39]
+    (dy, u_ref, hg_ref) = held = refs[39:42]
+    (tg_ref, dw_ref, end_sem) = refs[42:45]
+    (load_sem, dus, dur, ps, pr, zs, zr, wps, wpr, ws, wr, wzs, wzr, gs, gr) = refs[45:]
     tg_store = pltpu.make_async_copy(tg_ref, tg_hbm, end_sem.at[0])
     dw_store = pltpu.make_async_copy(dw_ref, dw_hbm, end_sem.at[1])
     s, z, c, g = place(seq_count, line)
@@ -716,6 +716,8 @@
     lanes = 128
     ar_chunks = ar_rows // lanes
     share = gg_ref.shape[0]
+    hn = n // 2
+    down_share = dg_ref.shape[0]
     mine = pl.ds(pl.multiple_of(s * block, block), block)
     low = (z < line // 2).astype(jnp.int32)
 
@@ -728,8 +730,9 @@
         )
 
     load_w = pltpu.make_async_copy(w_hbm, w_buf, load_sem.at[2])
-    fetch = [pltpu.make_async_copy(large[i], held[i], load_sem.at[3 + i]) for i in range(7)]
-    for x in fetch[:2] + [load(0), load(1)] + fetch[2:] + [load_w]:
+    fetch = [pltpu.make_async_copy(large[i], held[i], load_sem.at[3 + i]) for i in range(3)]
+    load_wide = pltpu.make_async_copy(wide_hbm.at[c], wide, load_sem.at[6])
+    for x in fetch[:1] + [load(0)] + fetch[1:2] + [load(1), load_wide, fetch[2], load_w]:
         x.start()
     greet(seq_count, line, s, z, c, g, twin=True, side=True, whole_line=True)
 
@@ -739,8 +742,94 @@
         col = lax.rem(at, width // lanes)
         return lag, pl.ds(pl.multiple_of(col * lanes, lanes), lanes)
 
-    for x in fetch[:2]:
-        x.wait()
+    halves = (pl.ds(0, hn), pl.ds(hn, deep_in.shape[1] - hn))
+
+    def twin_deep(i, h):
+        l = dest(i)
+        src, dst = deep.at[1 - c, l, halves[h]], deep_in.at[l, halves[h]]
+        return remote(src, dst, ps.at[h, i], pr.at[h, i], twin)
+
+    def hop(kind, way, t, h, first):
+        run, own, send, recv, parts = kind
+        target = line - 1 - t if way == 0 else t
+        dst = run.at[way, t, parts[h]]
+        src = own(target, parts[h]) if first else dst
+        to = g + CORES if way == 0 else g - CORES
+        return remote(src, dst, send.at[h, way, t], recv.at[h, way, t], {"grp": to})
+
+    def deep_own(l, part):
+        return deep_in.at[l, part]
+
+    def wide_own(l, part):
+        return wide_in.at[s, l, part]
+
+    deep_line = (deep_run, deep_own, zs, zr, halves)
+    wide_line = (wide_run, wide_own, wzs, wzr, (pl.ds(0, wide_run.shape[2]),))
+
+    def begin(kind, t, h):
+        for way in (0, 1):
+
+            @pl.when(z == 0 if way == 0 else z == line - 1)
+            def _():
+                hop(kind, way, t, h, True).start()
+
+    def relay(kind, phase, h):
+        run, own, part = kind[0], kind[1], kind[4][h]
+        for way in (0, 1):
+            for t in range(phase):
+                at = phase - t if way == 0 else line - 1 - (phase - t)
+                target = line - 1 - t if way == 0 else t
+
+                @pl.when(z == at)
+                def _():
+                    hop(kind, way, t, h, False).wait_recv()
+                    mixed = run[way, t, part].astype(F32) + own(target, part)[...].astype(F32)
+                    run[way, t, part] = mixed.astype(BF16)
+                    hop(kind, way, t, h, False).start()
+
+    def segment(i, cc, lo, hi):
+        j = lo // width
+        cols = slice(lo - j * width, hi - j * width)
+        val = dot_tn(ul_buf[i % 2, j, 0, :, cols], dy[0])
+        val = (val + dot_tn(ul_buf[i % 2, j, 1, :, cols], dy[1])).astype(BF16)
+        deep[cc, dest(i), lo - cc * n : hi - cc * n, :] = val
+
+    def compute_half(i, h):
+        for cc in range(CORES):
+            lo, end = cc * n + h * hn, cc * n + (h + 1) * hn
+            while lo < end:
+                hi = min(end, (lo // width + 1) * width)
+                segment(i, cc, lo, hi)
+                lo = hi
+        twin_deep(i, h).start()
+
+    def compute(i):
+        l = dest(i)
+        load(i).wait()
+        for j in range(per_chip):
+            val = dot_tn(ul_buf[i % 2, j, 0], dy[0]) + dot_tn(ul_buf[i % 2, j, 1], dy[1])
+            val = val.astype(BF16)
+            for cc in range(CORES):
+                lo, hi = max(j * width, cc * n), min((j + 1) * width, (cc + 1) * n)
+                if lo < hi:
+                    deep[cc, l, lo - cc * n : hi - cc * n, :] = val[lo - j * width : hi - j * width]
+        for h in range(2):
+            twin_deep(i, h).start()
+        if i + 2 < line:
+            load(i + 2).start()
+
+    def combine(i, h):
+        l, part = dest(i), halves[h]
+        twin_deep(i, h).wait_recv()
+        mixed = deep[c, l, part].astype(F32) + deep_in[l, part].astype(F32)
+        deep_in[l, part] = mixed.astype(BF16)
+        if i < line - 1:
+            begin(deep_line, i, h)
+
+    fetch[0].wait()
+    load(0).wait()
+    compute_half(0, 0)
+    fetch[1].wait()
     for i in range(ar_chunks):
         lag, cols = ar_place(i)
         total = 0.0
@@ -752,111 +841,21 @@
         for cc in range(CORES):
             r = (l * CORES + cc) * ar_share
             deep[cc, l, n:, :] = dar[r : r + ar_share, :]
-
-    def twin_deep(i):
-        l = dest(i)
-        return remote(deep.at[1 - c, l], deep_in.at[l], ps.at[i], pr.at[i], twin)
-
-    def hop(run, own, send, recv, way, t, first):
-        target = line - 1 - t if way == 0 else t
-        src = own(target) if first else run.at[way, t]
-        to = g + CORES if way == 0 else g - CORES
-        return remote(src, run.at[way, t], send.at[way, t], recv.at[way, t], {"grp": to})
-
-    def deep_own(l):
-        return deep_in.at[l]
-
-    def wide_own(l):
-        return wide_in.at[s, l]
-
-    deep_line = (deep_run, deep_own, zs, zr)
-    wide_line = (wide_run, wide_own, wzs, wzr)
-
-    def begin(kind, t):
-        for way in (0, 1):
-
-            @pl.when(z == 0 if way == 0 else z == line - 1)
-            def _():
-                hop(*kind, way, t, True).start()
-
-    def relay(kind, phase):
-        run, own = kind[0], kind[1]
-        for way in (0, 1):
-            for t in range(phase):
-                at = phase - t if way == 0 else line - 1 - (phase - t)
-                target = line - 1 - t if way == 0 else t
-
-                @pl.when(z == at)
-                def _():
-                    hop(*kind, way, t, False).wait_recv()
-                    mixed = run[way, t].astype(F32) + own(target)[...].astype(F32)
-                    run[way, t] = mixed.astype(BF16)
-                    hop(*kind, way, t, False).start()
-
-    def compute(i):
-        l = dest(i)
-        load(i).wait()
-        for j in range(per_chip):
-            val = dot_tn(ul_buf[i % 2, j, 0], dy[0]) + dot_tn(ul_buf[i % 2, j, 1], dy[1])
-            val = val.astype(BF16)
-            for cc in range(CORES):
-                lo, hi = max(j * width, cc * n), min((j + 1) * width, (cc + 1) * n)
-                if lo < hi:
-                    deep[cc, l, lo - cc * n : hi - cc * n, :] = val[lo - j * width : hi - j * width]
-        twin_deep(i).start()
-        if i + 2 < line:
-            load(i + 2).start()
-
-    def combine(i):
-        l = dest(i)
-        twin_deep(i).wait_recv()
-        deep_in[l] = (deep[c, l].astype(F32) + deep_in[l].astype(F32)).astype(BF16)
-        if i < line - 1:
-            begin(deep_line, i)
-
-    compute(0)
+    compute_half(0, 1)
+    load(2).start()
+    wide_twin = remote(wide_hbm.at[1 - c], wide_in, wps, wpr, twin)
+    wide_twin.start()
+    combine(0, 0)
+    combine(0, 1)
     compute(1)
-    combine(0)
-
-    span_f = gb_ref.shape[1] // seq_count
-    down_share = dg_ref.shape[0]
-    for x in fetch[2:]:
-        x.wait()
-
-    @pl.loop(0, seq_count)
-    def _(j):
-        part = pl.ds(pl.multiple_of(j * span_f, span_f), span_f)
-        for which, back in ((0, gb_ref), (1, ub_ref)):
-            val = dot_tn(z_ref[...], back[:, part]).astype(BF16)
-            for k in range(seq_count):
-                for l in range(line):
-                    for cc in range(CORES):
-                        r = ((k * line + l) * CORES + cc) * share
-                        wide[cc, k, l, which * share : (which + 1) * share, part] = val[
-                            r : r + share
-                        ]
-        val = dot_tn(mixed_ref[:, part], cot_ref[...]).astype(BF16)
-        for l in range(line):
-            for cc in range(CORES):
-                r = (l * CORES + cc) * down_share
-                for q in range(down_share // share):
-                    wide[cc, j, l, 2 * share :, q * width : (q + 1) * width] = val[
-                        r + q * share : r + (q + 1) * share
-                    ]
-    wide_twin = remote(wide.at[1 - c], wide_in, wps, wpr, twin)
-    wide_twin.start()
-
-    for i in range(2, line):
-        compute(i)
-        combine(i - 1)
-    combine(line - 1)
-
+
+    load_wide.wait()
     wide_twin.wait_recv()
     for k in range(seq_count):
 
         @pl.loop(0, line)
         def _(l):
-            mixed = wide[c, k, l].astype(F32) + wide_in[k, l].astype(F32)
+            mixed = wide[k, l].astype(F32) + wide_in[k, l].astype(F32)
             wide_in[k, l] = mixed.astype(BF16)
 
     sides = []
@@ -866,6 +865,16 @@
             remote(wide_in.at[to], wide_side.at[j - 1], ws.at[j - 1], wr.at[j - 1], {"seq": to})
         )
         sides[-1].start()
+
+    for h in range(2):
+        combine(1, h)
+    for i in range(2, line):
+        compute(i)
+        for h in range(2):
+            combine(i, h)
+    for phase in range(1, line - 2):
+        for h in range(2):
+            relay(deep_line, phase, h)
 
     signs = signs_of(rows)
     for m in range(2):
@@ -887,11 +896,12 @@
             conv[1] = (dot_nn(kept_table, dsig[m]) * signs).astype(BF16)
             acc[m] += dot_nt(conv[0], w_buf[k, 0]) + dot_nt(conv[1], w_buf[k, 1])
 
-    half = count // 2
-    pl.loop(0, half)(filter_step)
-    for phase in range(1, line - 2):
-        relay(deep_line, phase)
-    pl.loop(half, count)(filter_step)
+    third = count // 3
+    pl.loop(0, third)(filter_step)
+    relay(deep_line, line - 2, 0)
+    pl.loop(third, 2 * third)(filter_step)
+    relay(deep_line, line - 2, 1)
+    pl.loop(2 * third, count)(filter_step)
     conv[...] = acc[...].astype(BF16)
     du_copies = []
     for i in range(1, seq_count):
@@ -906,9 +916,8 @@
             )
         )
         du_copies[-1].start()
-    if line > 2:
-        relay(deep_line, line - 2)
-
+
+    fetch[2].wait()
     for x in du_copies:
         x.wait_recv()
     gain = jnp.zeros((1, width), F32)
@@ -940,7 +949,7 @@
         wide_in[s, l] = mixed.astype(BF16)
 
     for t in range(line - 1):
-        begin(wide_line, t)
+        begin(wide_line, t, 0)
 
     small_pair.wait()
     g_own[...] = g_own[...] + g_pair[...]
@@ -981,7 +990,8 @@
 
                 @pl.when(z == target)
                 def _():
-                    hop(*kind, way, t, False).wait_recv()
+                    for h in range(len(kind[4])):
+                        hop(kind, way, t, h, False).wait_recv()
                     add(kind[0][way, t].astype(F32))
 
     def add_deep(val):
@@ -997,7 +1007,7 @@
     last(deep_line, add_deep)
     dw_store.start()
     for phase in range(1, line - 1):
-        relay(wide_line, phase)
+        relay(wide_line, phase, 0)
     own = wide_in[s, z].astype(F32)
     gg_ref[...] = own[:share]
     ug_ref[...] = own[share : 2 * share]
@@ -1019,7 +1029,8 @@
     dw_store.wait()
     wide_twin.wait_send()
     for i in range(line):
-        twin_deep(i).wait_send()
+        for h in range(2):
+            twin_deep(i, h).wait_send()
     for kind in (deep_line, wide_line):
         for t in range(line - 1):
             for way in (0, 1):
@@ -1027,21 +1038,21 @@
 
                 @pl.when(z < target if way == 0 else z > target)
                 def _():
-                    hop(*kind, way, t, False).wait_send()
+                    for h in range(len(kind[4])):
+                        hop(kind, way, t, h, False).wait_send()
 
 
 def mix_back(
-    seq_count, line, layout, dy, u, filters, w, ul, ar, x, hg, scale, mlp, mlp_grad, shares
+    seq_count, line, layout, dy, u, filters, w, ul, ar, x, hg, scale, grads, mlp_grad, shares
 ):
-    z, gate_back, up_back, mixed, cot = mlp
     share, down_share, deep_share, ar_share = shares
     _, block, width = x.shape
     rows = block * seq_count
     count = w.shape[0]
     per_chip = 2 * count // line
     small = (8, width)
-    hidden_units = gate_back.shape[1]
-    part = (2 * share + down_share * width // hidden_units, hidden_units)
+    part = grads.shape[3:]
+    hidden_units = part[1]
     out_shape = [
         jax.ShapeDtypeStruct((2, block, width), F32),
         jax.ShapeDtypeStruct((deep_share, width), F32),
@@ -1064,7 +1075,7 @@
         pltpu.VMEM((CORES, line) + deep, BF16),
         pltpu.VMEM((line,) + deep, BF16),
         pltpu.VMEM((2, line - 1) + deep, BF16),
-        pltpu.VMEM((CORES, seq_count, line) + part, BF16),
+        pltpu.VMEM((seq_count, line) + part, BF16),
         pltpu.VMEM((seq_count, line) + part, BF16),
         pltpu.VMEM((seq_count - 1, line) + part, BF16),
         pltpu.VMEM((2, line - 1) + part, BF16),
@@ -1074,36 +1085,36 @@
         pltpu.VMEM(small, F32),
         pltpu.VMEM((line - 1,) + small, F32),
     ]
-    large = [dy, u, z, gate_back, up_back, mixed, hg]
+    large = [dy, u, hg]
     scratch += [pltpu.VMEM(v.shape, v.dtype) for v in large]
     scratch += [pltpu.VMEM(v.shape, F32) for v in out_shape[:2]]
     scratch += [
         DMA((2,)),
-        DMA((10,)),
+        DMA((7,)),
         DMA((seq_count - 1,)),
         DMA((seq_count - 1,)),
-        DMA((line,)),
-        DMA((line,)),
-        DMA((2, line - 1)),
-        DMA((2, line - 1)),
+        DMA((2, line)),
+        DMA((2, line)),
+        DMA((2, 2, line - 1)),
+        DMA((2, 2, line - 1)),
         DMA,
         DMA,
         DMA((seq_count - 1,)),
         DMA((seq_count - 1,)),
-        DMA((2, line - 1)),
-        DMA((2, line - 1)),
+        DMA((1, 2, line - 1)),
+        DMA((1, 2, line - 1)),
         DMA((seq_count + line,)),
         DMA((seq_count + line,)),
     ]
     return pl.pallas_call(
         functools.partial(mix_back_kernel, seq_count, line),
         out_shape=out_shape,
-        in_specs=[pl.BlockSpec(memory_space=pltpu.SMEM)] + [WHOLE] * 6 + [ANY] * 9,
+        in_specs=[pl.BlockSpec(memory_space=pltpu.SMEM)] + [WHOLE] * 5 + [ANY] * 6,
         out_specs=[ANY] * 2 + [WHOLE] * 5,
         scratch_shapes=scratch,
         compiler_params=params(6),
         name="mix_back",
-    )(layout, filters, ar, x, scale, cot, mlp_grad, w, ul, *large)
+    )(layout, filters, ar, x, scale, mlp_grad, w, ul, grads, *large)
 
 
 def kept(rows, short, lag):
@@ -1142,15 +1153,15 @@
     (layout_ref, tok_ref, row_ref, mix_gain, mlp_gain, cot_ref, spec_hbm, ar_hbm) = refs[:8]
     wide_in = refs[8:11]
     (w_hbm, ul_hbm, u_hbm) = refs[11:14]
-    results = refs[14:20]
-    dy_hbm = refs[20]
-    (ar_ref, gain_out, mlp_ref) = refs[21:24]
-    (x_all, both, acc, y_bf, y_in, w_buf, ul_buf, keep, hid, dz, dy_own) = refs[24:35]
-    (z_ref, gb_ref, ub_ref, mixed_ref, hg_ref, out_ref) = local = refs[35:41]
-    wide_buf = refs[41:44]
-    (g_pad, g_own, g_side, g_sum, g_line, g_all, g_twin) = refs[44:51]
-    (load_sem, ul_sem, w_sem, ts, tr, ys, yr, zs, zr, hs, hr) = refs[51:62]
-    (ps, pr, ws, wr, wps, wpr, gs, gr, ds_, dr_, end_sem) = refs[62:]
+    results = refs[14:16]
+    (dy_hbm, grads_hbm) = refs[16:18]
+    (ar_ref, gain_out, mlp_ref) = refs[18:21]
+    (grads, x_all, both, acc, y_bf, y_in, w_buf, ul_buf, keep, hid, dz, dy_own) = refs[21:33]
+    (z_ref, gb_ref, ub_ref, mixed_ref, hg_ref, out_ref) = refs[33:39]
+    wide_buf = refs[39:42]
+    (g_pad, g_own, g_side, g_sum, g_line, g_all, g_twin) = refs[42:49]
+    (load_sem, ul_sem, w_sem, ts, tr, ys, yr, zs, zr, hs, hr) = refs[49:60]
+    (ps, pr, ws, wr, wps, wpr, gs, gr, ds_, dr_, end_sem) = refs[60:]
     s, z, c, g = place(seq_count, line)
     twin = {"grp": g + 1 - 2 * c}
     rows, width = x_all.shape[1], x_all.shape[2]
@@ -1525,10 +1536,35 @@
         ends[-1].start()
         hg_ref[m] = dh
         mlp_ref[0:1, :] += jnp.sum(grad * h * inv_two, axis=0, keepdims=True)
-    for i in range(5):
-        ends.append(pltpu.make_async_copy(local[i], results[i], end_sem.at[1 + i]))
-        ends[-1].start()
-    last = pltpu.make_async_copy(local[5], results[5], end_sem.at[6])
+    ends.append(pltpu.make_async_copy(hg_ref, results[0], end_sem.at[5]))
+    ends[-1].start()
+    share = wide_in[0].shape[0]
+    down_share = wide_in[2].shape[0]
+
+    @pl.loop(0, seq_count)
+    def _(j):
+        part = pl.ds(pl.multiple_of(j * step, step), step)
+        for which, back in ((0, gb_ref), (1, ub_ref)):
+            val = dot_tn(z_ref[...], back[:, part]).astype(BF16)
+            for k in range(seq_count):
+                for l in range(line):
+                    for cc in range(CORES):
+                        r = ((k * line + l) * CORES + cc) * share
+                        grads[cc, k, l, which * share : (which + 1) * share, part] = val[
+                            r : r + share
+                        ]
+        val = dot_tn(mixed_ref[:, part], cot_ref[...]).astype(BF16)
+        for l in range(line):
+            for cc in range(CORES):
+                r = (l * CORES + cc) * down_share
+                for q in range(down_share // share):
+                    grads[cc, j, l, 2 * share :, q * width : (q + 1) * width] = val[
+                        r + q * share : r + (q + 1) * share
+                    ]
+
+    ends.append(pltpu.make_async_copy(grads, grads_hbm, end_sem.at[9]))
+    ends[-1].start()
+    last = pltpu.make_async_copy(out_ref, results[1], end_sem.at[6])
     total = hid[...]
     for j in range(seq_count):
         down_w = wide_buf[2][j].reshape(step, width)
@@ -1551,6 +1587,9 @@
     hidden_units = wide[0].shape[1]
     small = (16, width)
     vmem = pltpu.VMEM
+    share = wide[0].shape[0]
+    part = 2 * share + wide[2].shape[0] * width // hidden_units
+    grads = (CORES, seq_count, line, part, hidden_units)
     out_shape = [
         jax.ShapeDtypeStruct((line, CORES * spec.shape[0], width), BF16),
         jax.ShapeDtypeStruct((2 * count, 2, rows, width), BF16),
@@ -1564,14 +1603,16 @@
         ((2, block, width), F32),
         ((2, block, width), F32),
     ]
-    out_shape += [jax.ShapeDtypeStruct(*x) for x in local]
+    out_shape += [jax.ShapeDtypeStruct(*x) for x in local[4:]]
     out_shape += [
         jax.ShapeDtypeStruct((2, rows, width), BF16),
+        jax.ShapeDtypeStruct(grads, BF16),
         jax.ShapeDtypeStruct((line, CORES) + ar.shape, BF16),
         jax.ShapeDtypeStruct((8, width), F32),
         jax.ShapeDtypeStruct((8, width), F32),
     ]
     scratch = [
+        vmem(grads, BF16),
         vmem((2, rows, width), BF16),
         vmem((2, rows, 2 * width), BF16),
         vmem((2, rows, width), F32),
@@ -1615,13 +1656,13 @@
         DMA((seq_count + line,)),
         DMA((2, seq_count - 1)),
         DMA((2, seq_count - 1)),
-        DMA((9,)),
+        DMA((10,)),
     ]
     return pl.pallas_call(
         functools.partial(mix_front_kernel, seq_count, line),
         out_shape=out_shape,
         in_specs=[pl.BlockSpec(memory_space=pltpu.SMEM)] + [WHOLE] * 5 + [ANY] * 5,
-        out_specs=[ANY] * 10 + [WHOLE] * 3,
+        out_specs=[ANY] * 7 + [WHOLE] * 3,
         scratch_shapes=scratch,
         compiler_params=params(7),
         name="mix_front",
@@ -1694,7 +1735,7 @@
         own = tokens[:, 0]
         cot = out_grad.reshape(2 * block, width)
         flags = layout.reshape(1, 2)
-        spec, ul, u, mlp_in, gate_back, up_back, mixed, dh, out, dy, ar, gains, mlp_grad = mix_front(
+        spec, ul, u, dh, out, dy, grads, ar, gains, mlp_grad = mix_front(
             seq_count,
             line,
             flags,
@@ -1719,7 +1760,7 @@
             own,
             dh,
             gains,
-            (mlp_in, gate_back, up_back, mixed, cot),
+            grads,
             mlp_grad,
             (share, w_down.shape[0], spectral_proj.shape[0], ar_proj.shape[0]),
         )

time: 196 us -> 190 us (0.969)
  Pallas kernels: 195 us -> 189 us
    pallas_call x1, Pallas kernels: 86.2 us -> 80 us  [mix_back(): pl.pallas_call(functools.partial(mix_back_kernel, seq_count, line), out_s...]
where the time goes in v7:
time: 190 us
  Pallas kernels  189 us (99%)
    pallas_call x1, Pallas kernels, mix_front(): pl.pallas_call(functools.partial(mix_front_kernel, seq_count, line), out_...  104 us
    pallas_call x1, Pallas kernels, mix_back(): pl.pallas_call(functools.partial(mix_back_kernel, seq_count, line), out_s...  80 us
    pallas_call x1, Pallas kernels, finish(): pl.pallas_call(functools.partial(finish_kernel, count, share), out_shape=...  4.4 us

profile of v7, /device:TPU:0, one launch (start us, length us, event | category | flops | bytes accessed | tf_op | source)
XLA Modules:
  0.0 189.6 jit_solution(2582571713439727287)
XLA Ops:
  0.6 104.4 %mix_front.1 = (bf16[4,1536,512]{2,1,0:T(8,128)(2,1)}, bf16[12,2,512,512]{3,2,1,0:T(8,128)(2,1)}, bf16[2,512,512]{2,1,0:T(8,128)(2,1)}, f32[2,128,512]{2,1,0:T(8...) custom-call(s32[1,2]{1,0:T(1,128)} %bitcast.23, ...), custom_call_target="tpu_custom_call" | custom-call | tf_op jit(solution)/shard_map/mix_front/pallas_call | solution.py:1661
  105.0 80.0 %mix_back.1 = (f32[2,128,512]{2,1,0:T(8,128)}, f32[768,512]{1,0:T(8,128)}, f32[48,512]{1,0:T(8,128)}, f32[16,2048]{1,0:T(8,128)}, f32[16,2048]{1,0:T(8,128)}, /*index=5*/f32[64,512]{1,0:T(8,128)}, f32[8,512]{1,0:T(8,128)}) custom-call(s32[1,2]{1,0:T(1,128)} %bitcast.24, f32[24,512]{1,0:T(8,128)} %bitcast.22, bf16[384,512]{1,0:T(8,128)(2,1)} %bitcast.19, ...), custom_call_target="tpu_custom_call" | custom-call | tf_op jit(solution)/shard_map/mix_back/pallas_call | solution.py:1109
  185.1 4.4 %finish.1 = (f32[768,512]{1,0:T(8,128)}, f32[2,128,512]{2,1,0:T(8,128)}, f32[2,128,512]{2,1,0:T(8,128)}, f32[64,512]{1,0:T(8,128)}, f32[16,2048]{1,0:T(8,128)}, ...) custom-call(f32[768,512]{1,0:T(8,128)} %get-tuple-element.44.refs_0_, ...), custom_call_target="tpu_custom_call" | custom-call | tf_op jit(solution)/shard_map/finish/pallas_call | solution.py:1692
